TPU v7x, 32 devices: a whole 2x2x4 slice. The times are simulated.
32 devices in a mesh: dom: 32 (over z, y, x, core).
Axes of the slice: x: 2, y: 2, z: 4, core: 2. Of those that a mesh axis runs over, the one named last changes fastest.
Arguments:
- states: float32 [16384, 128], P('dom'), may hold values from -6 to 6
- diag_blocks: float32 [128, 128, 128], P('dom'), may hold values from -0.5 to 0.5
- couplings: float32 [128, 128, 128], P('dom'), may hold values from -0.5 to 0.5
Outputs:
- orthonormal: float32 [16384, 128], P('dom')
- projected: float32 [128, 128], replicated
All inputs are finite; a program needn't handle non-finite values.
Results may differ from a plain program's by a relative error of at most 0.00012.
Values sent between devices are 32-bit elements; how exact they have to be, the bound alone decides.
No kernel may reach another device: no remote copies, remote signals or barrier semaphores. Data moves between devices by JAX's collectives and lax.ppermute only.
A program may use at most 64 MiB of HBM per device.

v0:
```python
import math

import jax
import jax.numpy as jnp
from jax import lax
from jax.sharding import PartitionSpec as P

center = 0.5
half_width = 4.0


def from_behind(block, axis, distance):
    devices = range(lax.axis_size(axis))
    route = [(i - distance, i) for i in devices if i - distance in devices]
    return lax.ppermute(block, axis, route)


def with_halo(block, sides, width):
    for axis, dim in sides:
        count = lax.axis_size(axis)
        forward = [(i, i + 1) for i in range(count - 1)]
        backward = [(target, source) for source, target in forward]
        low = lax.ppermute(
            lax.slice_in_dim(block, block.shape[dim] - width, None, axis=dim), axis, forward
        )
        high = lax.ppermute(lax.slice_in_dim(block, 0, width, axis=dim), axis, backward)
        block = jnp.concatenate([low, block, high], axis=dim)
    return block


def lower_solve(factor, values):
    return lax.linalg.triangular_solve(factor, values, left_side=True, lower=True)


def apply_band(extended, diag_ext, coup_ext):
    inside = jnp.einsum(
        "bij,bjs->bis", diag_ext[1:-1], extended[1:-1], precision=lax.Precision.HIGHEST
    )
    upward = jnp.einsum(
        "bij,bjs->bis", coup_ext[1:-1], extended[2:], precision=lax.Precision.HIGHEST
    )
    downward = jnp.einsum(
        "bji,bjs->bis", coup_ext[:-2], extended[:-2], precision=lax.Precision.HIGHEST
    )
    return inside + upward + downward


def gram_matrix(left, right):
    return jnp.einsum("ns,nt->st", left, right, precision=lax.Precision.HIGHEST)


def body(states, diag_blocks, couplings):
    nodes_dev, width = states.shape
    nblocks, block, unused_width = diag_blocks.shape
    devices = lax.axis_size("dom")
    total_nodes = nodes_dev * devices
    symmetric = 0.5 * (diag_blocks + jnp.swapaxes(diag_blocks, 1, 2))
    field = states.reshape(nblocks, block, width)
    empty = jnp.zeros((1, block, block), jnp.float32)
    coup_left = from_behind(couplings[-1:], "dom", 1)
    diag_ext = jnp.concatenate([empty, symmetric, empty], 0)
    coup_ext = jnp.concatenate([coup_left, couplings, empty], 0)
    previous = field
    current = field
    for turn in range(2):
        extended = with_halo(current, (("dom", 0),), 1)
        result = apply_band(extended, diag_ext, coup_ext) - center * current
        if turn == 0:
            following = result / half_width
        else:
            following = 2.0 * result / half_width - previous
        previous = current
        current = following
    flat = current.reshape(nodes_dev, width)
    extended = with_halo(current, (("dom", 0),), 1)
    image = apply_band(extended, diag_ext, coup_ext).reshape(nodes_dev, width)
    correlation, mixed = lax.psum((gram_matrix(flat, flat), gram_matrix(flat, image)), "dom")
    lower = jnp.linalg.cholesky(correlation)
    orthonormal = lower_solve(lower, flat.T).T * math.sqrt(total_nodes)
    left = lower_solve(lower, mixed)
    projected = lower_solve(lower, left.T).T
    return (orthonormal, projected)


def solution(mesh):
    in_specs = (P("dom", None), P("dom", None, None), P("dom", None, None))
    out_specs = (P("dom", None), P())
    return jax.shard_map(body, mesh=mesh, in_specs=in_specs, out_specs=out_specs, check_vma=False)
```

profile of v0, /device:TPU:0, one launch (start us, length us, event | category | flops | bytes accessed | tf_op | source)
XLA Modules:
  0.0 209.1 jit_solution(8059239828355264017)
XLA Ops:
  7.2 0.9 slice_bitcast_fusion
  8.1 2.4 %collective-permute-start.2 = (f32[1,128,128]{2,1,0:T(8,128)S(1)}, f32[1,128,128]{2,1,0:T(8,128)S(1)}, u32[]{:S(2)}, u32[]{:S(2)}) collective-permute-start(f32[1,128,128]{2,1,0:T(8,128)S(1)} %get-tuple-element.11), channel_id=1, source_target_pairs={{0,1},{1,2},{2,3},{3,4},{4,5},{5,6},{6,7},{7,8},{8,9},{9,10},{10,1... | collective-permute-start | bytes 196616 | tf_op jit(solution)/shard_map/ppermute | solution.py:23
  10.6 1.4 collective-permute-start
  12.2 5.3 %collective-permute-start.1 = (f32[1,128,128]{1,2,0:T(8,128)S(1)}, f32[1,128,128]{1,2,0:T(8,128)S(1)}, u32[]{:S(2)}, u32[]{:S(2)}) collective-permute-start(f32[1,128,128]{1,2,0:T(8,128)S(1)} %slice.85), channel_id=1, source_target_pairs={{0,1},{1,2},{2,3},{3,4},{4,5},{5,6},{6,7},{7,8},{8,9},{9,10},{10,1... | collective-permute-start | bytes 196616 | tf_op jit(solution)/shard_map/ppermute | solution.py:15
  17.4 0.1 copy.5
  17.6 0.4 fusion.35
  18.0 0.4 fusion.4
  18.4 0.4 broadcast_multiply_fusion
  18.8 4.2 %collective-permute-start.4 = (f32[1,128,128]{2,1,0:T(8,128)S(1)}, f32[1,128,128]{2,1,0:T(8,128)S(1)}, u32[]{:S(2)}, u32[]{:S(2)}) collective-permute-start(f32[1,128,128]{2,1,0:T(8,128)S(1)} %get-tuple-element.9), channel_id=1, source_target_pairs={{0,1},{1,2},{2,3},{3,4},{4,5},{5,6},{6,7},{7,8},{8,9},{9,10},{10,1... | collective-permute-start | bytes 196616 | tf_op jit(solution)/shard_map/ppermute | solution.py:23
  23.1 1.3 collective-permute-start.3
  24.4 0.4 fusion.31
  24.8 3.4 %collective-permute-done.3 = f32[1,128,128]{2,1,0:T(8,128)S(1)} collective-permute-done((f32[1,128,128]{2,1,0:T(8,128)S(1)}, f32[1,128,128]{2,1,0:T(8,128)S(1)}, u32[]{:S(2)}, u32[]{:S(2)}) %collective-permute-start.3) | collective-permute-done | bytes 65568 | tf_op jit(solution)/shard_map/ppermute | solution.py:26
  28.2 0.4 fusion.2
  28.6 0.4 fusion.6
  29.0 0.4 fusion.32
  29.5 1.3 collective-permute-start.5
  30.8 1.2 convolution_bitcast_fusion.6
  32.0 5.6 %collective-permute-start.6 = (f32[1,128,128]{2,1,0:T(8,128)S(1)}, f32[1,128,128]{2,1,0:T(8,128)S(1)}, u32[]{:S(2)}, u32[]{:S(2)}) collective-permute-start(f32[1,128,128]{2,1,0:T(8,128)S(1)} %get-tuple-element.7), channel_id=1, source_target_pairs={{0,1},{1,2},{2,3},{3,4},{4,5},{5,6},{6,7},{7,8},{8,9},{9,10},{10,1... | collective-permute-start | bytes 196616 | tf_op jit(solution)/shard_map/ppermute | solution.py:23
  37.6 0.4 fusion
  38.0 0.3 collective-permute-done.6
  38.3 0.4 convolution_add_fusion
  38.7 1.2 convolution_bitcast_fusion.5
  40.0 135.9 %all-reduce.3.cloned.1.call-done = (f32[128,128]{0,1:T(8,128)}, f32[128,128]{1,0:T(8,128)}) async-done(((f32[128,128]{0,1:T(8,128)}, f32[128,128]{1,0:T(8,128)}), (f32[128,128]{0,1:T(8,128)}, f32[128,128]{1,0:T(8,128)})) %all-reduce.3.cloned.1.call-update) | async-done | bytes 131088 | tf_op jit(solution)/shard_map/psum | solution.py:77
  175.9 1.0 copy.10
  176.9 11.7 %cholesky.16 = f32[128,128]{1,0:T(8,128)S(1)} custom-call(f32[128,128]{1,0:T(8,128)S(1)} %fusion.24), custom_call_target="Cholesky" | custom-call | tf_op jit(solution)/shard_map/jit(cholesky)/cholesky | solution.py:78
  188.7 0.6 compare_reduce_fusion
  189.3 0.7 fusion.20
  190.0 9.8 %custom-call.9 = f32[1,128,128]{1,2,0:T(8,128)S(1)} custom-call(f32[1,128,128]{2,1,0:T(8,128)S(1)} %fusion.20), custom_call_target="InvertDiagBlocksLowerTriangular" | custom-call | tf_op jit(solution)/shard_map/triangular_solve | solution.py:32
  199.8 0.3 convolution_bitcast_fusion.4
  200.1 0.3 convolution_bitcast_fusion.3
  200.4 1.1 convolution_multiply_fusion
  201.5 0.7 copy.11
  (23 shorter events, 0.3 us)
Async XLA Ops:
  7.2 4.8 %copy-start.1 = (f32[4,128,128]{2,1,0:T(8,128)S(1)}, f32[4,128,128]{2,1,0:T(8,128)}, u32[]{:S(2)}) copy-start(f32[4,128,128]{2,1,0:T(8,128)} %param.7) | copy-start | bytes 786436
  7.2 168.7 %all-reduce.3.cloned.1.call-start = ((), (), s32[]{:S(2)}) async-start(), calls=%async_computation | async-start | bytes 262144 | tf_op jit(solution)/shard_map/psum | solution.py:77
  8.1 10.3 %collective-permute-start.2 = (f32[1,128,128]{2,1,0:T(8,128)S(1)}, f32[1,128,128]{2,1,0:T(8,128)S(1)}, u32[]{:S(2)}, u32[]{:S(2)}) collective-permute-start(f32[1,128,128]{2,1,0:T(8,128)S(1)} %get-tuple-element.11), channel_id=1, source_target_pairs={{0,1},{1,2},{2,3},{3,4},{4,5},{5,6},{6,7},{7,8},{8,9},{9,10},{10,1... | collective-permute-start | bytes 196616 | tf_op jit(solution)/shard_map/ppermute | solution.py:23
  10.5 6.9 %copy-start.2 = (f32[4,128,128]{2,1,0:T(8,128)S(1)}, f32[4,128,128]{2,1,0:T(8,128)}, u32[]{:S(2)}) copy-start(f32[4,128,128]{2,1,0:T(8,128)} %param.6) | copy-start | bytes 786436
  10.6 7.4 %collective-permute-start = (f32[1,128,128]{2,1,0:T(8,128)S(1)}, f32[1,128,128]{2,1,0:T(8,128)S(1)}, u32[]{:S(2)}, u32[]{:S(2)}) collective-permute-start(f32[1,128,128]{2,1,0:T(8,128)S(1)} %get-tuple-element.12), channel_id=1, source_target_pairs={{1,0},{2,1},{3,2},{4,3},{5,4},{6,5},{7,6},{8,7},{9,8},{10,9},{11,1... | collective-permute-start | bytes 196616 | tf_op jit(solution)/shard_map/ppermute | solution.py:26
  12.2 5.4 %copy-start = (f32[512,128]{1,0:T(8,128)S(1)}, f32[512,128]{1,0:T(8,128)}, u32[]{:S(2)}) copy-start(f32[512,128]{1,0:T(8,128)} %param.5) | copy-start | bytes 786436
  12.2 6.2 %collective-permute-start.1 = (f32[1,128,128]{1,2,0:T(8,128)S(1)}, f32[1,128,128]{1,2,0:T(8,128)S(1)}, u32[]{:S(2)}, u32[]{:S(2)}) collective-permute-start(f32[1,128,128]{1,2,0:T(8,128)S(1)} %slice.85), channel_id=1, source_target_pairs={{0,1},{1,2},{2,3},{3,4},{4,5},{5,6},{6,7},{7,8},{8,9},{9,10},{10,1... | collective-permute-start | bytes 196616 | tf_op jit(solution)/shard_map/ppermute | solution.py:15
  18.8 9.7 %collective-permute-start.4 = (f32[1,128,128]{2,1,0:T(8,128)S(1)}, f32[1,128,128]{2,1,0:T(8,128)S(1)}, u32[]{:S(2)}, u32[]{:S(2)}) collective-permute-start(f32[1,128,128]{2,1,0:T(8,128)S(1)} %get-tuple-element.9), channel_id=1, source_target_pairs={{0,1},{1,2},{2,3},{3,4},{4,5},{5,6},{6,7},{7,8},{8,9},{9,10},{10,1... | collective-permute-start | bytes 196616 | tf_op jit(solution)/shard_map/ppermute | solution.py:23
  23.1 5.1 %collective-permute-start.3 = (f32[1,128,128]{2,1,0:T(8,128)S(1)}, f32[1,128,128]{2,1,0:T(8,128)S(1)}, u32[]{:S(2)}, u32[]{:S(2)}) collective-permute-start(f32[1,128,128]{2,1,0:T(8,128)S(1)} %get-tuple-element.10), channel_id=1, source_target_pairs={{1,0},{2,1},{3,2},{4,3},{5,4},{6,5},{7,6},{8,7},{9,8},{10,9},{11,1... | collective-permute-start | bytes 196616 | tf_op jit(solution)/shard_map/ppermute | solution.py:26
  29.5 8.2 %collective-permute-start.5 = (f32[1,128,128]{2,1,0:T(8,128)S(1)}, f32[1,128,128]{2,1,0:T(8,128)S(1)}, u32[]{:S(2)}, u32[]{:S(2)}) collective-permute-start(f32[1,128,128]{2,1,0:T(8,128)S(1)} %get-tuple-element.8), channel_id=1, source_target_pairs={{1,0},{2,1},{3,2},{4,3},{5,4},{6,5},{7,6},{8,7},{9,8},{10,9},{11,1... | collective-permute-start | bytes 196616 | tf_op jit(solution)/shard_map/ppermute | solution.py:26
  32.0 6.3 %collective-permute-start.6 = (f32[1,128,128]{2,1,0:T(8,128)S(1)}, f32[1,128,128]{2,1,0:T(8,128)S(1)}, u32[]{:S(2)}, u32[]{:S(2)}) collective-permute-start(f32[1,128,128]{2,1,0:T(8,128)S(1)} %get-tuple-element.7), channel_id=1, source_target_pairs={{0,1},{1,2},{2,3},{3,4},{4,5},{5,6},{6,7},{7,8},{8,9},{9,10},{10,1... | collective-permute-start | bytes 196616 | tf_op jit(solution)/shard_map/ppermute | solution.py:23
  175.9 1.0 copy-start.3
  189.3 10.5 %copy-start.4 = (f32[128,128]{1,0:T(8,128)S(1)}, f32[128,128]{1,0:T(8,128)}, u32[]{:S(2)}) copy-start(f32[128,128]{1,0:T(8,128)} %get-tuple-element.6) | copy-start | bytes 196612
Sparse Core Ops, SparseCore 0:
  40.1 135.7 all-reduce.2
where the time goes:
time: 209 us
  waiting for transfers between devices  140 us (67%)
  other arithmetic  22.9 us (11%)
  starting transfers between devices  21.6 us (10%)
  between operations  14.3 us (7%)
  matrix products  7.64 us (4%)
  local copies, waits for them, and re-layouts  2.95 us (1%)
    psum x1, waiting for transfers between devices, body(): lax.psum((gram_matrix(flat, flat), gram_matrix(flat, image)), 'dom')  136 us
    another operation x3, other arithmetic, body(): lower = jnp.linalg.cholesky(correlation)  12.4 us
    ppermute x3, starting transfers between devices, with_halo(): lax.ppermute(lax.slice_in_dim(block, block.shape[dim] - width, None, axis...  12.3 us
    another operation x2, other arithmetic, lower_solve(): lax.linalg.triangular_solve(factor, values, left_side=True, lower=True)  10.5 us
    ppermute x1, starting transfers between devices, from_behind(): return lax.ppermute(block, axis, route)  5.26 us
  transfers between devices with their start and end apart: 8, of which 3 were waited for; matrix products, arithmetic and copies ran while one was open for 2% of the time, Pallas kernels for 0%

commit v1 on v0

v1 whole, which is shorter than its diff:
```python
import math

import jax
import jax.numpy as jnp
from jax import lax
from jax.experimental import pallas as pl
from jax.experimental.pallas import tpu as pltpu
from jax.sharding import PartitionSpec as P

center = 0.5
half_width = 4.0
exact = lax.Precision.HIGHEST
vmem = pl.BlockSpec(memory_space=pltpu.VMEM)
smem = pl.BlockSpec(memory_space=pltpu.SMEM)


def mm(a, b):
    return lax.dot_general(
        a, b, (((1,), (0,)), ((), ())), precision=exact, preferred_element_type=jnp.float32
    )


def mm_tn(a, b):
    return lax.dot_general(
        a, b, (((0,), (0,)), ((), ())), precision=exact, preferred_element_type=jnp.float32
    )


def mm_nt(a, b):
    return lax.dot_general(
        a, b, (((1,), (1,)), ((), ())), precision=exact, preferred_element_type=jnp.float32
    )


def iotas(shape):
    return (
        lax.broadcasted_iota(jnp.int32, shape, 0),
        lax.broadcasted_iota(jnp.int32, shape, 1),
    )


def prepare(where_ref, s_ref, d_ref, c_ref, even_ref, odd_ref, sym_ref, clast_ref, first_ref, pass_ref):
    nblocks, block, unused = d_ref.shape
    last = nblocks - 1
    rows, cols = iotas((block, block))
    shift = jnp.where(rows == cols, center, 0.0)
    s = [s_ref[b * block : (b + 1) * block, :] for b in range(nblocks)]
    c = [c_ref[b] for b in range(nblocks)]
    c[last] = jnp.where(where_ref[1] == 1, jnp.zeros_like(c[last]), c[last])
    clast_ref[...] = c[last]
    sym = []
    for b in range(nblocks):
        d = d_ref[b]
        sym.append(0.5 * (d + d.T) - shift)
        sym_ref[b] = sym[b]
    first = []
    for b in range(nblocks):
        acc = mm(sym[b], s[b])
        if b < last:
            acc += mm(c[b], s[b + 1])
        if b > 0:
            acc += mm_tn(c[b - 1], s[b - 1])
        first.append(acc / half_width)
        first_ref[b * block : (b + 1) * block, :] = first[b]
    onward = mm_tn(c[last], s[last])
    pass_ref[...] = onward
    second = 2.0 * (mm(sym[0], first[0]) + mm(c[0], first[1])) / half_width - s[0]
    again = mm_tn(c[last], first[last])

    def put(left_ref, right_ref):
        left_ref[0] = s[0]
        left_ref[1] = first[0]
        left_ref[2] = second
        left_ref[3] = sym[0]
        right_ref[0] = onward
        right_ref[1] = again
        right_ref[2] = c[last]
        right_ref[3] = jnp.zeros_like(s[0])

    @pl.when(where_ref[0] == 0)
    def _():
        put(odd_ref, even_ref)

    @pl.when(where_ref[0] != 0)
    def _():
        put(even_ref, odd_ref)


def project(where_ref, s_ref, c_ref, sym_ref, clast_ref, first_ref, pass_ref, even_ref, odd_ref, filt_ref, sums_ref):
    nblocks, block, unused = c_ref.shape
    last = nblocks - 1
    rows, cols = iotas((block, block))
    even_is_right = where_ref[0] == 0
    s = [s_ref[b * block : (b + 1) * block, :] for b in range(nblocks)]
    first = [first_ref[b * block : (b + 1) * block, :] for b in range(nblocks)]
    sym = [sym_ref[b] for b in range(nblocks)]
    c = [c_ref[b] for b in range(last)] + [clast_ref[...]]
    right = [jnp.where(even_is_right, even_ref[k], odd_ref[k]) for k in range(4)]
    left = [jnp.where(even_is_right, odd_ref[k], even_ref[k]) for k in range(3)]
    onward = pass_ref[...]
    scale = 2.0 / half_width
    behind = left[1] + mm_tn(left[2], mm(left[2], s[0])) / half_width
    ahead = right[1] + onward / half_width
    first[0] = first[0] + left[0] / half_width
    first[last] = first[last] + mm(c[last], right[0]) / half_width
    first.append(ahead)
    filtered = []
    for b in range(nblocks):
        acc = mm(sym[b], first[b]) + mm(c[b], first[b + 1])
        acc += behind if b == 0 else mm_tn(c[b - 1], first[b - 1])
        filtered.append(scale * acc - s[b])
        filt_ref[b * block : (b + 1) * block, :] = filtered[b]
    beyond = right[2] + scale * (mm(right[3], onward) / half_width + mm_tn(c[last], first[last]))
    filtered.append(beyond)
    correlation = mm_tn(filtered[0], filtered[0])
    half = None
    for b in range(nblocks):
        image = 0.5 * (mm(sym[b], filtered[b]) + center * filtered[b]) + mm(c[b], filtered[b + 1])
        if b:
            correlation += mm_tn(filtered[b], filtered[b])
        term = mm_tn(filtered[b], image)
        half = term if half is None else half + term
    mixed = half + half.T
    width = mixed.shape[0]
    rows, cols = iotas((width, width))
    sums_ref[0:width, :] = jnp.where(rows >= cols, correlation, mixed)
    diagonal = jnp.sum(jnp.where(rows == cols, mixed, 0.0), axis=0, keepdims=True)
    sums_ref[width : width + 8, :] = jnp.broadcast_to(diagonal, (8, width))


def finish(total_nodes, sums_ref, filt_ref, orth_ref, proj_ref, inv_ref):
    width = filt_ref.shape[1]
    tiles = width // 8
    packed = sums_ref[0:width, :]
    rows, cols = iotas((width, width))
    upper = jnp.where(rows < cols, packed, 0.0)
    diagonal = jnp.where(rows == cols, sums_ref[width : width + 1, :], 0.0)
    mixed = upper + upper.T + diagonal
    low = jnp.where(rows >= cols, packed, 0.0)
    full = low + jnp.where(rows > cols, packed, 0.0).T
    sub, lane = iotas((8, width))
    work = [full[8 * t : 8 * t + 8, :] for t in range(tiles)]
    for p in range(tiles):
        at = 8 * p
        inside = (lane >= at) & (lane < at + 8)
        row = [jnp.broadcast_to(work[p][j : j + 1, :], (8, width)) for j in range(8)]
        a = {}
        for i in range(8):
            for j in range(i + 1):
                a[i, j] = jnp.broadcast_to(row[i][:, at + j : at + j + 1], (8, width))
        m, recip = {}, []
        for j in range(8):
            recip.append(1.0 / a[j, j])
            for i in range(j + 1, 8):
                m[i, j] = a[i, j] * recip[j]
            for i in range(j + 1, 8):
                for k in range(j + 1, i + 1):
                    a[i, k] = a[i, k] - m[i, j] * a[k, j]
        pivot = []
        for j in range(8):
            r = jnp.where(inside, jnp.where(lane == at + j, 1.0, 0.0), row[j])
            for k in range(j):
                r = r - m[j, k] * pivot[k]
            pivot.append(r)
        out = jnp.zeros((8, width), jnp.float32)
        for j in range(8):
            out = jnp.where(sub == j, pivot[j] * lax.rsqrt(a[j, j]), out)
        inv_ref[at : at + 8, :] = jnp.where(lane <= sub + at, out, 0.0)
        for t in range(p + 1, tiles):
            w = []
            for j in range(8):
                x = jnp.broadcast_to(work[t][:, at + j : at + j + 1], (8, width))
                for k in range(j):
                    x = x - w[k] * m[j, k]
                w.append(x)
            acc = jnp.where(inside, 0.0, work[t])
            for j in range(8):
                acc = acc - (w[j] * recip[j]) * pivot[j]
            work[t] = acc
    inv = inv_ref[...]
    orth_ref[...] = mm_nt(filt_ref[...], inv) * math.sqrt(total_nodes)
    proj_ref[...] = mm_nt(mm(inv, mixed), inv)


def shape(*dims):
    return jax.ShapeDtypeStruct(dims, jnp.float32)


def total_over(values, axis):
    count = lax.axis_size(axis)
    index = lax.axis_index(axis)
    stride = 1
    while stride < count:
        left = count // stride
        radix = next(r for r in range(2, left + 1) if left % r == 0)
        if radix == 2:
            route = [(i, i + stride if (i // stride) % 2 == 0 else i - stride) for i in range(count)]
            values = values + lax.ppermute(values, axis, route)
        else:
            place = (index // stride) % radix
            parts = [values]
            for hop in range(1, radix):
                route = []
                for i in range(count):
                    digit = (i // stride) % radix
                    route.append((i, i + ((digit - hop) % radix - digit) * stride))
                parts.append(lax.ppermute(values, axis, route))
            stacked = jnp.stack(parts)
            total = None
            for digit in range(radix):
                term = lax.dynamic_index_in_dim(stacked, (digit - place) % radix, 0, keepdims=False)
                total = term if total is None else total + term
            values = total
        stride *= radix
    return values


def swap(values, axis, start):
    count = lax.axis_size(axis)
    route = []
    for i in range(start, count - 1, 2):
        route += [(i, i + 1), (i + 1, i)]
    return lax.ppermute(values, axis, route)


def body(states, diag_blocks, couplings):
    nodes_dev, width = states.shape
    nblocks, block, unused = diag_blocks.shape
    devices = lax.axis_size("dom")
    index = lax.axis_index("dom")
    where = jnp.stack([index % 2, (index == devices - 1).astype(jnp.int32)])
    params = pltpu.CompilerParams(vmem_limit_bytes=48 << 20)
    cross = shape(4, block, width)
    even, odd, sym, clast, first, onward = pl.pallas_call(
        prepare,
        out_shape=(cross, cross, shape(nblocks, block, block), shape(block, block), shape(nodes_dev, width), shape(block, width)),
        in_specs=[smem, vmem, vmem, vmem],
        out_specs=(vmem,) * 6,
        compiler_params=params,
        name="prepare",
    )(where, states, diag_blocks, couplings)
    even = swap(even, "dom", 0)
    odd = swap(odd, "dom", 1)
    filtered, sums = pl.pallas_call(
        project,
        out_shape=(shape(nodes_dev, width), shape(width + 8, width)),
        in_specs=[smem] + [vmem] * 8,
        out_specs=(vmem,) * 2,
        compiler_params=params,
        name="project",
    )(where, states, couplings, sym, clast, first, onward, even, odd)
    sums = total_over(sums, "dom")
    orthonormal, projected, unused = pl.pallas_call(
        lambda *refs: finish(nodes_dev * devices, *refs),
        out_shape=(shape(nodes_dev, width), shape(width, width), shape(width, width)),
        in_specs=[vmem] * 2,
        out_specs=(vmem,) * 3,
        compiler_params=params,
        name="finish",
    )(sums, filtered)
    return orthonormal, projected


def solution(mesh):
    in_specs = (P("dom", None), P("dom", None, None), P("dom", None, None))
    out_specs = (P("dom", None), P())
    return jax.shard_map(body, mesh=mesh, in_specs=in_specs, out_specs=out_specs, check_vma=False)
```

time: 209 us -> 46.4 us (0.22)
  waiting for transfers between devices: 140 us -> 12.5 us
  other arithmetic: 22.9 us -> 0.13 us
  between operations: 14.3 us -> 0.69 us
  Pallas kernels: 0 us -> 10.5 us
  matrix products: 7.64 us -> 0 us
  starting transfers between devices: 21.6 us -> 19.5 us
    psum x1 -> x0, waiting for transfers between devices: 136 us -> none  [body(): lax.psum((gram_matrix(flat, flat), gram_matrix(flat, image)), 'dom')]
    another operation x5 -> x1, other arithmetic: 22.9 us -> 0.08 us  [body(): where = jnp.stack([index % 2, (index == devices - 1).astype(jnp.int32)])]
    pallas_call x0 -> x3, Pallas kernels: none -> 10.5 us  [the longest x1 5.88 us: body(): pl.pallas_call(lambda *refs: finish(nodes_dev * devices, *refs), out_shap...]
    ppermute x7, waiting for transfers between devices: 3.74 us -> 12.5 us  [the longest x5 12.1 us: total_over(): values = values + lax.ppermute(values, axis, route)]
    dot_general x11 -> x0, matrix products: 6.01 us -> none  [the longest x2 2.44 us: gram_matrix(): return jnp.einsum('ns,nt->st', left, right, precision=lax.Precision.HIGHEST)]
  transfers between devices with their start and end apart: 8 -> 7, of which waited for: 3 -> 6; matrix products, arithmetic and copies ran while one was open for 2% -> 0% of each run, Pallas kernels for 0% -> 0%
where the time goes in v1:
time: 46.4 us; the launch traced here: 46.2 us
  starting transfers between devices  19.5 us (42%)
  waiting for transfers between devices  12.5 us (27%)
  Pallas kernels  10.5 us (23%)
  local copies, waits for them, and re-layouts  2.85 us (6%)
  between operations  0.69 us (1%)
    ppermute x5, starting transfers between devices, total_over(): values = values + lax.ppermute(values, axis, route)  18.3 us
    ppermute x5, waiting for transfers between devices, total_over(): values = values + lax.ppermute(values, axis, route)  12.1 us
    pallas_call x1, Pallas kernels, body(): pl.pallas_call(lambda *refs: finish(nodes_dev * devices, *refs), out_shap...  5.88 us
    pallas_call x1, Pallas kernels, body(): pl.pallas_call(project, out_shape=(shape(nodes_dev, width), shape(width +...  3.06 us
    unnamed x8, local copies, waits for them, and re-layouts  2.85 us
    pallas_call x1, Pallas kernels, body(): pl.pallas_call(prepare, out_shape=(cross, cross, shape(nblocks, block, bl...  1.51 us
    ppermute x2, starting transfers between devices, swap(): return lax.ppermute(values, axis, route)  1.24 us
  transfers between devices with their start and end apart: 7, of which 6 were waited for; matrix products, arithmetic and copies ran while one was open for 0% of the time, Pallas kernels for 0%

profile of v1, /device:TPU:0, one launch (start us, length us, event | category | flops | bytes accessed | tf_op | source)
XLA Modules:
  0.0 46.2 jit_solution(14615295265440173501)
XLA Ops:
  0.6 0.1 pad_add_fusion.where_ref
  0.7 0.0 copy-start
  0.7 0.9 %copy-done = f32[512,128]{1,0:T(8,128)S(1)} copy-done((f32[512,128]{1,0:T(8,128)S(1)}, f32[512,128]{1,0:T(8,128)}, u32[]{:S(2)}) %copy-start) | copy-done | bytes 262168
  1.7 0.0 copy-start.1
  1.7 0.9 %copy-done.1 = f32[4,128,128]{2,1,0:T(8,128)S(1)} copy-done((f32[4,128,128]{2,1,0:T(8,128)S(1)}, f32[4,128,128]{2,1,0:T(8,128)}, u32[]{:S(2)}) %copy-start.1) | copy-done | bytes 262168
  2.6 0.0 copy-start.3
  2.6 0.9 %copy-done.3 = f32[4,128,128]{2,1,0:T(8,128)S(1)} copy-done((f32[4,128,128]{2,1,0:T(8,128)S(1)}, f32[4,128,128]{2,1,0:T(8,128)}, u32[]{:S(2)}) %copy-start.3) | copy-done | bytes 262168
  3.6 0.0 copy-start.2
  3.6 1.5 %prepare.1 = (f32[4,128,128]{2,1,0:T(8,128)S(1)}, f32[4,128,128]{2,1,0:T(8,128)S(1)}, f32[4,128,128]{2,1,0:T(8,128)S(1)}, f32[128,128]{1,0:T(8,128)S(1)}, f32[51...) custom-call(s32[2]{0:T(128)S(1)} %pad_add_fusion.where_ref, f32[512,128]{1,0:T(8,128)S(1)} %copy-done, ...), custom_call_target="tpu_custom_call" | custom-call | tf_op jit(solution)/shard_map/prepare/pallas_call | solution.py:234
  5.1 0.6 %collective-permute-start = (f32[4,128,128]{2,1,0:T(8,128)S(1)}, f32[4,128,128]{2,1,0:T(8,128)S(1)}, u32[]{:S(2)}, u32[]{:S(2)}) collective-permute-start(f32[4,128,128]{2,1,0:T(8,128)S(1)} %get-tuple-element.16), channel_id=1, source_target_pairs={{0,1},{1,0},{2,3},{3,2},{4,5},{5,4},{6,7},{7,6},{8,9},{9,8},{10,11... | collective-permute-start | bytes 786440 | tf_op jit(solution)/shard_map/ppermute | solution.py:223
  5.7 0.7 %collective-permute-start.1 = (f32[4,128,128]{2,1,0:T(8,128)S(1)}, f32[4,128,128]{2,1,0:T(8,128)S(1)}, u32[]{:S(2)}, u32[]{:S(2)}) collective-permute-start(f32[4,128,128]{2,1,0:T(8,128)S(1)} %get-tuple-element.17), channel_id=1, source_target_pairs={{1,2},{2,1},{3,4},{4,3},{5,6},{6,5},{7,8},{8,7},{9,10},{10,9},{11,... | collective-permute-start | bytes 786440 | tf_op jit(solution)/shard_map/ppermute | solution.py:223
  6.3 0.5 %collective-permute-done.even_ref = f32[4,128,128]{2,1,0:T(8,128)S(1)} collective-permute-done((f32[4,128,128]{2,1,0:T(8,128)S(1)}, f32[4,128,128]{2,1,0:T(8,128)S(1)}, u32[]{:S(2)}, u32[]{:S(2)}) %collective-permute-start) | collective-permute-done | bytes 262176 | tf_op jit(solution)/shard_map/ppermute | solution.py:223
  6.8 0.0 collective-permute-done.1.odd_ref
  6.8 0.0 copy-done.2
  6.8 3.1 %project.1 = (f32[512,128]{1,0:T(8,128)S(1)}, f32[136,128]{1,0:T(8,128)S(1)}) custom-call(s32[2]{0:T(128)S(1)} %pad_add_fusion.where_ref, f32[512,128]{1,0:T(8,128)S(1)} %copy-done, f32[4,128,128]{2,1,0:T(8,128)S(1)} %copy-done.2, f32[4,128,128]{2,1,0:T(8,128)S(1)} %get-tuple-element.12.sym_ref, f32[128,128]{1,0:T(8,128)S(1)} %get-tuple-element.13.clast_ref, ...), custom_call_target="tpu_custom_call" | custom-call | tf_op jit(solution)/shard_map/project/pallas_call | solution.py:244
  9.9 9.3 %collective-permute-start.2 = (f32[136,128]{1,0:T(8,128)S(1)}, f32[136,128]{1,0:T(8,128)S(1)}, u32[]{:S(2)}, u32[]{:S(2)}) collective-permute-start(f32[136,128]{1,0:T(8,128)S(1)} %get-tuple-element.18), channel_id=1, source_target_pairs={{0,1},{1,0},{2,3},{3,2},{4,5},{5,4},{6,7},{7,6},{8,9},{9,8},{10,11... | collective-permute-start | bytes 208904 | tf_op jit(solution)/shard_map/ppermute | solution.py:198
  19.2 0.9 %collective-permute-done.2 = f32[136,128]{1,0:T(8,128)S(1)} collective-permute-done((f32[136,128]{1,0:T(8,128)S(1)}, f32[136,128]{1,0:T(8,128)S(1)}, u32[]{:S(2)}, u32[]{:S(2)}) %collective-permute-start.2) | collective-permute-done | bytes 69664 | tf_op jit(solution)/shard_map/ppermute | solution.py:198
  20.2 3.4 %collective-permute-start.3 = (f32[136,128]{1,0:T(8,128)S(1)}, f32[136,128]{1,0:T(8,128)S(1)}, u32[]{:S(2)}, u32[]{:S(2)}) collective-permute-start(f32[136,128]{1,0:T(8,128)S(1)} %add.20), channel_id=1, source_target_pairs={{0,2},{1,3},{2,0},{3,1},{4,6},{5,7},{6,4},{7,5},{8,10},{9,11},{10,... | collective-permute-start | bytes 208904 | tf_op jit(solution)/shard_map/ppermute | solution.py:198
  23.5 2.7 %collective-permute-done.3 = f32[136,128]{1,0:T(8,128)S(1)} collective-permute-done((f32[136,128]{1,0:T(8,128)S(1)}, f32[136,128]{1,0:T(8,128)S(1)}, u32[]{:S(2)}, u32[]{:S(2)}) %collective-permute-start.3) | collective-permute-done | bytes 69664 | tf_op jit(solution)/shard_map/ppermute | solution.py:198
  26.2 1.3 %collective-permute-start.4 = (f32[136,128]{1,0:T(8,128)S(1)}, f32[136,128]{1,0:T(8,128)S(1)}, u32[]{:S(2)}, u32[]{:S(2)}) collective-permute-start(f32[136,128]{1,0:T(8,128)S(1)} %add.21), channel_id=1, source_target_pairs={{0,4},{1,5},{2,6},{3,7},{4,0},{5,1},{6,2},{7,3},{8,12},{9,13},{10,... | collective-permute-start | bytes 208904 | tf_op jit(solution)/shard_map/ppermute | solution.py:198
  27.5 3.1 %collective-permute-done.4 = f32[136,128]{1,0:T(8,128)S(1)} collective-permute-done((f32[136,128]{1,0:T(8,128)S(1)}, f32[136,128]{1,0:T(8,128)S(1)}, u32[]{:S(2)}, u32[]{:S(2)}) %collective-permute-start.4) | collective-permute-done | bytes 69664 | tf_op jit(solution)/shard_map/ppermute | solution.py:198
  30.6 1.6 %collective-permute-start.5 = (f32[136,128]{1,0:T(8,128)S(1)}, f32[136,128]{1,0:T(8,128)S(1)}, u32[]{:S(2)}, u32[]{:S(2)}) collective-permute-start(f32[136,128]{1,0:T(8,128)S(1)} %add.22), channel_id=1, source_target_pairs={{0,8},{1,9},{2,10},{3,11},{4,12},{5,13},{6,14},{7,15},{8,0},{9,1},... | collective-permute-start | bytes 208904 | tf_op jit(solution)/shard_map/ppermute | solution.py:198
  32.3 2.7 %collective-permute-done.5 = f32[136,128]{1,0:T(8,128)S(1)} collective-permute-done((f32[136,128]{1,0:T(8,128)S(1)}, f32[136,128]{1,0:T(8,128)S(1)}, u32[]{:S(2)}, u32[]{:S(2)}) %collective-permute-start.5) | collective-permute-done | bytes 69664 | tf_op jit(solution)/shard_map/ppermute | solution.py:198
  35.0 2.7 %collective-permute-start.6 = (f32[136,128]{1,0:T(8,128)S(1)}, f32[136,128]{1,0:T(8,128)S(1)}, u32[]{:S(2)}, u32[]{:S(2)}) collective-permute-start(f32[136,128]{1,0:T(8,128)S(1)} %add.23), channel_id=1, source_target_pairs={{0,16},{1,17},{2,18},{3,19},{4,20},{5,21},{6,22},{7,23},{8,24},{9,... | collective-permute-start | bytes 208904 | tf_op jit(solution)/shard_map/ppermute | solution.py:198
  37.7 2.6 %collective-permute-done.6 = f32[136,128]{1,0:T(8,128)S(1)} collective-permute-done((f32[136,128]{1,0:T(8,128)S(1)}, f32[136,128]{1,0:T(8,128)S(1)}, u32[]{:S(2)}, u32[]{:S(2)}) %collective-permute-start.6) | collective-permute-done | bytes 69664 | tf_op jit(solution)/shard_map/ppermute | solution.py:198
  40.3 5.9 %finish.1 = (f32[512,128]{1,0:T(8,128)}, f32[128,128]{1,0:T(8,128)}, f32[128,128]{1,0:T(8,128)}) custom-call(f32[136,128]{1,0:T(8,128)S(1)} %add.24.refs_0_, f32[512,128]{1,0:T(8,128)S(1)} %get-tuple-element.19.refs_1_), custom_call_target="tpu_custom_call" | custom-call | tf_op jit(solution)/shard_map/finish/pallas_call | solution.py:253
  (5 shorter events, 0.0 us)
Async XLA Ops:
  0.7 1.0 %copy-start = (f32[512,128]{1,0:T(8,128)S(1)}, f32[512,128]{1,0:T(8,128)}, u32[]{:S(2)}) copy-start(f32[512,128]{1,0:T(8,128)} %s_ref.3) | copy-start | bytes 786436
  1.7 0.9 %copy-start.1 = (f32[4,128,128]{2,1,0:T(8,128)S(1)}, f32[4,128,128]{2,1,0:T(8,128)}, u32[]{:S(2)}) copy-start(f32[4,128,128]{2,1,0:T(8,128)} %c_ref.3) | copy-start | bytes 786436
  2.6 0.9 %copy-start.3 = (f32[4,128,128]{2,1,0:T(8,128)S(1)}, f32[4,128,128]{2,1,0:T(8,128)}, u32[]{:S(2)}) copy-start(f32[4,128,128]{2,1,0:T(8,128)} %d_ref.1) | copy-start | bytes 786436
  3.6 3.3 %copy-start.2 = (f32[4,128,128]{2,1,0:T(8,128)S(1)}, f32[4,128,128]{2,1,0:T(8,128)}, u32[]{:S(2)}) copy-start(f32[4,128,128]{2,1,0:T(8,128)} %c_ref.3) | copy-start | bytes 786436
  5.1 1.7 %collective-permute-start = (f32[4,128,128]{2,1,0:T(8,128)S(1)}, f32[4,128,128]{2,1,0:T(8,128)S(1)}, u32[]{:S(2)}, u32[]{:S(2)}) collective-permute-start(f32[4,128,128]{2,1,0:T(8,128)S(1)} %get-tuple-element.16), channel_id=1, source_target_pairs={{0,1},{1,0},{2,3},{3,2},{4,5},{5,4},{6,7},{7,6},{8,9},{9,8},{10,11... | collective-permute-start | bytes 786440 | tf_op jit(solution)/shard_map/ppermute | solution.py:223
  5.7 1.2 %collective-permute-start.1 = (f32[4,128,128]{2,1,0:T(8,128)S(1)}, f32[4,128,128]{2,1,0:T(8,128)S(1)}, u32[]{:S(2)}, u32[]{:S(2)}) collective-permute-start(f32[4,128,128]{2,1,0:T(8,128)S(1)} %get-tuple-element.17), channel_id=1, source_target_pairs={{1,2},{2,1},{3,4},{4,3},{5,6},{6,5},{7,8},{8,7},{9,10},{10,9},{11,... | collective-permute-start | bytes 786440 | tf_op jit(solution)/shard_map/ppermute | solution.py:223
  9.9 10.3 %collective-permute-start.2 = (f32[136,128]{1,0:T(8,128)S(1)}, f32[136,128]{1,0:T(8,128)S(1)}, u32[]{:S(2)}, u32[]{:S(2)}) collective-permute-start(f32[136,128]{1,0:T(8,128)S(1)} %get-tuple-element.18), channel_id=1, source_target_pairs={{0,1},{1,0},{2,3},{3,2},{4,5},{5,4},{6,7},{7,6},{8,9},{9,8},{10,11... | collective-permute-start | bytes 208904 | tf_op jit(solution)/shard_map/ppermute | solution.py:198
  20.2 6.1 %collective-permute-start.3 = (f32[136,128]{1,0:T(8,128)S(1)}, f32[136,128]{1,0:T(8,128)S(1)}, u32[]{:S(2)}, u32[]{:S(2)}) collective-permute-start(f32[136,128]{1,0:T(8,128)S(1)} %add.20), channel_id=1, source_target_pairs={{0,2},{1,3},{2,0},{3,1},{4,6},{5,7},{6,4},{7,5},{8,10},{9,11},{10,... | collective-permute-start | bytes 208904 | tf_op jit(solution)/shard_map/ppermute | solution.py:198
  26.2 4.4 %collective-permute-start.4 = (f32[136,128]{1,0:T(8,128)S(1)}, f32[136,128]{1,0:T(8,128)S(1)}, u32[]{:S(2)}, u32[]{:S(2)}) collective-permute-start(f32[136,128]{1,0:T(8,128)S(1)} %add.21), channel_id=1, source_target_pairs={{0,4},{1,5},{2,6},{3,7},{4,0},{5,1},{6,2},{7,3},{8,12},{9,13},{10,... | collective-permute-start | bytes 208904 | tf_op jit(solution)/shard_map/ppermute | solution.py:198
  30.6 4.4 %collective-permute-start.5 = (f32[136,128]{1,0:T(8,128)S(1)}, f32[136,128]{1,0:T(8,128)S(1)}, u32[]{:S(2)}, u32[]{:S(2)}) collective-permute-start(f32[136,128]{1,0:T(8,128)S(1)} %add.22), channel_id=1, source_target_pairs={{0,8},{1,9},{2,10},{3,11},{4,12},{5,13},{6,14},{7,15},{8,0},{9,1},... | collective-permute-start | bytes 208904 | tf_op jit(solution)/shard_map/ppermute | solution.py:198
  35.0 5.3 %collective-permute-start.6 = (f32[136,128]{1,0:T(8,128)S(1)}, f32[136,128]{1,0:T(8,128)S(1)}, u32[]{:S(2)}, u32[]{:S(2)}) collective-permute-start(f32[136,128]{1,0:T(8,128)S(1)} %add.23), channel_id=1, source_target_pairs={{0,16},{1,17},{2,18},{3,19},{4,20},{5,21},{6,22},{7,23},{8,24},{9,... | collective-permute-start | bytes 208904 | tf_op jit(solution)/shard_map/ppermute | solution.py:198

commit v2 on v0

v2 whole, which is shorter than its diff:
```python
import math

import jax
import jax.numpy as jnp
from jax import lax
from jax.experimental import pallas as pl
from jax.experimental.pallas import tpu as pltpu
from jax.sharding import PartitionSpec as P

center = 0.5
half_width = 4.0
scale = 2.0 / half_width
here = pl.BlockSpec(memory_space=pltpu.VMEM)
far = pl.BlockSpec(memory_space=pltpu.HBM)


def two(x):
    high = x.astype(jnp.bfloat16)
    return high, (x - high.astype(jnp.float32)).astype(jnp.bfloat16)


def three(x):
    high = x.astype(jnp.bfloat16)
    rest = x - high.astype(jnp.float32)
    mid = rest.astype(jnp.bfloat16)
    return high, mid, (rest - mid.astype(jnp.float32)).astype(jnp.bfloat16)


def dot(a, b, on=(1, 0)):
    return lax.dot_general(a, b, (((on[0],), (on[1],)), ((), ())), preferred_element_type=jnp.float32)


def left3(x, axis=1):
    high, low = two(x)
    return jnp.concatenate([high, high, low], axis)


def right3(x, axis=0):
    high, low = two(x)
    return jnp.concatenate([high, low, high], axis)


def left6(x, axis=1):
    high, mid, low = three(x)
    return jnp.concatenate([high, high, mid, high, low, mid], axis)


def right6(x, axis=0):
    high, mid, low = three(x)
    return jnp.concatenate([high, mid, high, low, high, mid], axis)


def iotas(shape):
    return (
        lax.broadcasted_iota(jnp.int32, shape, 0),
        lax.broadcasted_iota(jnp.int32, shape, 1),
    )


def symmetric(d):
    rows, cols = iotas(d.shape)
    return 0.5 * (d + d.T) - jnp.where(rows == cols, center, 0.0)


def leftward(s0, s1, s2, sym0, sym1, c0, c1, out_ref):
    l0, r0, r1 = left3(sym0), right3(s0), right3(s1)
    c0l = left3(c0)
    part = (dot(l0, r0) + dot(c0l, r1)) / half_width
    first1 = (dot(left3(sym1), r1) + dot(left3(c1), right3(s2)) + dot(left3(c0.T), r0)) / half_width
    out_ref[0] = s0
    out_ref[1] = part
    out_ref[2] = scale * (dot(l0, right3(part)) + dot(c0l, right3(first1))) - s0
    out_ref[3] = sym0


def rightward(s_prev, s_last, sym_last, c_prev, c_last, out_ref):
    rl = right3(s_last)
    part = (dot(left3(sym_last), rl) + dot(left3(c_prev.T), right3(s_prev))) / half_width
    turned = left3(c_last.T)
    out_ref[0] = dot(turned, rl)
    out_ref[1] = dot(turned, right3(part))
    out_ref[2] = c_last
    out_ref[3] = jnp.zeros_like(c_last)


def edge(axis, s_hbm, d_hbm, c_hbm, odd_ref, s_ref, d_ref, c_ref, sems):
    nblocks = d_hbm.shape[0]
    last = nblocks - 1
    parity = lax.rem(lax.axis_index(axis), 2)
    is_last = lax.axis_index(axis) == lax.axis_size(axis) - 1
    copies = []
    for k, (source, target) in enumerate(((s_hbm, s_ref), (d_hbm, d_ref), (c_hbm, c_ref))):
        copies.append(pltpu.make_async_copy(source, target, sems.at[k]))
    for copy in copies:
        copy.start()
    for copy in copies:
        copy.wait()

    @pl.when(is_last)
    def _():
        c_ref[last] = jnp.zeros_like(c_ref[last])

    @pl.when(parity == 0)
    def _():
        leftward(s_ref[0], s_ref[1], s_ref[2], symmetric(d_ref[0]), symmetric(d_ref[1]), c_ref[0], c_ref[1], odd_ref)

    @pl.when(parity != 0)
    def _():
        rightward(s_ref[last - 1], s_ref[last], symmetric(d_ref[last]), c_ref[last - 1], c_ref[last], odd_ref)


def inner(axis, s_ref, d_ref, c_ref, even_ref, sym_ref, cl_ref, ct_ref, first_ref, pre_ref, pass_ref):
    nblocks = d_ref.shape[0]
    last = nblocks - 1
    parity = lax.rem(lax.axis_index(axis), 2)

    @pl.when(parity != 0)
    def _():
        leftward(s_ref[0], s_ref[1], s_ref[2], symmetric(d_ref[0]), symmetric(d_ref[1]), c_ref[0], c_ref[1], even_ref)

    @pl.when(parity == 0)
    def _():
        rightward(s_ref[last - 1], s_ref[last], symmetric(d_ref[last]), c_ref[last - 1], c_ref[last], even_ref)

    s = [s_ref[b] for b in range(nblocks)]
    sr = [right3(x) for x in s]
    for b in range(nblocks):
        sym_ref[b] = left3(symmetric(d_ref[b]))
        cl_ref[b] = left3(c_ref[b])
        ct_ref[b] = left3(c_ref[b].T)
    first = []
    for b in range(nblocks):
        acc = dot(sym_ref[b], sr[b])
        if b < last:
            acc += dot(cl_ref[b], sr[b + 1])
        if b > 0:
            acc += dot(ct_ref[b - 1], sr[b - 1])
        first.append(acc / half_width)
        first_ref[b] = first[b]
    pass_ref[...] = dot(ct_ref[last], sr[last])
    fr = [right3(x) for x in first]
    for b in range(nblocks):
        acc = None
        terms = []
        if 0 < b < last:
            terms.append((sym_ref, b, b))
        if b + 1 < last:
            terms.append((cl_ref, b, b + 1))
        if b > 1:
            terms.append((ct_ref, b - 1, b - 1))
        for ref, which, operand in terms:
            term = dot(ref[which], fr[operand])
            acc = term if acc is None else acc + term
        pre_ref[b] = -s[b] if acc is None else scale * acc - s[b]


def project(axis, s_ref, sym_ref, cl_ref, ct_ref, first_ref, pre_ref, pass_ref, even_ref, odd_ref, filt_ref, keep_ref, send_ref):
    nblocks, block, unused = s_ref.shape
    last = nblocks - 1
    parity = lax.rem(lax.axis_index(axis), 2)
    right = [jnp.where(parity == 0, even_ref[k], odd_ref[k]) for k in range(4)]
    left = [jnp.where(parity == 0, odd_ref[k], even_ref[k]) for k in range(3)]
    onward = pass_ref[...]
    tail = first_ref[last] + dot(cl_ref[last], right3(right[0])) / half_width
    head = first_ref[0] + left[0] / half_width
    ahead = right[1] + onward / half_width
    back = dot(left3(left[2]), right3(s_ref[0]))
    behind = left[1] + dot(left3(left[2].T), right3(back)) / half_width
    tail_r, head_r = right3(tail), right3(head)
    filtered = [pre_ref[b] for b in range(nblocks)]
    filtered[0] += scale * (dot(sym_ref[0], head_r) + behind)
    filtered[1] += scale * dot(ct_ref[0], head_r)
    filtered[last - 1] += scale * dot(cl_ref[last - 1], tail_r)
    filtered[last] += scale * (dot(sym_ref[last], tail_r) + dot(cl_ref[last], right3(ahead)))
    beyond = right[2] + scale * (dot(left3(right[3]), right3(onward)) / half_width + dot(ct_ref[last], tail_r))
    filtered.append(beyond)
    fr = [right3(x) for x in filtered]
    both = []
    for b in range(nblocks):
        filt_ref[b] = filtered[b]
        image = 0.5 * (dot(sym_ref[b], fr[b]) + center * filtered[b]) + dot(cl_ref[b], fr[b + 1])
        both.append(jnp.concatenate([filtered[b], image], 1))
    total = None
    for b in range(nblocks):
        term = dot(left6(filtered[b], 0), right6(both[b], 0), (0, 0))
        total = term if total is None else total + term
    width = filtered[0].shape[1]
    correlation, half = total[:, :width], total[:, width:]
    mixed = half + half.T
    rows, cols = iotas((width, width))
    packed = jnp.where(rows >= cols, correlation, mixed)
    diagonal = jnp.sum(jnp.where(rows == cols, mixed, 0.0), axis=0, keepdims=True)
    mid = width // 2

    def put(top_ref, low_ref):
        top_ref[0:mid, :] = packed[:mid]
        top_ref[mid : mid + 8, :] = jnp.broadcast_to(diagonal, (8, width))
        low_ref[0:mid, :] = packed[mid:]
        low_ref[mid : mid + 8, :] = jnp.broadcast_to(diagonal, (8, width))

    @pl.when(parity == 0)
    def _():
        put(keep_ref, send_ref)

    @pl.when(parity != 0)
    def _():
        put(send_ref, keep_ref)


def factor(full, inv_ref):
    width = full.shape[1]
    tiles = width // 8
    sub, lane = iotas((8, width))
    work = [full[8 * t : 8 * t + 8, :] for t in range(tiles)]
    nought = jnp.where(lane < 0, 1.0, 0.0)
    for p in range(tiles):
        at = 8 * p
        inside = (lane >= at) & (lane < at + 8)
        column = [jnp.broadcast_to(work[p][:, at + j : at + j + 1], (8, width)) + nought for j in range(8)]
        a = {}
        for j in range(8):
            for i in range(j, 8):
                a[i, j] = jnp.broadcast_to(column[j][i : i + 1, :], (8, width))
        m, recip = {}, []
        for j in range(8):
            recip.append(1.0 / a[j, j])
            for i in range(j + 1, 8):
                m[i, j] = a[i, j] * recip[j]
            for i in range(j + 1, 8):
                for k in range(j + 1, i + 1):
                    a[i, k] = a[i, k] - m[i, j] * a[k, j]
        cleared = jnp.where(inside, jnp.where(lane == sub + at, 1.0, 0.0), work[p])
        pivot = []
        for j in range(8):
            r = jnp.broadcast_to(cleared[j : j + 1, :], (8, width))
            for k in range(j):
                r = r - m[j, k] * pivot[k]
            pivot.append(r)
        out = jnp.zeros((8, width), jnp.float32)
        for j in range(8):
            out = jnp.where(sub == j, pivot[j] * lax.rsqrt(a[j, j]), out)
        inv_ref[at : at + 8, :] = jnp.where(lane <= sub + at, out, 0.0)
        scaled = [pivot[j] * recip[j] for j in range(8)]
        solved = [None] * 8
        for k in reversed(range(8)):
            q = scaled[k]
            for j in range(k + 1, 8):
                q = q - m[j, k] * solved[j]
            solved[k] = q
        for t in range(p + 1, tiles):
            raw = [jnp.broadcast_to(work[t][:, at + j : at + j + 1], (8, width)) for j in range(8)]
            acc = jnp.where(inside, 0.0, work[t])
            if t == p + 1:
                w = []
                for j in range(8):
                    x = raw[j]
                    for k in range(j):
                        x = x - w[k] * m[j, k]
                    w.append(x)
                    acc = acc - x * scaled[j]
            else:
                for j in range(8):
                    acc = acc - raw[j] * solved[j]
            work[t] = acc


def finish(axis, total_nodes, mine_ref, other_ref, filt_ref, orth_hbm, proj_hbm, inv_ref, orth_ref, proj_ref, sems):
    nblocks, block, width = filt_ref.shape
    mid = width // 2
    swapped = lax.rem(lax.axis_index(axis), 2) != 0
    mine, other = mine_ref[...], other_ref[...]
    top = jnp.where(swapped, other, mine)
    low = jnp.where(swapped, mine, other)
    packed = jnp.concatenate([top[:mid], low[:mid]], 0)
    rows, cols = iotas((width, width))
    turned = packed.T
    full = jnp.where(rows >= cols, packed, turned)
    mixed = jnp.where(rows < cols, packed, jnp.where(rows > cols, turned, top[mid : mid + 1, :]))
    factor(full, inv_ref)
    inv = inv_ref[...]
    inv_r = right6(inv, 1)
    copies = []
    grown = right6(inv * math.sqrt(total_nodes), 1)
    for b in range(nblocks):
        orth_ref[b] = dot(left6(filt_ref[b]), grown, (1, 1))
        copies.append(pltpu.make_async_copy(orth_ref.at[b], orth_hbm.at[b], sems.at[b]))
        copies[b].start()
    half = dot(left6(inv), right6(mixed))
    proj_ref[...] = dot(left6(half), inv_r, (1, 1))
    copies.append(pltpu.make_async_copy(proj_ref, proj_hbm, sems.at[nblocks]))
    copies[nblocks].start()
    for copy in copies:
        copy.wait()


def shape(*dims, kind=jnp.float32):
    return jax.ShapeDtypeStruct(dims, kind)


def add_up(values, axis, stride=1):
    count = lax.axis_size(axis)
    index = lax.axis_index(axis)
    while stride < count:
        left = count // stride
        radix = next(r for r in range(2, left + 1) if left % r == 0)
        if radix == 2:
            route = [(i, i + stride if (i // stride) % 2 == 0 else i - stride) for i in range(count)]
            values = values + lax.ppermute(values, axis, route)
        else:
            place = (index // stride) % radix
            parts = [values]
            for hop in range(1, radix):
                route = []
                for i in range(count):
                    digit = (i // stride) % radix
                    route.append((i, i + ((digit - hop) % radix - digit) * stride))
                parts.append(lax.ppermute(values, axis, route))
            stacked = jnp.stack(parts)
            total = None
            for digit in range(radix):
                term = lax.dynamic_index_in_dim(stacked, (digit - place) % radix, 0, keepdims=False)
                total = term if total is None else total + term
            values = total
        stride *= radix
    return values


def swap(values, axis, start):
    count = lax.axis_size(axis)
    route = []
    for i in range(start, count - 1, 2):
        route += [(i, i + 1), (i + 1, i)]
    return lax.ppermute(values, axis, route)


def body(states, diag_blocks, couplings):
    axis = "dom"
    nodes_dev, width = states.shape
    nblocks, block, unused = diag_blocks.shape
    devices = lax.axis_size(axis)
    field = states.reshape(nblocks, block, width)
    params = pltpu.CompilerParams(vmem_limit_bytes=40 << 20)
    cross = shape(4, block, width)
    tall = shape(nblocks, block, width)
    square = shape(nblocks, block, block)
    wide = shape(nblocks, block, 3 * block, kind=jnp.bfloat16)

    def call(kernel, name, ins, outs, scratch=()):
        return pl.pallas_call(
            kernel,
            out_shape=tuple(s for s, spec in outs),
            in_specs=ins,
            out_specs=tuple(spec for s, spec in outs),
            scratch_shapes=scratch,
            compiler_params=params,
            name=name,
        )

    odd, s, d, c = call(
        lambda *refs: edge(axis, *refs),
        "edge",
        [far] * 3,
        [(cross, here), (tall, here), (square, here), (square, here)],
        [pltpu.SemaphoreType.DMA((3,))],
    )(*(pltpu.with_memory_space_constraint(x, pltpu.HBM) for x in (field, diag_blocks, couplings)))
    odd = swap(odd, axis, 1)
    even, sym, cl, ct, first, pre, onward = call(
        lambda *refs: inner(axis, *refs),
        "inner",
        [here] * 3,
        [(cross, here), (wide, here), (wide, here), (wide, here), (tall, here), (tall, here), (shape(block, width), here)],
    )(s, d, c)
    even = swap(even, axis, 0)
    piece = shape(width // 2 + 8, width)
    filtered, keep, send = call(
        lambda *refs: project(axis, *refs),
        "project",
        [here] * 9,
        [(tall, here), (piece, here), (piece, here)],
    )(s, sym, cl, ct, first, pre, onward, even, odd)
    mine = add_up(keep + swap(send, axis, 0), axis, 2)
    other = swap(mine, axis, 0)
    orthonormal, projected = call(
        lambda *refs: finish(axis, nodes_dev * devices, *refs),
        "finish",
        [here] * 3,
        [(tall, far), (shape(width, width), far)],
        [
            pltpu.VMEM((width, width), jnp.float32),
            pltpu.VMEM((nblocks, block, width), jnp.float32),
            pltpu.VMEM((width, width), jnp.float32),
            pltpu.SemaphoreType.DMA((nblocks + 1,)),
        ],
    )(mine, other, filtered)
    return orthonormal.reshape(nodes_dev, width), projected


def solution(mesh):
    in_specs = (P("dom", None), P("dom", None, None), P("dom", None, None))
    out_specs = (P("dom", None), P())
    return jax.shard_map(body, mesh=mesh, in_specs=in_specs, out_specs=out_specs, check_vma=False)
```

time: 209 us -> 39.1 us (0.19)
  waiting for transfers between devices: 140 us -> 12.1 us
  other arithmetic: 22.9 us -> 0.03 us
  between operations: 14.3 us -> 0.67 us
  Pallas kernels: 0 us -> 8.51 us
  matrix products: 7.64 us -> 0 us
  starting transfers between devices: 21.6 us -> 17.7 us
  local copies, waits for them, and re-layouts: 2.95 us -> 0 us
    psum x1 -> x0, waiting for transfers between devices: 136 us -> none  [body(): lax.psum((gram_matrix(flat, flat), gram_matrix(flat, image)), 'dom')]
    another operation x5 -> x0, other arithmetic: 22.9 us -> none  [the longest x3 12.4 us: body(): lower = jnp.linalg.cholesky(correlation)]
    pallas_call x0 -> x4, Pallas kernels: none -> 8.51 us  [the longest x1 4.19 us: body(): call(lambda *refs: finish(axis, nodes_dev * devices, *refs), 'finish', [h...]
    ppermute x7 -> x8, waiting for transfers between devices: 3.74 us -> 12.1 us  [the longest x4 8.83 us: add_up(): values = values + lax.ppermute(values, axis, route)]
    dot_general x11 -> x0, matrix products: 6.01 us -> none  [the longest x2 2.44 us: gram_matrix(): return jnp.einsum('ns,nt->st', left, right, precision=lax.Precision.HIGHEST)]
    ppermute x7 -> x8, starting transfers between devices: 21.5 us -> 17.7 us  [the longest x4 8.89 us: add_up(): values = values + lax.ppermute(values, axis, route)]
  transfers between devices with their start and end apart: 8 -> 8, of which waited for: 3 -> 7; matrix products, arithmetic and copies ran while one was open for 2% -> 0% of each run, Pallas kernels for 0% -> 3%
where the time goes in v2:
time: 39.1 us; the launch traced here: 39 us
  starting transfers between devices  17.7 us (45%)
  waiting for transfers between devices  12.1 us (31%)
  Pallas kernels  8.51 us (22%)
  between operations  0.67 us (2%)
    ppermute x4, starting transfers between devices, add_up(): values = values + lax.ppermute(values, axis, route)  8.89 us
    ppermute x4, waiting for transfers between devices, add_up(): values = values + lax.ppermute(values, axis, route)  8.83 us
    ppermute x4, starting transfers between devices, swap(): return lax.ppermute(values, axis, route)  8.82 us
    pallas_call x1, Pallas kernels, body(): call(lambda *refs: finish(axis, nodes_dev * devices, *refs), 'finish', [h...  4.19 us
    ppermute x4, waiting for transfers between devices, swap(): return lax.ppermute(values, axis, route)  3.23 us
    pallas_call x1, Pallas kernels, body(): call(lambda *refs: edge(axis, *refs), 'edge', [far] * 3, [(cross, here),...  1.64 us
    pallas_call x1, Pallas kernels, body(): call(lambda *refs: project(axis, *refs), 'project', [here] * 9, [(tall, h...  1.51 us
    pallas_call x1, Pallas kernels, body(): call(lambda *refs: inner(axis, *refs), 'inner', [here] * 3, [(cross, here...  1.18 us
  transfers between devices with their start and end apart: 8, of which 7 were waited for; matrix products, arithmetic and copies ran while one was open for 0% of the time, Pallas kernels for 3%

profile of v2, /device:TPU:0, one launch (start us, length us, event | category | flops | bytes accessed | tf_op | source)
XLA Modules:
  0.0 39.0 jit_solution(15707725742325805184)
XLA Ops:
  0.6 1.6 %edge.1 = (f32[4,128,128]{2,1,0:T(8,128)S(1)}, f32[4,128,128]{2,1,0:T(8,128)S(1)}, f32[4,128,128]{2,1,0:T(8,128)S(1)}, f32[4,128,128]{2,1,0:T(8,128)S(1)}) custom-call(f32[4,128,128]{2,1,0:T(8,128)} %bitcast.2, f32[4,128,128]{2,1,0:T(8,128)} %refs_1_.1, f32[4,128,128]{2,1,0:T(8,128)} %refs_2_.1), custom_call_target="tpu_custom_call" | custom-call | tf_op jit(solution)/shard_map/edge/pallas_call | solution.py:359
  2.3 0.7 %collective-permute-start.1 = (f32[4,128,128]{2,1,0:T(8,128)S(1)}, f32[4,128,128]{2,1,0:T(8,128)S(1)}, u32[]{:S(2)}, u32[]{:S(2)}) collective-permute-start(f32[4,128,128]{2,1,0:T(8,128)S(1)} %get-tuple-element.28), channel_id=1, source_target_pairs={{1,2},{2,1},{3,4},{4,3},{5,6},{6,5},{7,8},{8,7},{9,10},{10,9},{11,... | collective-permute-start | bytes 786440 | tf_op jit(solution)/shard_map/ppermute | solution.py:333
  3.0 1.2 %inner.1 = (f32[4,128,128]{2,1,0:T(8,128)S(1)}, bf16[4,128,384]{2,1,0:T(8,128)(2,1)S(1)}, bf16[4,128,384]{2,1,0:T(8,128)(2,1)S(1)}, bf16[4,128,384]{2,1,0:T(8,12...) custom-call(f32[4,128,128]{2,1,0:T(8,128)S(1)} %get-tuple-element.18.refs_0_, ...), custom_call_target="tpu_custom_call" | custom-call | tf_op jit(solution)/shard_map/inner/pallas_call | solution.py:367
  4.1 4.4 %collective-permute-start = (f32[4,128,128]{2,1,0:T(8,128)S(1)}, f32[4,128,128]{2,1,0:T(8,128)S(1)}, u32[]{:S(2)}, u32[]{:S(2)}) collective-permute-start(f32[4,128,128]{2,1,0:T(8,128)S(1)} %get-tuple-element.27), channel_id=1, source_target_pairs={{0,1},{1,0},{2,3},{3,2},{4,5},{5,4},{6,7},{7,6},{8,9},{9,8},{10,11... | collective-permute-start | bytes 786440 | tf_op jit(solution)/shard_map/ppermute | solution.py:333
  8.6 0.0 collective-permute-done.1.refs_8_
  8.6 1.2 %collective-permute-done.refs_7_ = f32[4,128,128]{2,1,0:T(8,128)S(1)} collective-permute-done((f32[4,128,128]{2,1,0:T(8,128)S(1)}, f32[4,128,128]{2,1,0:T(8,128)S(1)}, u32[]{:S(2)}, u32[]{:S(2)}) %collective-permute-start) | collective-permute-done | bytes 262176 | tf_op jit(solution)/shard_map/ppermute | solution.py:333
  9.7 1.5 %project.1 = (f32[4,128,128]{2,1,0:T(8,128)S(1)}, f32[72,128]{1,0:T(8,128)S(1)}, f32[72,128]{1,0:T(8,128)S(1)}) custom-call(f32[4,128,128]{2,1,0:T(8,128)S(1)} %get-tuple-element.18.refs_0_, bf16[4,128,384]{2,1,0:T(8,128)(2,1)S(1)} %get-tuple-element.21.refs_1_, bf16[4,128,384]{2,1,0:T(8,128)(2,1)S(1)} %get-tuple-element.22.refs_2_, ...), custom_call_target="tpu_custom_call" | custom-call | tf_op jit(solution)/shard_map/project/pallas_call | solution.py:375
  11.2 3.7 %collective-permute-start.2 = (f32[72,128]{1,0:T(8,128)S(1)}, f32[72,128]{1,0:T(8,128)S(1)}, u32[]{:S(2)}, u32[]{:S(2)}) collective-permute-start(f32[72,128]{1,0:T(8,128)S(1)} %get-tuple-element.30), channel_id=1, source_target_pairs={{0,1},{1,0},{2,3},{3,2},{4,5},{5,4},{6,7},{7,6},{8,9},{9,8},{10,11... | collective-permute-start | bytes 110600 | tf_op jit(solution)/shard_map/ppermute | solution.py:333
  15.0 0.9 %collective-permute-done.2 = f32[72,128]{1,0:T(8,128)S(1)} collective-permute-done((f32[72,128]{1,0:T(8,128)S(1)}, f32[72,128]{1,0:T(8,128)S(1)}, u32[]{:S(2)}, u32[]{:S(2)}) %collective-permute-start.2) | collective-permute-done | bytes 36896 | tf_op jit(solution)/shard_map/ppermute | solution.py:333
  15.8 3.0 %collective-permute-start.3 = (f32[72,128]{1,0:T(8,128)S(1)}, f32[72,128]{1,0:T(8,128)S(1)}, u32[]{:S(2)}, u32[]{:S(2)}) collective-permute-start(f32[72,128]{1,0:T(8,128)S(1)} %add.15), channel_id=1, source_target_pairs={{0,2},{1,3},{2,0},{3,1},{4,6},{5,7},{6,4},{7,5},{8,10},{9,11},{10,... | collective-permute-start | bytes 110600 | tf_op jit(solution)/shard_map/ppermute | solution.py:308
  18.8 2.0 %collective-permute-done.3 = f32[72,128]{1,0:T(8,128)S(1)} collective-permute-done((f32[72,128]{1,0:T(8,128)S(1)}, f32[72,128]{1,0:T(8,128)S(1)}, u32[]{:S(2)}, u32[]{:S(2)}) %collective-permute-start.3) | collective-permute-done | bytes 36896 | tf_op jit(solution)/shard_map/ppermute | solution.py:308
  20.8 1.7 %collective-permute-start.4 = (f32[72,128]{1,0:T(8,128)S(1)}, f32[72,128]{1,0:T(8,128)S(1)}, u32[]{:S(2)}, u32[]{:S(2)}) collective-permute-start(f32[72,128]{1,0:T(8,128)S(1)} %add.16), channel_id=1, source_target_pairs={{0,4},{1,5},{2,6},{3,7},{4,0},{5,1},{6,2},{7,3},{8,12},{9,13},{10,... | collective-permute-start | bytes 110600 | tf_op jit(solution)/shard_map/ppermute | solution.py:308
  22.5 2.2 %collective-permute-done.4 = f32[72,128]{1,0:T(8,128)S(1)} collective-permute-done((f32[72,128]{1,0:T(8,128)S(1)}, f32[72,128]{1,0:T(8,128)S(1)}, u32[]{:S(2)}, u32[]{:S(2)}) %collective-permute-start.4) | collective-permute-done | bytes 36896 | tf_op jit(solution)/shard_map/ppermute | solution.py:308
  24.8 1.6 %collective-permute-start.5 = (f32[72,128]{1,0:T(8,128)S(1)}, f32[72,128]{1,0:T(8,128)S(1)}, u32[]{:S(2)}, u32[]{:S(2)}) collective-permute-start(f32[72,128]{1,0:T(8,128)S(1)} %add.17), channel_id=1, source_target_pairs={{0,8},{1,9},{2,10},{3,11},{4,12},{5,13},{6,14},{7,15},{8,0},{9,1},... | collective-permute-start | bytes 110600 | tf_op jit(solution)/shard_map/ppermute | solution.py:308
  26.3 2.4 %collective-permute-done.5 = f32[72,128]{1,0:T(8,128)S(1)} collective-permute-done((f32[72,128]{1,0:T(8,128)S(1)}, f32[72,128]{1,0:T(8,128)S(1)}, u32[]{:S(2)}, u32[]{:S(2)}) %collective-permute-start.5) | collective-permute-done | bytes 36896 | tf_op jit(solution)/shard_map/ppermute | solution.py:308
  28.7 2.6 %collective-permute-start.6 = (f32[72,128]{1,0:T(8,128)S(1)}, f32[72,128]{1,0:T(8,128)S(1)}, u32[]{:S(2)}, u32[]{:S(2)}) collective-permute-start(f32[72,128]{1,0:T(8,128)S(1)} %add.18), channel_id=1, source_target_pairs={{0,16},{1,17},{2,18},{3,19},{4,20},{5,21},{6,22},{7,23},{8,24},{9,... | collective-permute-start | bytes 110600 | tf_op jit(solution)/shard_map/ppermute | solution.py:308
  31.3 2.2 %collective-permute-done.6 = f32[72,128]{1,0:T(8,128)S(1)} collective-permute-done((f32[72,128]{1,0:T(8,128)S(1)}, f32[72,128]{1,0:T(8,128)S(1)}, u32[]{:S(2)}, u32[]{:S(2)}) %collective-permute-start.6) | collective-permute-done | bytes 36896 | tf_op jit(solution)/shard_map/ppermute | solution.py:308
  33.6 0.0 collective-permute-start.7
  33.6 1.2 %collective-permute-done.7.refs_1_ = f32[72,128]{1,0:T(8,128)S(1)} collective-permute-done((f32[72,128]{1,0:T(8,128)S(1)}, f32[72,128]{1,0:T(8,128)S(1)}, u32[]{:S(2)}, u32[]{:S(2)}) %collective-permute-start.7) | collective-permute-done | bytes 36896 | tf_op jit(solution)/shard_map/ppermute | solution.py:333
  34.8 4.2 %finish.1 = (f32[4,128,128]{2,1,0:T(8,128)}, f32[128,128]{1,0:T(8,128)}) custom-call(f32[72,128]{1,0:T(8,128)S(1)} %add.19.refs_0_, f32[72,128]{1,0:T(8,128)S(1)} %collective-permute-done.7.refs_1_, f32[4,128,128]{2,1,0:T(8,128)S(1)} %get-tuple-element.31.refs_2_), custom_call_target="tpu_custom_call" | custom-call | tf_op jit(solution)/shard_map/finish/pallas_call | solution.py:383
  (5 shorter events, 0.0 us)
Async XLA Ops:
  2.3 6.3 %collective-permute-start.1 = (f32[4,128,128]{2,1,0:T(8,128)S(1)}, f32[4,128,128]{2,1,0:T(8,128)S(1)}, u32[]{:S(2)}, u32[]{:S(2)}) collective-permute-start(f32[4,128,128]{2,1,0:T(8,128)S(1)} %get-tuple-element.28), channel_id=1, source_target_pairs={{1,2},{2,1},{3,4},{4,3},{5,6},{6,5},{7,8},{8,7},{9,10},{10,9},{11,... | collective-permute-start | bytes 786440 | tf_op jit(solution)/shard_map/ppermute | solution.py:333
  4.1 5.6 %collective-permute-start = (f32[4,128,128]{2,1,0:T(8,128)S(1)}, f32[4,128,128]{2,1,0:T(8,128)S(1)}, u32[]{:S(2)}, u32[]{:S(2)}) collective-permute-start(f32[4,128,128]{2,1,0:T(8,128)S(1)} %get-tuple-element.27), channel_id=1, source_target_pairs={{0,1},{1,0},{2,3},{3,2},{4,5},{5,4},{6,7},{7,6},{8,9},{9,8},{10,11... | collective-permute-start | bytes 786440 | tf_op jit(solution)/shard_map/ppermute | solution.py:333
  11.2 4.6 %collective-permute-start.2 = (f32[72,128]{1,0:T(8,128)S(1)}, f32[72,128]{1,0:T(8,128)S(1)}, u32[]{:S(2)}, u32[]{:S(2)}) collective-permute-start(f32[72,128]{1,0:T(8,128)S(1)} %get-tuple-element.30), channel_id=1, source_target_pairs={{0,1},{1,0},{2,3},{3,2},{4,5},{5,4},{6,7},{7,6},{8,9},{9,8},{10,11... | collective-permute-start | bytes 110600 | tf_op jit(solution)/shard_map/ppermute | solution.py:333
  15.8 4.9 %collective-permute-start.3 = (f32[72,128]{1,0:T(8,128)S(1)}, f32[72,128]{1,0:T(8,128)S(1)}, u32[]{:S(2)}, u32[]{:S(2)}) collective-permute-start(f32[72,128]{1,0:T(8,128)S(1)} %add.15), channel_id=1, source_target_pairs={{0,2},{1,3},{2,0},{3,1},{4,6},{5,7},{6,4},{7,5},{8,10},{9,11},{10,... | collective-permute-start | bytes 110600 | tf_op jit(solution)/shard_map/ppermute | solution.py:308
  20.8 4.0 %collective-permute-start.4 = (f32[72,128]{1,0:T(8,128)S(1)}, f32[72,128]{1,0:T(8,128)S(1)}, u32[]{:S(2)}, u32[]{:S(2)}) collective-permute-start(f32[72,128]{1,0:T(8,128)S(1)} %add.16), channel_id=1, source_target_pairs={{0,4},{1,5},{2,6},{3,7},{4,0},{5,1},{6,2},{7,3},{8,12},{9,13},{10,... | collective-permute-start | bytes 110600 | tf_op jit(solution)/shard_map/ppermute | solution.py:308
  24.8 4.0 %collective-permute-start.5 = (f32[72,128]{1,0:T(8,128)S(1)}, f32[72,128]{1,0:T(8,128)S(1)}, u32[]{:S(2)}, u32[]{:S(2)}) collective-permute-start(f32[72,128]{1,0:T(8,128)S(1)} %add.17), channel_id=1, source_target_pairs={{0,8},{1,9},{2,10},{3,11},{4,12},{5,13},{6,14},{7,15},{8,0},{9,1},... | collective-permute-start | bytes 110600 | tf_op jit(solution)/shard_map/ppermute | solution.py:308
  28.7 4.9 %collective-permute-start.6 = (f32[72,128]{1,0:T(8,128)S(1)}, f32[72,128]{1,0:T(8,128)S(1)}, u32[]{:S(2)}, u32[]{:S(2)}) collective-permute-start(f32[72,128]{1,0:T(8,128)S(1)} %add.18), channel_id=1, source_target_pairs={{0,16},{1,17},{2,18},{3,19},{4,20},{5,21},{6,22},{7,23},{8,24},{9,... | collective-permute-start | bytes 110600 | tf_op jit(solution)/shard_map/ppermute | solution.py:308
  33.6 1.2 %collective-permute-start.7 = (f32[72,128]{1,0:T(8,128)S(1)}, f32[72,128]{1,0:T(8,128)S(1)}, u32[]{:S(2)}, u32[]{:S(2)}) collective-permute-start(f32[72,128]{1,0:T(8,128)S(1)} %add.19.refs_0_), channel_id=1, source_target_pairs={{0,1},{1,0},{2,3},{3,2},{4,5},{5,4},{6,7},{7,6},{8,9},{9,8},{10,11... | collective-permute-start | bytes 110600 | tf_op jit(solution)/shard_map/ppermute | solution.py:333

commit v3 on v2

--- a/solution.py
+++ b/solution.py
@@ -302,19 +302,24 @@
     index = lax.axis_index(axis)
     while stride < count:
         left = count // stride
-        radix = next(r for r in range(2, left + 1) if left % r == 0)
-        if radix == 2:
-            route = [(i, i + stride if (i // stride) % 2 == 0 else i - stride) for i in range(count)]
-            values = values + lax.ppermute(values, axis, route)
+        radix = 4 if left % 4 == 0 else next(r for r in range(2, left + 1) if left % r == 0)
+
+        def route(partner):
+            digits = [(i // stride) % radix for i in range(count)]
+            return [(i, i + (partner(k) - k) * stride) for i, k in enumerate(digits)]
+
+        if radix in (2, 4):
+            parts = [values]
+            for flip in range(1, radix):
+                parts.append(lax.ppermute(values, axis, route(lambda k: k ^ flip)))
+            while len(parts) > 1:
+                parts = [a + b for a, b in zip(parts[::2], parts[1::2])]
+            values = parts[0]
         else:
             place = (index // stride) % radix
             parts = [values]
             for hop in range(1, radix):
-                route = []
-                for i in range(count):
-                    digit = (i // stride) % radix
-                    route.append((i, i + ((digit - hop) % radix - digit) * stride))
-                parts.append(lax.ppermute(values, axis, route))
+                parts.append(lax.ppermute(values, axis, route(lambda k: (k - hop) % radix)))
             stacked = jnp.stack(parts)
             total = None
             for digit in range(radix):

time: 39.1 us -> 38.4 us (0.982)
  waiting for transfers between devices: 12.1 us -> 11.2 us
    ppermute x4 -> x6, waiting for transfers between devices: 8.83 us -> 8.02 us  [add_up(): parts.append(lax.ppermute(values, axis, route(lambda k: k ^ flip)))]
    ppermute x4 -> x6, starting transfers between devices: 8.89 us -> 8.87 us  [add_up(): parts.append(lax.ppermute(values, axis, route(lambda k: k ^ flip)))]
  transfers between devices with their start and end apart: 8 -> 10, of which waited for: 7 -> 8; matrix products, arithmetic and copies ran while one was open for 0% -> 0% of each run, Pallas kernels for 3% -> 3%
where the time goes in v3:
time: 38.4 us; the launch traced here: 38.2 us
  starting transfers between devices  17.8 us (46%)
  waiting for transfers between devices  11.2 us (29%)
  Pallas kernels  8.51 us (22%)
  between operations  0.68 us (2%)
    ppermute x4, starting transfers between devices, swap(): return lax.ppermute(values, axis, route)  8.89 us
    ppermute x6, starting transfers between devices, add_up(): parts.append(lax.ppermute(values, axis, route(lambda k: k ^ flip)))  8.87 us
    ppermute x6, waiting for transfers between devices, add_up(): parts.append(lax.ppermute(values, axis, route(lambda k: k ^ flip)))  8.02 us
    pallas_call x1, Pallas kernels, body(): call(lambda *refs: finish(axis, nodes_dev * devices, *refs), 'finish', [h...  4.19 us
    ppermute x4, waiting for transfers between devices, swap(): return lax.ppermute(values, axis, route)  3.23 us
    pallas_call x1, Pallas kernels, body(): call(lambda *refs: edge(axis, *refs), 'edge', [far] * 3, [(cross, here),...  1.64 us
    pallas_call x1, Pallas kernels, body(): call(lambda *refs: project(axis, *refs), 'project', [here] * 9, [(tall, h...  1.51 us
    pallas_call x1, Pallas kernels, body(): call(lambda *refs: inner(axis, *refs), 'inner', [here] * 3, [(cross, here...  1.18 us
  transfers between devices with their start and end apart: 10, of which 8 were waited for; matrix products, arithmetic and copies ran while one was open for 0% of the time, Pallas kernels for 3%

profile of v3, /device:TPU:0, one launch (start us, length us, event | category | flops | bytes accessed | tf_op | source)
XLA Modules:
  0.0 38.2 jit_solution(3183008186274825833)
XLA Ops:
  0.6 1.6 %edge.1 = (f32[4,128,128]{2,1,0:T(8,128)S(1)}, f32[4,128,128]{2,1,0:T(8,128)S(1)}, f32[4,128,128]{2,1,0:T(8,128)S(1)}, f32[4,128,128]{2,1,0:T(8,128)S(1)}) custom-call(f32[4,128,128]{2,1,0:T(8,128)} %bitcast.2, f32[4,128,128]{2,1,0:T(8,128)} %refs_1_.1, f32[4,128,128]{2,1,0:T(8,128)} %refs_2_.1), custom_call_target="tpu_custom_call" | custom-call | tf_op jit(solution)/shard_map/edge/pallas_call | solution.py:364
  2.3 0.7 %collective-permute-start.1 = (f32[4,128,128]{2,1,0:T(8,128)S(1)}, f32[4,128,128]{2,1,0:T(8,128)S(1)}, u32[]{:S(2)}, u32[]{:S(2)}) collective-permute-start(f32[4,128,128]{2,1,0:T(8,128)S(1)} %get-tuple-element.28), channel_id=1, source_target_pairs={{1,2},{2,1},{3,4},{4,3},{5,6},{6,5},{7,8},{8,7},{9,10},{10,9},{11,... | collective-permute-start | bytes 786440 | tf_op jit(solution)/shard_map/ppermute | solution.py:338
  3.0 1.2 %inner.1 = (f32[4,128,128]{2,1,0:T(8,128)S(1)}, bf16[4,128,384]{2,1,0:T(8,128)(2,1)S(1)}, bf16[4,128,384]{2,1,0:T(8,128)(2,1)S(1)}, bf16[4,128,384]{2,1,0:T(8,12...) custom-call(f32[4,128,128]{2,1,0:T(8,128)S(1)} %get-tuple-element.18.refs_0_, ...), custom_call_target="tpu_custom_call" | custom-call | tf_op jit(solution)/shard_map/inner/pallas_call | solution.py:372
  4.1 4.4 %collective-permute-start = (f32[4,128,128]{2,1,0:T(8,128)S(1)}, f32[4,128,128]{2,1,0:T(8,128)S(1)}, u32[]{:S(2)}, u32[]{:S(2)}) collective-permute-start(f32[4,128,128]{2,1,0:T(8,128)S(1)} %get-tuple-element.27), channel_id=1, source_target_pairs={{0,1},{1,0},{2,3},{3,2},{4,5},{5,4},{6,7},{7,6},{8,9},{9,8},{10,11... | collective-permute-start | bytes 786440 | tf_op jit(solution)/shard_map/ppermute | solution.py:338
  8.6 0.0 collective-permute-done.1.refs_8_
  8.6 1.2 %collective-permute-done.refs_7_ = f32[4,128,128]{2,1,0:T(8,128)S(1)} collective-permute-done((f32[4,128,128]{2,1,0:T(8,128)S(1)}, f32[4,128,128]{2,1,0:T(8,128)S(1)}, u32[]{:S(2)}, u32[]{:S(2)}) %collective-permute-start) | collective-permute-done | bytes 262176 | tf_op jit(solution)/shard_map/ppermute | solution.py:338
  9.7 1.5 %project.1 = (f32[4,128,128]{2,1,0:T(8,128)S(1)}, f32[72,128]{1,0:T(8,128)S(1)}, f32[72,128]{1,0:T(8,128)S(1)}) custom-call(f32[4,128,128]{2,1,0:T(8,128)S(1)} %get-tuple-element.18.refs_0_, bf16[4,128,384]{2,1,0:T(8,128)(2,1)S(1)} %get-tuple-element.21.refs_1_, bf16[4,128,384]{2,1,0:T(8,128)(2,1)S(1)} %get-tuple-element.22.refs_2_, ...), custom_call_target="tpu_custom_call" | custom-call | tf_op jit(solution)/shard_map/project/pallas_call | solution.py:380
  11.2 3.7 %collective-permute-start.2 = (f32[72,128]{1,0:T(8,128)S(1)}, f32[72,128]{1,0:T(8,128)S(1)}, u32[]{:S(2)}, u32[]{:S(2)}) collective-permute-start(f32[72,128]{1,0:T(8,128)S(1)} %get-tuple-element.30), channel_id=1, source_target_pairs={{0,1},{1,0},{2,3},{3,2},{4,5},{5,4},{6,7},{7,6},{8,9},{9,8},{10,11... | collective-permute-start | bytes 110600 | tf_op jit(solution)/shard_map/ppermute | solution.py:338
  15.0 0.9 %collective-permute-done.2 = f32[72,128]{1,0:T(8,128)S(1)} collective-permute-done((f32[72,128]{1,0:T(8,128)S(1)}, f32[72,128]{1,0:T(8,128)S(1)}, u32[]{:S(2)}, u32[]{:S(2)}) %collective-permute-start.2) | collective-permute-done | bytes 36896 | tf_op jit(solution)/shard_map/ppermute | solution.py:338
  15.8 3.6 %collective-permute-start.5 = (f32[72,128]{1,0:T(8,128)S(1)}, f32[72,128]{1,0:T(8,128)S(1)}, u32[]{:S(2)}, u32[]{:S(2)}) collective-permute-start(f32[72,128]{1,0:T(8,128)S(1)} %add.21), channel_id=1, source_target_pairs={{0,6},{1,7},{2,4},{3,5},{4,2},{5,3},{6,0},{7,1},{8,14},{9,15},{10,... | collective-permute-start | bytes 110600 | tf_op jit(solution)/shard_map/ppermute | solution.py:314
  19.4 0.8 %collective-permute-start.4 = (f32[72,128]{1,0:T(8,128)S(1)}, f32[72,128]{1,0:T(8,128)S(1)}, u32[]{:S(2)}, u32[]{:S(2)}) collective-permute-start(f32[72,128]{1,0:T(8,128)S(1)} %add.21), channel_id=1, source_target_pairs={{0,4},{1,5},{2,6},{3,7},{4,0},{5,1},{6,2},{7,3},{8,12},{9,13},{10,... | collective-permute-start | bytes 110600 | tf_op jit(solution)/shard_map/ppermute | solution.py:314
  20.3 0.0 collective-permute-start.3
  20.3 1.1 %collective-permute-done.5 = f32[72,128]{1,0:T(8,128)S(1)} collective-permute-done((f32[72,128]{1,0:T(8,128)S(1)}, f32[72,128]{1,0:T(8,128)S(1)}, u32[]{:S(2)}, u32[]{:S(2)}) %collective-permute-start.5) | collective-permute-done | bytes 36896 | tf_op jit(solution)/shard_map/ppermute | solution.py:314
  21.3 2.0 %collective-permute-done.4 = f32[72,128]{1,0:T(8,128)S(1)} collective-permute-done((f32[72,128]{1,0:T(8,128)S(1)}, f32[72,128]{1,0:T(8,128)S(1)}, u32[]{:S(2)}, u32[]{:S(2)}) %collective-permute-start.4) | collective-permute-done | bytes 36896 | tf_op jit(solution)/shard_map/ppermute | solution.py:314
  23.4 0.8 %collective-permute-done.3 = f32[72,128]{1,0:T(8,128)S(1)} collective-permute-done((f32[72,128]{1,0:T(8,128)S(1)}, f32[72,128]{1,0:T(8,128)S(1)}, u32[]{:S(2)}, u32[]{:S(2)}) %collective-permute-start.3) | collective-permute-done | bytes 36896 | tf_op jit(solution)/shard_map/ppermute | solution.py:314
  24.2 3.7 %collective-permute-start.8 = (f32[72,128]{1,0:T(8,128)S(1)}, f32[72,128]{1,0:T(8,128)S(1)}, u32[]{:S(2)}, u32[]{:S(2)}) collective-permute-start(f32[72,128]{1,0:T(8,128)S(1)} %add_add_fusion.1), channel_id=1, source_target_pairs={{0,24},{1,25},{2,26},{3,27},{4,28},{5,29},{6,30},{7,31},{8,16},{9,... | collective-permute-start | bytes 110600 | tf_op jit(solution)/shard_map/ppermute | solution.py:314
  27.9 0.0 collective-permute-start.7
  27.9 0.8 %collective-permute-start.6 = (f32[72,128]{1,0:T(8,128)S(1)}, f32[72,128]{1,0:T(8,128)S(1)}, u32[]{:S(2)}, u32[]{:S(2)}) collective-permute-start(f32[72,128]{1,0:T(8,128)S(1)} %add_add_fusion.1), channel_id=1, source_target_pairs={{0,8},{1,9},{2,10},{3,11},{4,12},{5,13},{6,14},{7,15},{8,0},{9,1},... | collective-permute-start | bytes 110600 | tf_op jit(solution)/shard_map/ppermute | solution.py:314
  28.7 1.4 %collective-permute-done.8 = f32[72,128]{1,0:T(8,128)S(1)} collective-permute-done((f32[72,128]{1,0:T(8,128)S(1)}, f32[72,128]{1,0:T(8,128)S(1)}, u32[]{:S(2)}, u32[]{:S(2)}) %collective-permute-start.8) | collective-permute-done | bytes 36896 | tf_op jit(solution)/shard_map/ppermute | solution.py:314
  30.0 2.7 %collective-permute-done.7 = f32[72,128]{1,0:T(8,128)S(1)} collective-permute-done((f32[72,128]{1,0:T(8,128)S(1)}, f32[72,128]{1,0:T(8,128)S(1)}, u32[]{:S(2)}, u32[]{:S(2)}) %collective-permute-start.7) | collective-permute-done | bytes 36896 | tf_op jit(solution)/shard_map/ppermute | solution.py:314
  32.7 0.0 collective-permute-done.6
  32.8 0.1 collective-permute-start.9
  32.8 1.2 %collective-permute-done.9.refs_1_ = f32[72,128]{1,0:T(8,128)S(1)} collective-permute-done((f32[72,128]{1,0:T(8,128)S(1)}, f32[72,128]{1,0:T(8,128)S(1)}, u32[]{:S(2)}, u32[]{:S(2)}) %collective-permute-start.9) | collective-permute-done | bytes 36896 | tf_op jit(solution)/shard_map/ppermute | solution.py:338
  34.0 4.2 %finish.1 = (f32[4,128,128]{2,1,0:T(8,128)}, f32[128,128]{1,0:T(8,128)}) custom-call(f32[72,128]{1,0:T(8,128)S(1)} %add_add_fusion.refs_0_, f32[72,128]{1,0:T(8,128)S(1)} %collective-permute-done.9.refs_1_, f32[4,128,128]{2,1,0:T(8,128)S(1)} %get-tuple-element.31.refs_2_), custom_call_target="tpu_custom_call" | custom-call | tf_op jit(solution)/shard_map/finish/pallas_call | solution.py:388
  (3 shorter events, 0.0 us)
Async XLA Ops:
  2.3 6.3 %collective-permute-start.1 = (f32[4,128,128]{2,1,0:T(8,128)S(1)}, f32[4,128,128]{2,1,0:T(8,128)S(1)}, u32[]{:S(2)}, u32[]{:S(2)}) collective-permute-start(f32[4,128,128]{2,1,0:T(8,128)S(1)} %get-tuple-element.28), channel_id=1, source_target_pairs={{1,2},{2,1},{3,4},{4,3},{5,6},{6,5},{7,8},{8,7},{9,10},{10,9},{11,... | collective-permute-start | bytes 786440 | tf_op jit(solution)/shard_map/ppermute | solution.py:338
  4.1 5.6 %collective-permute-start = (f32[4,128,128]{2,1,0:T(8,128)S(1)}, f32[4,128,128]{2,1,0:T(8,128)S(1)}, u32[]{:S(2)}, u32[]{:S(2)}) collective-permute-start(f32[4,128,128]{2,1,0:T(8,128)S(1)} %get-tuple-element.27), channel_id=1, source_target_pairs={{0,1},{1,0},{2,3},{3,2},{4,5},{5,4},{6,7},{7,6},{8,9},{9,8},{10,11... | collective-permute-start | bytes 786440 | tf_op jit(solution)/shard_map/ppermute | solution.py:338
  11.2 4.6 %collective-permute-start.2 = (f32[72,128]{1,0:T(8,128)S(1)}, f32[72,128]{1,0:T(8,128)S(1)}, u32[]{:S(2)}, u32[]{:S(2)}) collective-permute-start(f32[72,128]{1,0:T(8,128)S(1)} %get-tuple-element.30), channel_id=1, source_target_pairs={{0,1},{1,0},{2,3},{3,2},{4,5},{5,4},{6,7},{7,6},{8,9},{9,8},{10,11... | collective-permute-start | bytes 110600 | tf_op jit(solution)/shard_map/ppermute | solution.py:338
  15.8 5.5 %collective-permute-start.5 = (f32[72,128]{1,0:T(8,128)S(1)}, f32[72,128]{1,0:T(8,128)S(1)}, u32[]{:S(2)}, u32[]{:S(2)}) collective-permute-start(f32[72,128]{1,0:T(8,128)S(1)} %add.21), channel_id=1, source_target_pairs={{0,6},{1,7},{2,4},{3,5},{4,2},{5,3},{6,0},{7,1},{8,14},{9,15},{10,... | collective-permute-start | bytes 110600 | tf_op jit(solution)/shard_map/ppermute | solution.py:314
  19.4 4.0 %collective-permute-start.4 = (f32[72,128]{1,0:T(8,128)S(1)}, f32[72,128]{1,0:T(8,128)S(1)}, u32[]{:S(2)}, u32[]{:S(2)}) collective-permute-start(f32[72,128]{1,0:T(8,128)S(1)} %add.21), channel_id=1, source_target_pairs={{0,4},{1,5},{2,6},{3,7},{4,0},{5,1},{6,2},{7,3},{8,12},{9,13},{10,... | collective-permute-start | bytes 110600 | tf_op jit(solution)/shard_map/ppermute | solution.py:314
  20.3 4.0 %collective-permute-start.3 = (f32[72,128]{1,0:T(8,128)S(1)}, f32[72,128]{1,0:T(8,128)S(1)}, u32[]{:S(2)}, u32[]{:S(2)}) collective-permute-start(f32[72,128]{1,0:T(8,128)S(1)} %add.21), channel_id=1, source_target_pairs={{0,2},{1,3},{2,0},{3,1},{4,6},{5,7},{6,4},{7,5},{8,10},{9,11},{10,... | collective-permute-start | bytes 110600 | tf_op jit(solution)/shard_map/ppermute | solution.py:314
  24.2 5.8 %collective-permute-start.8 = (f32[72,128]{1,0:T(8,128)S(1)}, f32[72,128]{1,0:T(8,128)S(1)}, u32[]{:S(2)}, u32[]{:S(2)}) collective-permute-start(f32[72,128]{1,0:T(8,128)S(1)} %add_add_fusion.1), channel_id=1, source_target_pairs={{0,24},{1,25},{2,26},{3,27},{4,28},{5,29},{6,30},{7,31},{8,16},{9,... | collective-permute-start | bytes 110600 | tf_op jit(solution)/shard_map/ppermute | solution.py:314
  27.9 4.9 %collective-permute-start.7 = (f32[72,128]{1,0:T(8,128)S(1)}, f32[72,128]{1,0:T(8,128)S(1)}, u32[]{:S(2)}, u32[]{:S(2)}) collective-permute-start(f32[72,128]{1,0:T(8,128)S(1)} %add_add_fusion.1), channel_id=1, source_target_pairs={{0,16},{1,17},{2,18},{3,19},{4,20},{5,21},{6,22},{7,23},{8,24},{9,... | collective-permute-start | bytes 110600 | tf_op jit(solution)/shard_map/ppermute | solution.py:314
  27.9 4.9 %collective-permute-start.6 = (f32[72,128]{1,0:T(8,128)S(1)}, f32[72,128]{1,0:T(8,128)S(1)}, u32[]{:S(2)}, u32[]{:S(2)}) collective-permute-start(f32[72,128]{1,0:T(8,128)S(1)} %add_add_fusion.1), channel_id=1, source_target_pairs={{0,8},{1,9},{2,10},{3,11},{4,12},{5,13},{6,14},{7,15},{8,0},{9,1},... | collective-permute-start | bytes 110600 | tf_op jit(solution)/shard_map/ppermute | solution.py:314
  32.8 1.3 %collective-permute-start.9 = (f32[72,128]{1,0:T(8,128)S(1)}, f32[72,128]{1,0:T(8,128)S(1)}, u32[]{:S(2)}, u32[]{:S(2)}) collective-permute-start(f32[72,128]{1,0:T(8,128)S(1)} %add_add_fusion.refs_0_), channel_id=1, source_target_pairs={{0,1},{1,0},{2,3},{3,2},{4,5},{5,4},{6,7},{7,6},{8,9},{9,8},{10,11... | collective-permute-start | bytes 110600 | tf_op jit(solution)/shard_map/ppermute | solution.py:338

commit v4 on v3

--- a/solution.py
+++ b/solution.py
@@ -62,31 +62,57 @@
     return 0.5 * (d + d.T) - jnp.where(rows == cols, center, 0.0)
 
 
-def leftward(s0, s1, s2, sym0, sym1, c0, c1, out_ref):
+def pack(sym):
+    block = sym.shape[0]
+    mid = block // 2
+    rows, cols = iotas((mid, block))
+    top, low = sym[:mid], sym[mid:]
+    body = jnp.where((cols >= mid) | (rows >= cols), top, pltpu.roll(low, mid, 1))
+    diagonal = jnp.sum(jnp.where(cols == rows + mid, low, 0.0), axis=0, keepdims=True)
+    return jnp.concatenate([body, jnp.broadcast_to(diagonal, (8, block))], 0)
+
+
+def unpack(packed):
+    block = packed.shape[1]
+    mid = block // 2
+    rows, cols = iotas((mid, block))
+    body, diagonal = packed[:mid], packed[mid : mid + 1]
+    top = jnp.where((cols >= mid) | (rows > cols), body, 0.0)
+    low = pltpu.roll(jnp.where((cols < mid) & (rows < cols), body, 0.0), mid, 1)
+    part = jnp.concatenate([top, low], 0)
+    middle = jnp.concatenate([jnp.where(rows == cols, body, 0.0), jnp.where(cols == rows + mid, diagonal, 0.0)], 0)
+    return part + part.T + middle
+
+
+def leftward(s0, s1, s2, sym0, sym1, c0, c1, out_ref, more_ref):
+    block = s0.shape[0]
     l0, r0, r1 = left3(sym0), right3(s0), right3(s1)
     c0l = left3(c0)
     part = (dot(l0, r0) + dot(c0l, r1)) / half_width
     first1 = (dot(left3(sym1), r1) + dot(left3(c1), right3(s2)) + dot(left3(c0.T), r0)) / half_width
-    out_ref[0] = s0
-    out_ref[1] = part
-    out_ref[2] = scale * (dot(l0, right3(part)) + dot(c0l, right3(first1))) - s0
-    out_ref[3] = sym0
-
-
-def rightward(s_prev, s_last, sym_last, c_prev, c_last, out_ref):
+    out_ref[0:block] = s0
+    out_ref[block : 2 * block] = part
+    out_ref[2 * block : 2 * block + block // 2 + 8] = pack(sym0)
+    more_ref[...] = scale * (dot(l0, right3(part)) + dot(c0l, right3(first1))) - s0
+
+
+def rightward(s_prev, s_last, sym_last, c_prev, c_last, out_ref, more_ref):
+    block = s_last.shape[0]
     rl = right3(s_last)
     part = (dot(left3(sym_last), rl) + dot(left3(c_prev.T), right3(s_prev))) / half_width
     turned = left3(c_last.T)
-    out_ref[0] = dot(turned, rl)
-    out_ref[1] = dot(turned, right3(part))
-    out_ref[2] = c_last
-    out_ref[3] = jnp.zeros_like(c_last)
+    out_ref[0:block] = dot(turned, rl)
+    out_ref[block : 2 * block] = dot(turned, right3(part))
+    out_ref[2 * block : 2 * block + block // 2 + 8] = pack(dot(turned, right3(c_last)))
+    more_ref[...] = jnp.zeros_like(c_last)
 
 
 def edge(axis, s_hbm, d_hbm, c_hbm, odd_ref, s_ref, d_ref, c_ref, sems):
     nblocks = d_hbm.shape[0]
     last = nblocks - 1
     parity = lax.rem(lax.axis_index(axis), 2)
+    block = s_hbm.shape[1]
+    swap_ref, more_ref = odd_ref.at[: odd_ref.shape[0] - block], odd_ref.at[odd_ref.shape[0] - block :]
     is_last = lax.axis_index(axis) == lax.axis_size(axis) - 1
     copies = []
     for k, (source, target) in enumerate(((s_hbm, s_ref), (d_hbm, d_ref), (c_hbm, c_ref))):
@@ -102,25 +128,27 @@
 
     @pl.when(parity == 0)
     def _():
-        leftward(s_ref[0], s_ref[1], s_ref[2], symmetric(d_ref[0]), symmetric(d_ref[1]), c_ref[0], c_ref[1], odd_ref)
+        leftward(s_ref[0], s_ref[1], s_ref[2], symmetric(d_ref[0]), symmetric(d_ref[1]), c_ref[0], c_ref[1], swap_ref, more_ref)
 
     @pl.when(parity != 0)
     def _():
-        rightward(s_ref[last - 1], s_ref[last], symmetric(d_ref[last]), c_ref[last - 1], c_ref[last], odd_ref)
+        rightward(s_ref[last - 1], s_ref[last], symmetric(d_ref[last]), c_ref[last - 1], c_ref[last], swap_ref, more_ref)
 
 
 def inner(axis, s_ref, d_ref, c_ref, even_ref, sym_ref, cl_ref, ct_ref, first_ref, pre_ref, pass_ref):
     nblocks = d_ref.shape[0]
     last = nblocks - 1
+    block = s_ref.shape[1]
     parity = lax.rem(lax.axis_index(axis), 2)
+    swap_ref, more_ref = even_ref.at[: even_ref.shape[0] - block], even_ref.at[even_ref.shape[0] - block :]
 
     @pl.when(parity != 0)
     def _():
-        leftward(s_ref[0], s_ref[1], s_ref[2], symmetric(d_ref[0]), symmetric(d_ref[1]), c_ref[0], c_ref[1], even_ref)
+        leftward(s_ref[0], s_ref[1], s_ref[2], symmetric(d_ref[0]), symmetric(d_ref[1]), c_ref[0], c_ref[1], swap_ref, more_ref)
 
     @pl.when(parity == 0)
     def _():
-        rightward(s_ref[last - 1], s_ref[last], symmetric(d_ref[last]), c_ref[last - 1], c_ref[last], even_ref)
+        rightward(s_ref[last - 1], s_ref[last], symmetric(d_ref[last]), c_ref[last - 1], c_ref[last], swap_ref, more_ref)
 
     s = [s_ref[b] for b in range(nblocks)]
     sr = [right3(x) for x in s]
@@ -155,24 +183,26 @@
 
 
 def project(axis, s_ref, sym_ref, cl_ref, ct_ref, first_ref, pre_ref, pass_ref, even_ref, odd_ref, filt_ref, keep_ref, send_ref):
-    nblocks, block, unused = s_ref.shape
+    nblocks, block, _ = s_ref.shape
     last = nblocks - 1
     parity = lax.rem(lax.axis_index(axis), 2)
-    right = [jnp.where(parity == 0, even_ref[k], odd_ref[k]) for k in range(4)]
-    left = [jnp.where(parity == 0, odd_ref[k], even_ref[k]) for k in range(3)]
+    rows = odd_ref.shape[0] - block
+    cuts = ((0, block), (block, 2 * block), (2 * block, rows))
+    right = [jnp.where(parity == 0, even_ref[a:b], odd_ref[a:b]) for a, b in cuts]
+    left = [jnp.where(parity == 0, odd_ref[a:b], even_ref[a:b]) for a, b in cuts]
+    other = jnp.where(parity == 0, even_ref[rows:], odd_ref[rows:])
     onward = pass_ref[...]
     tail = first_ref[last] + dot(cl_ref[last], right3(right[0])) / half_width
     head = first_ref[0] + left[0] / half_width
     ahead = right[1] + onward / half_width
-    back = dot(left3(left[2]), right3(s_ref[0]))
-    behind = left[1] + dot(left3(left[2].T), right3(back)) / half_width
+    behind = left[1] + dot(left3(unpack(left[2])), right3(s_ref[0])) / half_width
     tail_r, head_r = right3(tail), right3(head)
     filtered = [pre_ref[b] for b in range(nblocks)]
     filtered[0] += scale * (dot(sym_ref[0], head_r) + behind)
     filtered[1] += scale * dot(ct_ref[0], head_r)
     filtered[last - 1] += scale * dot(cl_ref[last - 1], tail_r)
     filtered[last] += scale * (dot(sym_ref[last], tail_r) + dot(cl_ref[last], right3(ahead)))
-    beyond = right[2] + scale * (dot(left3(right[3]), right3(onward)) / half_width + dot(ct_ref[last], tail_r))
+    beyond = other + scale * (dot(left3(unpack(right[2])), right3(onward)) / half_width + dot(ct_ref[last], tail_r))
     filtered.append(beyond)
     fr = [right3(x) for x in filtered]
     both = []
@@ -207,65 +237,79 @@
         put(send_ref, keep_ref)
 
 
-def factor(full, inv_ref):
+def factor(full, inv_ref, group=8):
     width = full.shape[1]
     tiles = width // 8
     sub, lane = iotas((8, width))
+    nought = jnp.where(lane < 0, 1.0, 0.0)
+
+    def along(x, column):
+        return jnp.broadcast_to(x[:, column : column + 1], (8, width))
+
+    def down(x, row):
+        return jnp.broadcast_to(x[row : row + 1, :], (8, width))
+
     work = [full[8 * t : 8 * t + 8, :] for t in range(tiles)]
-    nought = jnp.where(lane < 0, 1.0, 0.0)
+    col, done = [], []
     for p in range(tiles):
         at = 8 * p
+        start = p - p % group
+        end = min(tiles, start + group)
         inside = (lane >= at) & (lane < at + 8)
-        column = [jnp.broadcast_to(work[p][:, at + j : at + j + 1], (8, width)) + nought for j in range(8)]
-        a = {}
+        if p == start:
+            done = []
+            col = [along(work[p], at + j) + nought for j in range(8)]
+        raw = {(t, j): along(work[t], at + j) for j in range(8) for t in range(p + 1, end)}
+        diagonal, recip, m = [], [], {}
         for j in range(8):
-            for i in range(j, 8):
-                a[i, j] = jnp.broadcast_to(column[j][i : i + 1, :], (8, width))
-        m, recip = {}, []
-        for j in range(8):
-            recip.append(1.0 / a[j, j])
-            for i in range(j + 1, 8):
-                m[i, j] = a[i, j] * recip[j]
-            for i in range(j + 1, 8):
-                for k in range(j + 1, i + 1):
-                    a[i, k] = a[i, k] - m[i, j] * a[k, j]
+            diagonal.append(down(col[j], j))
+            recip.append(1.0 / diagonal[j])
+            for k in range(j + 1, 8):
+                m[k, j] = down(col[j], k) * recip[j]
+                col[k] = col[k] - col[j] * m[k, j]
+        coming = []
+        if p + 1 < end:
+            w = [raw[p + 1, j] + nought for j in range(8)]
+            coming = [along(work[p + 1], at + 8 + k) + nought for k in range(8)]
+            for j in range(8):
+                for k in range(j + 1, 8):
+                    w[k] = w[k] - w[j] * m[k, j]
+                for k in range(8):
+                    coming[k] = coming[k] - w[j] * (down(w[j], k) * recip[j])
         cleared = jnp.where(inside, jnp.where(lane == sub + at, 1.0, 0.0), work[p])
         pivot = []
         for j in range(8):
-            r = jnp.broadcast_to(cleared[j : j + 1, :], (8, width))
+            r = down(cleared, j)
             for k in range(j):
                 r = r - m[j, k] * pivot[k]
             pivot.append(r)
         out = jnp.zeros((8, width), jnp.float32)
         for j in range(8):
-            out = jnp.where(sub == j, pivot[j] * lax.rsqrt(a[j, j]), out)
+            out = jnp.where(sub == j, pivot[j] * lax.rsqrt(diagonal[j]), out)
         inv_ref[at : at + 8, :] = jnp.where(lane <= sub + at, out, 0.0)
-        scaled = [pivot[j] * recip[j] for j in range(8)]
+        done.append(jnp.where((lane > sub + at) & (lane < 8 * end), 0.0, out))
         solved = [None] * 8
         for k in reversed(range(8)):
-            q = scaled[k]
-            for j in range(k + 1, 8):
+            q = pivot[k] * recip[k]
+            for j in reversed(range(k + 1, 8)):
                 q = q - m[j, k] * solved[j]
             solved[k] = q
-        for t in range(p + 1, tiles):
-            raw = [jnp.broadcast_to(work[t][:, at + j : at + j + 1], (8, width)) for j in range(8)]
+        for t in range(p + 1, end):
             acc = jnp.where(inside, 0.0, work[t])
-            if t == p + 1:
-                w = []
-                for j in range(8):
-                    x = raw[j]
-                    for k in range(j):
-                        x = x - w[k] * m[j, k]
-                    w.append(x)
-                    acc = acc - x * scaled[j]
-            else:
-                for j in range(8):
-                    acc = acc - raw[j] * solved[j]
+            for j in reversed(range(8)):
+                acc = acc - raw[t, j] * solved[j]
             work[t] = acc
+        col = coming
+        if p + 1 == end < tiles:
+            rows = jnp.concatenate(done, 0)
+            update = dot(left6(rows, 0), right6(rows, 0), (0, 0))
+            for t in range(end, tiles):
+                kept = jnp.where((lane >= 8 * start) & (lane < 8 * end), 0.0, work[t])
+                work[t] = kept - update[8 * t : 8 * t + 8]
 
 
 def finish(axis, total_nodes, mine_ref, other_ref, filt_ref, orth_hbm, proj_hbm, inv_ref, orth_ref, proj_ref, sems):
-    nblocks, block, width = filt_ref.shape
+    nblocks, _, width = filt_ref.shape
     mid = width // 2
     swapped = lax.rem(lax.axis_index(axis), 2) != 0
     mine, other = mine_ref[...], other_ref[...]
@@ -341,16 +385,16 @@
 def body(states, diag_blocks, couplings):
     axis = "dom"
     nodes_dev, width = states.shape
-    nblocks, block, unused = diag_blocks.shape
+    nblocks, block, _ = diag_blocks.shape
     devices = lax.axis_size(axis)
     field = states.reshape(nblocks, block, width)
     params = pltpu.CompilerParams(vmem_limit_bytes=40 << 20)
-    cross = shape(4, block, width)
+    cross = shape(3 * block + block // 2 + 8, width)
     tall = shape(nblocks, block, width)
     square = shape(nblocks, block, block)
     wide = shape(nblocks, block, 3 * block, kind=jnp.bfloat16)
 
-    def call(kernel, name, ins, outs, scratch=()):
+    def call(kernel, ins, outs, scratch=()):
         return pl.pallas_call(
             kernel,
             out_shape=tuple(s for s, spec in outs),
@@ -358,12 +402,10 @@
             out_specs=tuple(spec for s, spec in outs),
             scratch_shapes=scratch,
             compiler_params=params,
-            name=name,
         )
 
     odd, s, d, c = call(
         lambda *refs: edge(axis, *refs),
-        "edge",
         [far] * 3,
         [(cross, here), (tall, here), (square, here), (square, here)],
         [pltpu.SemaphoreType.DMA((3,))],
@@ -371,23 +413,18 @@
     odd = swap(odd, axis, 1)
     even, sym, cl, ct, first, pre, onward = call(
         lambda *refs: inner(axis, *refs),
-        "inner",
         [here] * 3,
         [(cross, here), (wide, here), (wide, here), (wide, here), (tall, here), (tall, here), (shape(block, width), here)],
     )(s, d, c)
     even = swap(even, axis, 0)
     piece = shape(width // 2 + 8, width)
     filtered, keep, send = call(
-        lambda *refs: project(axis, *refs),
-        "project",
-        [here] * 9,
-        [(tall, here), (piece, here), (piece, here)],
+        lambda *refs: project(axis, *refs), [here] * 9, [(tall, here), (piece, here), (piece, here)]
     )(s, sym, cl, ct, first, pre, onward, even, odd)
     mine = add_up(keep + swap(send, axis, 0), axis, 2)
     other = swap(mine, axis, 0)
     orthonormal, projected = call(
         lambda *refs: finish(axis, nodes_dev * devices, *refs),
-        "finish",
         [here] * 3,
         [(tall, far), (shape(width, width), far)],
         [
@@ -403,4 +440,5 @@
 def solution(mesh):
     in_specs = (P("dom", None), P("dom", None, None), P("dom", None, None))
     out_specs = (P("dom", None), P())
+
     return jax.shard_map(body, mesh=mesh, in_specs=in_specs, out_specs=out_specs, check_vma=False)

time: 38.4 us -> 37.4 us (0.974)
  starting transfers between devices: 17.8 us -> 17.3 us
  Pallas kernels: 8.51 us -> 8.02 us
    ppermute x4, starting transfers between devices: 8.89 us -> 8.21 us  [swap(): return lax.ppermute(values, axis, route)]
    pallas_call x4, Pallas kernels: 8.51 us -> 8.02 us  [the longest x1 3.71 us: body(): call(lambda *refs: finish(axis, nodes_dev * devices, *refs), [here] * 3,...]
where the time goes in v4:
time: 37.4 us; the launch traced here: 37.2 us
  starting transfers between devices  17.3 us (46%)
  waiting for transfers between devices  11.2 us (30%)
  Pallas kernels  8.02 us (21%)
  between operations  0.68 us (2%)
    ppermute x6, starting transfers between devices, add_up(): parts.append(lax.ppermute(values, axis, route(lambda k: k ^ flip)))  9.06 us
    ppermute x4, starting transfers between devices, swap(): return lax.ppermute(values, axis, route)  8.21 us
    ppermute x6, waiting for transfers between devices, add_up(): parts.append(lax.ppermute(values, axis, route(lambda k: k ^ flip)))  8.03 us
    pallas_call x1, Pallas kernels, body(): call(lambda *refs: finish(axis, nodes_dev * devices, *refs), [here] * 3,...  3.71 us
    ppermute x4, waiting for transfers between devices, swap(): return lax.ppermute(values, axis, route)  3.19 us
    pallas_call x1, Pallas kernels, body(): call(lambda *refs: edge(axis, *refs), [far] * 3, [(cross, here), (tall, h...  1.64 us
    pallas_call x1, Pallas kernels, body(): call(lambda *refs: project(axis, *refs), [here] * 9, [(tall, here), (piec...  1.4 us
    pallas_call x1, Pallas kernels, body(): call(lambda *refs: inner(axis, *refs), [here] * 3, [(cross, here), (wide,...  1.28 us
  transfers between devices with their start and end apart: 10, of which 8 were waited for; matrix products, arithmetic and copies ran while one was open for 0% of the time, Pallas kernels for 3%

profile of v4, /device:TPU:0, one launch (start us, length us, event | category | flops | bytes accessed | tf_op | source)
XLA Modules:
  0.0 37.2 jit_solution(15520614430477531216)
XLA Ops:
  0.6 1.6 %shard_map.50 = (f32[456,128]{1,0:T(8,128)S(1)}, f32[4,128,128]{2,1,0:T(8,128)S(1)}, f32[4,128,128]{2,1,0:T(8,128)S(1)}, f32[4,128,128]{2,1,0:T(8,128)S(1)}) custom-call(f32[4,128,128]{2,1,0:T(8,128)} %bitcast.2, f32[4,128,128]{2,1,0:T(8,128)} %refs_1_.1, f32[4,128,128]{2,1,0:T(8,128)} %refs_2_.1), custom_call_target="tpu_custom_call" | custom-call | tf_op jit(solution)/shard_map/pallas_call | solution.py:407
  2.3 0.7 %collective-permute-start.1 = (f32[456,128]{1,0:T(8,128)S(1)}, f32[456,128]{1,0:T(8,128)S(1)}, u32[]{:S(2)}, u32[]{:S(2)}) collective-permute-start(f32[456,128]{1,0:T(8,128)S(1)} %get-tuple-element.28), channel_id=1, source_target_pairs={{1,2},{2,1},{3,4},{4,3},{5,6},{6,5},{7,8},{8,7},{9,10},{10,9},{11,... | collective-permute-start | bytes 700424 | tf_op jit(solution)/shard_map/ppermute | solution.py:382
  3.0 1.3 %shard_map.51 = (f32[456,128]{1,0:T(8,128)S(1)}, bf16[4,128,384]{2,1,0:T(8,128)(2,1)S(1)}, bf16[4,128,384]{2,1,0:T(8,128)(2,1)S(1)}, bf16[4,128,384]{2,1,0:T(8,1...) custom-call(f32[4,128,128]{2,1,0:T(8,128)S(1)} %get-tuple-element.18.refs_0_, ...), custom_call_target="tpu_custom_call" | custom-call | tf_op jit(solution)/shard_map/pallas_call | solution.py:414
  4.2 4.3 %collective-permute-start = (f32[456,128]{1,0:T(8,128)S(1)}, f32[456,128]{1,0:T(8,128)S(1)}, u32[]{:S(2)}, u32[]{:S(2)}) collective-permute-start(f32[456,128]{1,0:T(8,128)S(1)} %get-tuple-element.27), channel_id=1, source_target_pairs={{0,1},{1,0},{2,3},{3,2},{4,5},{5,4},{6,7},{7,6},{8,9},{9,8},{10,11... | collective-permute-start | bytes 700424 | tf_op jit(solution)/shard_map/ppermute | solution.py:382
  8.6 0.0 collective-permute-done.1.refs_8_
  8.6 1.1 %collective-permute-done.refs_7_ = f32[456,128]{1,0:T(8,128)S(1)} collective-permute-done((f32[456,128]{1,0:T(8,128)S(1)}, f32[456,128]{1,0:T(8,128)S(1)}, u32[]{:S(2)}, u32[]{:S(2)}) %collective-permute-start) | collective-permute-done | bytes 233504 | tf_op jit(solution)/shard_map/ppermute | solution.py:382
  9.7 1.4 %shard_map.52 = (f32[4,128,128]{2,1,0:T(8,128)S(1)}, f32[72,128]{1,0:T(8,128)S(1)}, f32[72,128]{1,0:T(8,128)S(1)}) custom-call(f32[4,128,128]{2,1,0:T(8,128)S(1)} %get-tuple-element.18.refs_0_, bf16[4,128,384]{2,1,0:T(8,128)(2,1)S(1)} %get-tuple-element.21.refs_1_, bf16[4,128,384]{2,1,0:T(8,128)(2,1)S(1)} %get-tuple-element.22.refs_2_, ...), custom_call_target="tpu_custom_call" | custom-call | tf_op jit(solution)/shard_map/pallas_call | solution.py:421
  11.1 3.2 %collective-permute-start.2 = (f32[72,128]{1,0:T(8,128)S(1)}, f32[72,128]{1,0:T(8,128)S(1)}, u32[]{:S(2)}, u32[]{:S(2)}) collective-permute-start(f32[72,128]{1,0:T(8,128)S(1)} %get-tuple-element.30), channel_id=1, source_target_pairs={{0,1},{1,0},{2,3},{3,2},{4,5},{5,4},{6,7},{7,6},{8,9},{9,8},{10,11... | collective-permute-start | bytes 110600 | tf_op jit(solution)/shard_map/ppermute | solution.py:382
  14.2 0.9 %collective-permute-done.2 = f32[72,128]{1,0:T(8,128)S(1)} collective-permute-done((f32[72,128]{1,0:T(8,128)S(1)}, f32[72,128]{1,0:T(8,128)S(1)}, u32[]{:S(2)}, u32[]{:S(2)}) %collective-permute-start.2) | collective-permute-done | bytes 36896 | tf_op jit(solution)/shard_map/ppermute | solution.py:382
  15.1 3.7 %collective-permute-start.5 = (f32[72,128]{1,0:T(8,128)S(1)}, f32[72,128]{1,0:T(8,128)S(1)}, u32[]{:S(2)}, u32[]{:S(2)}) collective-permute-start(f32[72,128]{1,0:T(8,128)S(1)} %add.21), channel_id=1, source_target_pairs={{0,6},{1,7},{2,4},{3,5},{4,2},{5,3},{6,0},{7,1},{8,14},{9,15},{10,... | collective-permute-start | bytes 110600 | tf_op jit(solution)/shard_map/ppermute | solution.py:358
  18.8 0.9 %collective-permute-start.4 = (f32[72,128]{1,0:T(8,128)S(1)}, f32[72,128]{1,0:T(8,128)S(1)}, u32[]{:S(2)}, u32[]{:S(2)}) collective-permute-start(f32[72,128]{1,0:T(8,128)S(1)} %add.21), channel_id=1, source_target_pairs={{0,4},{1,5},{2,6},{3,7},{4,0},{5,1},{6,2},{7,3},{8,12},{9,13},{10,... | collective-permute-start | bytes 110600 | tf_op jit(solution)/shard_map/ppermute | solution.py:358
  19.7 0.0 collective-permute-start.3
  19.7 1.0 %collective-permute-done.5 = f32[72,128]{1,0:T(8,128)S(1)} collective-permute-done((f32[72,128]{1,0:T(8,128)S(1)}, f32[72,128]{1,0:T(8,128)S(1)}, u32[]{:S(2)}, u32[]{:S(2)}) %collective-permute-start.5) | collective-permute-done | bytes 36896 | tf_op jit(solution)/shard_map/ppermute | solution.py:358
  20.7 2.0 %collective-permute-done.4 = f32[72,128]{1,0:T(8,128)S(1)} collective-permute-done((f32[72,128]{1,0:T(8,128)S(1)}, f32[72,128]{1,0:T(8,128)S(1)}, u32[]{:S(2)}, u32[]{:S(2)}) %collective-permute-start.4) | collective-permute-done | bytes 36896 | tf_op jit(solution)/shard_map/ppermute | solution.py:358
  22.7 0.9 %collective-permute-done.3 = f32[72,128]{1,0:T(8,128)S(1)} collective-permute-done((f32[72,128]{1,0:T(8,128)S(1)}, f32[72,128]{1,0:T(8,128)S(1)}, u32[]{:S(2)}, u32[]{:S(2)}) %collective-permute-start.3) | collective-permute-done | bytes 36896 | tf_op jit(solution)/shard_map/ppermute | solution.py:358
  23.7 3.7 %collective-permute-start.8 = (f32[72,128]{1,0:T(8,128)S(1)}, f32[72,128]{1,0:T(8,128)S(1)}, u32[]{:S(2)}, u32[]{:S(2)}) collective-permute-start(f32[72,128]{1,0:T(8,128)S(1)} %add_add_fusion.1), channel_id=1, source_target_pairs={{0,24},{1,25},{2,26},{3,27},{4,28},{5,29},{6,30},{7,31},{8,16},{9,... | collective-permute-start | bytes 110600 | tf_op jit(solution)/shard_map/ppermute | solution.py:358
  27.4 0.0 collective-permute-start.7
  27.4 0.8 %collective-permute-start.6 = (f32[72,128]{1,0:T(8,128)S(1)}, f32[72,128]{1,0:T(8,128)S(1)}, u32[]{:S(2)}, u32[]{:S(2)}) collective-permute-start(f32[72,128]{1,0:T(8,128)S(1)} %add_add_fusion.1), channel_id=1, source_target_pairs={{0,8},{1,9},{2,10},{3,11},{4,12},{5,13},{6,14},{7,15},{8,0},{9,1},... | collective-permute-start | bytes 110600 | tf_op jit(solution)/shard_map/ppermute | solution.py:358
  28.1 1.4 %collective-permute-done.8 = f32[72,128]{1,0:T(8,128)S(1)} collective-permute-done((f32[72,128]{1,0:T(8,128)S(1)}, f32[72,128]{1,0:T(8,128)S(1)}, u32[]{:S(2)}, u32[]{:S(2)}) %collective-permute-start.8) | collective-permute-done | bytes 36896 | tf_op jit(solution)/shard_map/ppermute | solution.py:358
  29.5 2.7 %collective-permute-done.7 = f32[72,128]{1,0:T(8,128)S(1)} collective-permute-done((f32[72,128]{1,0:T(8,128)S(1)}, f32[72,128]{1,0:T(8,128)S(1)}, u32[]{:S(2)}, u32[]{:S(2)}) %collective-permute-start.7) | collective-permute-done | bytes 36896 | tf_op jit(solution)/shard_map/ppermute | solution.py:358
  32.2 0.0 collective-permute-done.6
  32.2 0.1 collective-permute-start.9
  32.3 1.2 %collective-permute-done.9.refs_1_ = f32[72,128]{1,0:T(8,128)S(1)} collective-permute-done((f32[72,128]{1,0:T(8,128)S(1)}, f32[72,128]{1,0:T(8,128)S(1)}, u32[]{:S(2)}, u32[]{:S(2)}) %collective-permute-start.9) | collective-permute-done | bytes 36896 | tf_op jit(solution)/shard_map/ppermute | solution.py:382
  33.5 3.7 %shard_map.53 = (f32[4,128,128]{2,1,0:T(8,128)}, f32[128,128]{1,0:T(8,128)}) custom-call(f32[72,128]{1,0:T(8,128)S(1)} %add_add_fusion.refs_0_, f32[72,128]{1,0:T(8,128)S(1)} %collective-permute-done.9.refs_1_, f32[4,128,128]{2,1,0:T(8,128)S(1)} %get-tuple-element.31.refs_2_), custom_call_target="tpu_custom_call" | custom-call | tf_op jit(solution)/shard_map/pallas_call | solution.py:426
  (3 shorter events, 0.0 us)
Async XLA Ops:
  2.3 6.3 %collective-permute-start.1 = (f32[456,128]{1,0:T(8,128)S(1)}, f32[456,128]{1,0:T(8,128)S(1)}, u32[]{:S(2)}, u32[]{:S(2)}) collective-permute-start(f32[456,128]{1,0:T(8,128)S(1)} %get-tuple-element.28), channel_id=1, source_target_pairs={{1,2},{2,1},{3,4},{4,3},{5,6},{6,5},{7,8},{8,7},{9,10},{10,9},{11,... | collective-permute-start | bytes 700424 | tf_op jit(solution)/shard_map/ppermute | solution.py:382
  4.2 5.4 %collective-permute-start = (f32[456,128]{1,0:T(8,128)S(1)}, f32[456,128]{1,0:T(8,128)S(1)}, u32[]{:S(2)}, u32[]{:S(2)}) collective-permute-start(f32[456,128]{1,0:T(8,128)S(1)} %get-tuple-element.27), channel_id=1, source_target_pairs={{0,1},{1,0},{2,3},{3,2},{4,5},{5,4},{6,7},{7,6},{8,9},{9,8},{10,11... | collective-permute-start | bytes 700424 | tf_op jit(solution)/shard_map/ppermute | solution.py:382
  11.1 4.0 %collective-permute-start.2 = (f32[72,128]{1,0:T(8,128)S(1)}, f32[72,128]{1,0:T(8,128)S(1)}, u32[]{:S(2)}, u32[]{:S(2)}) collective-permute-start(f32[72,128]{1,0:T(8,128)S(1)} %get-tuple-element.30), channel_id=1, source_target_pairs={{0,1},{1,0},{2,3},{3,2},{4,5},{5,4},{6,7},{7,6},{8,9},{9,8},{10,11... | collective-permute-start | bytes 110600 | tf_op jit(solution)/shard_map/ppermute | solution.py:382
  15.1 5.6 %collective-permute-start.5 = (f32[72,128]{1,0:T(8,128)S(1)}, f32[72,128]{1,0:T(8,128)S(1)}, u32[]{:S(2)}, u32[]{:S(2)}) collective-permute-start(f32[72,128]{1,0:T(8,128)S(1)} %add.21), channel_id=1, source_target_pairs={{0,6},{1,7},{2,4},{3,5},{4,2},{5,3},{6,0},{7,1},{8,14},{9,15},{10,... | collective-permute-start | bytes 110600 | tf_op jit(solution)/shard_map/ppermute | solution.py:358
  18.8 4.0 %collective-permute-start.4 = (f32[72,128]{1,0:T(8,128)S(1)}, f32[72,128]{1,0:T(8,128)S(1)}, u32[]{:S(2)}, u32[]{:S(2)}) collective-permute-start(f32[72,128]{1,0:T(8,128)S(1)} %add.21), channel_id=1, source_target_pairs={{0,4},{1,5},{2,6},{3,7},{4,0},{5,1},{6,2},{7,3},{8,12},{9,13},{10,... | collective-permute-start | bytes 110600 | tf_op jit(solution)/shard_map/ppermute | solution.py:358
  19.7 4.0 %collective-permute-start.3 = (f32[72,128]{1,0:T(8,128)S(1)}, f32[72,128]{1,0:T(8,128)S(1)}, u32[]{:S(2)}, u32[]{:S(2)}) collective-permute-start(f32[72,128]{1,0:T(8,128)S(1)} %add.21), channel_id=1, source_target_pairs={{0,2},{1,3},{2,0},{3,1},{4,6},{5,7},{6,4},{7,5},{8,10},{9,11},{10,... | collective-permute-start | bytes 110600 | tf_op jit(solution)/shard_map/ppermute | solution.py:358
  23.7 5.8 %collective-permute-start.8 = (f32[72,128]{1,0:T(8,128)S(1)}, f32[72,128]{1,0:T(8,128)S(1)}, u32[]{:S(2)}, u32[]{:S(2)}) collective-permute-start(f32[72,128]{1,0:T(8,128)S(1)} %add_add_fusion.1), channel_id=1, source_target_pairs={{0,24},{1,25},{2,26},{3,27},{4,28},{5,29},{6,30},{7,31},{8,16},{9,... | collective-permute-start | bytes 110600 | tf_op jit(solution)/shard_map/ppermute | solution.py:358
  27.4 4.9 %collective-permute-start.7 = (f32[72,128]{1,0:T(8,128)S(1)}, f32[72,128]{1,0:T(8,128)S(1)}, u32[]{:S(2)}, u32[]{:S(2)}) collective-permute-start(f32[72,128]{1,0:T(8,128)S(1)} %add_add_fusion.1), channel_id=1, source_target_pairs={{0,16},{1,17},{2,18},{3,19},{4,20},{5,21},{6,22},{7,23},{8,24},{9,... | collective-permute-start | bytes 110600 | tf_op jit(solution)/shard_map/ppermute | solution.py:358
  27.4 4.9 %collective-permute-start.6 = (f32[72,128]{1,0:T(8,128)S(1)}, f32[72,128]{1,0:T(8,128)S(1)}, u32[]{:S(2)}, u32[]{:S(2)}) collective-permute-start(f32[72,128]{1,0:T(8,128)S(1)} %add_add_fusion.1), channel_id=1, source_target_pairs={{0,8},{1,9},{2,10},{3,11},{4,12},{5,13},{6,14},{7,15},{8,0},{9,1},... | collective-permute-start | bytes 110600 | tf_op jit(solution)/shard_map/ppermute | solution.py:358
  32.2 1.3 %collective-permute-start.9 = (f32[72,128]{1,0:T(8,128)S(1)}, f32[72,128]{1,0:T(8,128)S(1)}, u32[]{:S(2)}, u32[]{:S(2)}) collective-permute-start(f32[72,128]{1,0:T(8,128)S(1)} %add_add_fusion.refs_0_), channel_id=1, source_target_pairs={{0,1},{1,0},{2,3},{3,2},{4,5},{5,4},{6,7},{7,6},{8,9},{9,8},{10,11... | collective-permute-start | bytes 110600 | tf_op jit(solution)/shard_map/ppermute | solution.py:382

commit v5 on v4

--- a/solution.py
+++ b/solution.py
@@ -48,6 +48,14 @@
 def right6(x, axis=0):
     high, mid, low = three(x)
     return jnp.concatenate([high, mid, high, low, high, mid], axis)
+
+
+def beside(a, b):
+    return jnp.concatenate([a, b], 1)
+
+
+def stack(a, b):
+    return jnp.concatenate([a, b], 0)
 
 
 def iotas(shape):
@@ -201,14 +209,14 @@
     filtered[0] += scale * (dot(sym_ref[0], head_r) + behind)
     filtered[1] += scale * dot(ct_ref[0], head_r)
     filtered[last - 1] += scale * dot(cl_ref[last - 1], tail_r)
-    filtered[last] += scale * (dot(sym_ref[last], tail_r) + dot(cl_ref[last], right3(ahead)))
+    filtered[last] += scale * dot(beside(sym_ref[last], cl_ref[last]), stack(tail_r, right3(ahead)))
     beyond = other + scale * (dot(left3(unpack(right[2])), right3(onward)) / half_width + dot(ct_ref[last], tail_r))
     filtered.append(beyond)
     fr = [right3(x) for x in filtered]
     both = []
     for b in range(nblocks):
         filt_ref[b] = filtered[b]
-        image = 0.5 * (dot(sym_ref[b], fr[b]) + center * filtered[b]) + dot(cl_ref[b], fr[b + 1])
+        image = dot(beside(sym_ref[b] * 0.5, cl_ref[b]), stack(fr[b], fr[b + 1])) + 0.5 * center * filtered[b]
         both.append(jnp.concatenate([filtered[b], image], 1))
     total = None
     for b in range(nblocks):
@@ -323,16 +331,20 @@
     factor(full, inv_ref)
     inv = inv_ref[...]
     inv_r = right6(inv, 1)
+    half = dot(left6(inv), right6(mixed))
+    grown = right6(inv * math.sqrt(total_nodes), 1)
     copies = []
-    grown = right6(inv * math.sqrt(total_nodes), 1)
+
+    def send(source, target):
+        copies.append(pltpu.make_async_copy(source, target, sems.at[len(copies)]))
+        copies[-1].start()
+
     for b in range(nblocks):
         orth_ref[b] = dot(left6(filt_ref[b]), grown, (1, 1))
-        copies.append(pltpu.make_async_copy(orth_ref.at[b], orth_hbm.at[b], sems.at[b]))
-        copies[b].start()
-    half = dot(left6(inv), right6(mixed))
-    proj_ref[...] = dot(left6(half), inv_r, (1, 1))
-    copies.append(pltpu.make_async_copy(proj_ref, proj_hbm, sems.at[nblocks]))
-    copies[nblocks].start()
+        send(orth_ref.at[b], orth_hbm.at[b])
+        if b == 0:
+            proj_ref[...] = dot(left6(half), inv_r, (1, 1))
+            send(proj_ref, proj_hbm)
     for copy in copies:
         copy.wait()
 
@@ -377,8 +389,9 @@
 def swap(values, axis, start):
     count = lax.axis_size(axis)
     route = []
-    for i in range(start, count - 1, 2):
-        route += [(i, i + 1), (i + 1, i)]
+    for i in range(start, count - 1 + (start if count % 2 == 0 else 0), 2):
+        other = (i + 1) % count
+        route += [(i, other), (other, i)]
     return lax.ppermute(values, axis, route)
 
 

time: 37.4 us -> 35.4 us (0.947)
  starting transfers between devices: 17.3 us -> 14.7 us
  waiting for transfers between devices: 11.2 us -> 12 us
    ppermute x4, waiting for transfers between devices: 3.19 us -> 4.92 us  [swap(): return lax.ppermute(values, axis, route)]
    ppermute x4, starting transfers between devices: 8.21 us -> 6.73 us  [swap(): return lax.ppermute(values, axis, route)]
    ppermute x6, starting transfers between devices: 9.06 us -> 7.94 us  [add_up(): parts.append(lax.ppermute(values, axis, route(lambda k: k ^ flip)))]
    ppermute x6, waiting for transfers between devices: 8.03 us -> 7.08 us  [add_up(): parts.append(lax.ppermute(values, axis, route(lambda k: k ^ flip)))]
  transfers between devices with their start and end apart: 10 -> 10, of which waited for: 8 -> 8; matrix products, arithmetic and copies ran while one was open for 0% -> 0% of each run, Pallas kernels for 3% -> 4%
where the time goes in v5:
time: 35.4 us; the launch traced here: 35.2 us
  starting transfers between devices  14.7 us (42%)
  waiting for transfers between devices  12 us (34%)
  Pallas kernels  7.81 us (22%)
  between operations  0.69 us (2%)
    ppermute x6, starting transfers between devices, add_up(): parts.append(lax.ppermute(values, axis, route(lambda k: k ^ flip)))  7.94 us
    ppermute x6, waiting for transfers between devices, add_up(): parts.append(lax.ppermute(values, axis, route(lambda k: k ^ flip)))  7.08 us
    ppermute x4, starting transfers between devices, swap(): return lax.ppermute(values, axis, route)  6.73 us
    ppermute x4, waiting for transfers between devices, swap(): return lax.ppermute(values, axis, route)  4.92 us
    pallas_call x1, Pallas kernels, body(): call(lambda *refs: finish(axis, nodes_dev * devices, *refs), [here] * 3,...  3.56 us
    pallas_call x1, Pallas kernels, body(): call(lambda *refs: edge(axis, *refs), [far] * 3, [(cross, here), (tall, h...  1.64 us
    pallas_call x1, Pallas kernels, body(): call(lambda *refs: project(axis, *refs), [here] * 9, [(tall, here), (piec...  1.36 us
    pallas_call x1, Pallas kernels, body(): call(lambda *refs: inner(axis, *refs), [here] * 3, [(cross, here), (wide,...  1.25 us
  transfers between devices with their start and end apart: 10, of which 8 were waited for; matrix products, arithmetic and copies ran while one was open for 0% of the time, Pallas kernels for 4%

profile of v5, /device:TPU:0, one launch (start us, length us, event | category | flops | bytes accessed | tf_op | source)
XLA Modules:
  0.0 35.2 jit_solution(13107406218574223999)
XLA Ops:
  0.6 1.6 %shard_map.50 = (f32[456,128]{1,0:T(8,128)S(1)}, f32[4,128,128]{2,1,0:T(8,128)S(1)}, f32[4,128,128]{2,1,0:T(8,128)S(1)}, f32[4,128,128]{2,1,0:T(8,128)S(1)}) custom-call(f32[4,128,128]{2,1,0:T(8,128)} %bitcast.2, f32[4,128,128]{2,1,0:T(8,128)} %refs_1_.1, f32[4,128,128]{2,1,0:T(8,128)} %refs_2_.1), custom_call_target="tpu_custom_call" | custom-call | tf_op jit(solution)/shard_map/pallas_call | solution.py:420
  2.3 6.5 %collective-permute-start.1 = (f32[456,128]{1,0:T(8,128)S(1)}, f32[456,128]{1,0:T(8,128)S(1)}, u32[]{:S(2)}, u32[]{:S(2)}) collective-permute-start(f32[456,128]{1,0:T(8,128)S(1)} %get-tuple-element.28), channel_id=1, source_target_pairs={{1,2},{2,1},{3,4},{4,3},{5,6},{6,5},{7,8},{8,7},{9,10},{10,9},{11,... | collective-permute-start | bytes 700424 | tf_op jit(solution)/shard_map/ppermute | solution.py:395
  8.8 1.2 %shard_map.51 = (f32[456,128]{1,0:T(8,128)S(1)}, bf16[4,128,384]{2,1,0:T(8,128)(2,1)S(1)}, bf16[4,128,384]{2,1,0:T(8,128)(2,1)S(1)}, bf16[4,128,384]{2,1,0:T(8,1...) custom-call(f32[4,128,128]{2,1,0:T(8,128)S(1)} %get-tuple-element.18.refs_0_, ...), custom_call_target="tpu_custom_call" | custom-call | tf_op jit(solution)/shard_map/pallas_call | solution.py:427
  10.0 0.1 collective-permute-start
  10.1 2.5 %collective-permute-done.1.refs_8_ = f32[456,128]{1,0:T(8,128)S(1)} collective-permute-done((f32[456,128]{1,0:T(8,128)S(1)}, f32[456,128]{1,0:T(8,128)S(1)}, u32[]{:S(2)}, u32[]{:S(2)}) %collective-permute-start.1) | collective-permute-done | bytes 233504 | tf_op jit(solution)/shard_map/ppermute | solution.py:395
  12.6 0.0 collective-permute-done.refs_7_
  12.6 1.4 %shard_map.52 = (f32[4,128,128]{2,1,0:T(8,128)S(1)}, f32[72,128]{1,0:T(8,128)S(1)}, f32[72,128]{1,0:T(8,128)S(1)}) custom-call(f32[4,128,128]{2,1,0:T(8,128)S(1)} %get-tuple-element.18.refs_0_, bf16[4,128,384]{2,1,0:T(8,128)(2,1)S(1)} %get-tuple-element.21.refs_1_, bf16[4,128,384]{2,1,0:T(8,128)(2,1)S(1)} %get-tuple-element.22.refs_2_, ...), custom_call_target="tpu_custom_call" | custom-call | tf_op jit(solution)/shard_map/pallas_call | solution.py:434
  14.0 0.1 collective-permute-start.2
  14.1 1.2 %collective-permute-done.2 = f32[72,128]{1,0:T(8,128)S(1)} collective-permute-done((f32[72,128]{1,0:T(8,128)S(1)}, f32[72,128]{1,0:T(8,128)S(1)}, u32[]{:S(2)}, u32[]{:S(2)}) %collective-permute-start.2) | collective-permute-done | bytes 36896 | tf_op jit(solution)/shard_map/ppermute | solution.py:395
  15.3 1.6 %collective-permute-start.5 = (f32[72,128]{1,0:T(8,128)S(1)}, f32[72,128]{1,0:T(8,128)S(1)}, u32[]{:S(2)}, u32[]{:S(2)}) collective-permute-start(f32[72,128]{1,0:T(8,128)S(1)} %add.21), channel_id=1, source_target_pairs={{0,6},{1,7},{2,4},{3,5},{4,2},{5,3},{6,0},{7,1},{8,14},{9,15},{10,... | collective-permute-start | bytes 110600 | tf_op jit(solution)/shard_map/ppermute | solution.py:370
  16.9 0.9 %collective-permute-start.4 = (f32[72,128]{1,0:T(8,128)S(1)}, f32[72,128]{1,0:T(8,128)S(1)}, u32[]{:S(2)}, u32[]{:S(2)}) collective-permute-start(f32[72,128]{1,0:T(8,128)S(1)} %add.21), channel_id=1, source_target_pairs={{0,4},{1,5},{2,6},{3,7},{4,0},{5,1},{6,2},{7,3},{8,12},{9,13},{10,... | collective-permute-start | bytes 110600 | tf_op jit(solution)/shard_map/ppermute | solution.py:370
  17.8 0.9 %collective-permute-start.3 = (f32[72,128]{1,0:T(8,128)S(1)}, f32[72,128]{1,0:T(8,128)S(1)}, u32[]{:S(2)}, u32[]{:S(2)}) collective-permute-start(f32[72,128]{1,0:T(8,128)S(1)} %add.21), channel_id=1, source_target_pairs={{0,2},{1,3},{2,0},{3,1},{4,6},{5,7},{6,4},{7,5},{8,10},{9,11},{10,... | collective-permute-start | bytes 110600 | tf_op jit(solution)/shard_map/ppermute | solution.py:370
  18.8 1.4 %collective-permute-done.5 = f32[72,128]{1,0:T(8,128)S(1)} collective-permute-done((f32[72,128]{1,0:T(8,128)S(1)}, f32[72,128]{1,0:T(8,128)S(1)}, u32[]{:S(2)}, u32[]{:S(2)}) %collective-permute-start.5) | collective-permute-done | bytes 36896 | tf_op jit(solution)/shard_map/ppermute | solution.py:370
  20.2 0.7 %collective-permute-done.4 = f32[72,128]{1,0:T(8,128)S(1)} collective-permute-done((f32[72,128]{1,0:T(8,128)S(1)}, f32[72,128]{1,0:T(8,128)S(1)}, u32[]{:S(2)}, u32[]{:S(2)}) %collective-permute-start.4) | collective-permute-done | bytes 36896 | tf_op jit(solution)/shard_map/ppermute | solution.py:370
  20.9 0.9 %collective-permute-done.3 = f32[72,128]{1,0:T(8,128)S(1)} collective-permute-done((f32[72,128]{1,0:T(8,128)S(1)}, f32[72,128]{1,0:T(8,128)S(1)}, u32[]{:S(2)}, u32[]{:S(2)}) %collective-permute-start.3) | collective-permute-done | bytes 36896 | tf_op jit(solution)/shard_map/ppermute | solution.py:370
  21.8 3.7 %collective-permute-start.8 = (f32[72,128]{1,0:T(8,128)S(1)}, f32[72,128]{1,0:T(8,128)S(1)}, u32[]{:S(2)}, u32[]{:S(2)}) collective-permute-start(f32[72,128]{1,0:T(8,128)S(1)} %add_add_fusion.1), channel_id=1, source_target_pairs={{0,24},{1,25},{2,26},{3,27},{4,28},{5,29},{6,30},{7,31},{8,16},{9,... | collective-permute-start | bytes 110600 | tf_op jit(solution)/shard_map/ppermute | solution.py:370
  25.5 0.0 collective-permute-start.7
  25.5 0.8 %collective-permute-start.6 = (f32[72,128]{1,0:T(8,128)S(1)}, f32[72,128]{1,0:T(8,128)S(1)}, u32[]{:S(2)}, u32[]{:S(2)}) collective-permute-start(f32[72,128]{1,0:T(8,128)S(1)} %add_add_fusion.1), channel_id=1, source_target_pairs={{0,8},{1,9},{2,10},{3,11},{4,12},{5,13},{6,14},{7,15},{8,0},{9,1},... | collective-permute-start | bytes 110600 | tf_op jit(solution)/shard_map/ppermute | solution.py:370
  26.3 1.4 %collective-permute-done.8 = f32[72,128]{1,0:T(8,128)S(1)} collective-permute-done((f32[72,128]{1,0:T(8,128)S(1)}, f32[72,128]{1,0:T(8,128)S(1)}, u32[]{:S(2)}, u32[]{:S(2)}) %collective-permute-start.8) | collective-permute-done | bytes 36896 | tf_op jit(solution)/shard_map/ppermute | solution.py:370
  27.6 2.7 %collective-permute-done.7 = f32[72,128]{1,0:T(8,128)S(1)} collective-permute-done((f32[72,128]{1,0:T(8,128)S(1)}, f32[72,128]{1,0:T(8,128)S(1)}, u32[]{:S(2)}, u32[]{:S(2)}) %collective-permute-start.7) | collective-permute-done | bytes 36896 | tf_op jit(solution)/shard_map/ppermute | solution.py:370
  30.3 0.0 collective-permute-done.6
  30.4 0.1 collective-permute-start.9
  30.4 1.2 %collective-permute-done.9.refs_1_ = f32[72,128]{1,0:T(8,128)S(1)} collective-permute-done((f32[72,128]{1,0:T(8,128)S(1)}, f32[72,128]{1,0:T(8,128)S(1)}, u32[]{:S(2)}, u32[]{:S(2)}) %collective-permute-start.9) | collective-permute-done | bytes 36896 | tf_op jit(solution)/shard_map/ppermute | solution.py:395
  31.6 3.6 %shard_map.53 = (f32[4,128,128]{2,1,0:T(8,128)}, f32[128,128]{1,0:T(8,128)}) custom-call(f32[72,128]{1,0:T(8,128)S(1)} %add_add_fusion.refs_0_, f32[72,128]{1,0:T(8,128)S(1)} %collective-permute-done.9.refs_1_, f32[4,128,128]{2,1,0:T(8,128)S(1)} %get-tuple-element.31.refs_2_), custom_call_target="tpu_custom_call" | custom-call | tf_op jit(solution)/shard_map/pallas_call | solution.py:439
  (3 shorter events, 0.0 us)
Async XLA Ops:
  2.3 10.4 %collective-permute-start.1 = (f32[456,128]{1,0:T(8,128)S(1)}, f32[456,128]{1,0:T(8,128)S(1)}, u32[]{:S(2)}, u32[]{:S(2)}) collective-permute-start(f32[456,128]{1,0:T(8,128)S(1)} %get-tuple-element.28), channel_id=1, source_target_pairs={{1,2},{2,1},{3,4},{4,3},{5,6},{6,5},{7,8},{8,7},{9,10},{10,9},{11,... | collective-permute-start | bytes 700424 | tf_op jit(solution)/shard_map/ppermute | solution.py:395
  10.0 2.6 %collective-permute-start = (f32[456,128]{1,0:T(8,128)S(1)}, f32[456,128]{1,0:T(8,128)S(1)}, u32[]{:S(2)}, u32[]{:S(2)}) collective-permute-start(f32[456,128]{1,0:T(8,128)S(1)} %get-tuple-element.27), channel_id=1, source_target_pairs={{0,1},{1,0},{2,3},{3,2},{4,5},{5,4},{6,7},{7,6},{8,9},{9,8},{10,11... | collective-permute-start | bytes 700424 | tf_op jit(solution)/shard_map/ppermute | solution.py:395
  14.0 1.3 %collective-permute-start.2 = (f32[72,128]{1,0:T(8,128)S(1)}, f32[72,128]{1,0:T(8,128)S(1)}, u32[]{:S(2)}, u32[]{:S(2)}) collective-permute-start(f32[72,128]{1,0:T(8,128)S(1)} %get-tuple-element.30), channel_id=1, source_target_pairs={{0,1},{1,0},{2,3},{3,2},{4,5},{5,4},{6,7},{7,6},{8,9},{9,8},{10,11... | collective-permute-start | bytes 110600 | tf_op jit(solution)/shard_map/ppermute | solution.py:395
  15.3 4.9 %collective-permute-start.5 = (f32[72,128]{1,0:T(8,128)S(1)}, f32[72,128]{1,0:T(8,128)S(1)}, u32[]{:S(2)}, u32[]{:S(2)}) collective-permute-start(f32[72,128]{1,0:T(8,128)S(1)} %add.21), channel_id=1, source_target_pairs={{0,6},{1,7},{2,4},{3,5},{4,2},{5,3},{6,0},{7,1},{8,14},{9,15},{10,... | collective-permute-start | bytes 110600 | tf_op jit(solution)/shard_map/ppermute | solution.py:370
  16.9 4.0 %collective-permute-start.4 = (f32[72,128]{1,0:T(8,128)S(1)}, f32[72,128]{1,0:T(8,128)S(1)}, u32[]{:S(2)}, u32[]{:S(2)}) collective-permute-start(f32[72,128]{1,0:T(8,128)S(1)} %add.21), channel_id=1, source_target_pairs={{0,4},{1,5},{2,6},{3,7},{4,0},{5,1},{6,2},{7,3},{8,12},{9,13},{10,... | collective-permute-start | bytes 110600 | tf_op jit(solution)/shard_map/ppermute | solution.py:370
  17.8 4.0 %collective-permute-start.3 = (f32[72,128]{1,0:T(8,128)S(1)}, f32[72,128]{1,0:T(8,128)S(1)}, u32[]{:S(2)}, u32[]{:S(2)}) collective-permute-start(f32[72,128]{1,0:T(8,128)S(1)} %add.21), channel_id=1, source_target_pairs={{0,2},{1,3},{2,0},{3,1},{4,6},{5,7},{6,4},{7,5},{8,10},{9,11},{10,... | collective-permute-start | bytes 110600 | tf_op jit(solution)/shard_map/ppermute | solution.py:370
  21.8 5.8 %collective-permute-start.8 = (f32[72,128]{1,0:T(8,128)S(1)}, f32[72,128]{1,0:T(8,128)S(1)}, u32[]{:S(2)}, u32[]{:S(2)}) collective-permute-start(f32[72,128]{1,0:T(8,128)S(1)} %add_add_fusion.1), channel_id=1, source_target_pairs={{0,24},{1,25},{2,26},{3,27},{4,28},{5,29},{6,30},{7,31},{8,16},{9,... | collective-permute-start | bytes 110600 | tf_op jit(solution)/shard_map/ppermute | solution.py:370
  25.5 4.9 %collective-permute-start.7 = (f32[72,128]{1,0:T(8,128)S(1)}, f32[72,128]{1,0:T(8,128)S(1)}, u32[]{:S(2)}, u32[]{:S(2)}) collective-permute-start(f32[72,128]{1,0:T(8,128)S(1)} %add_add_fusion.1), channel_id=1, source_target_pairs={{0,16},{1,17},{2,18},{3,19},{4,20},{5,21},{6,22},{7,23},{8,24},{9,... | collective-permute-start | bytes 110600 | tf_op jit(solution)/shard_map/ppermute | solution.py:370
  25.5 4.9 %collective-permute-start.6 = (f32[72,128]{1,0:T(8,128)S(1)}, f32[72,128]{1,0:T(8,128)S(1)}, u32[]{:S(2)}, u32[]{:S(2)}) collective-permute-start(f32[72,128]{1,0:T(8,128)S(1)} %add_add_fusion.1), channel_id=1, source_target_pairs={{0,8},{1,9},{2,10},{3,11},{4,12},{5,13},{6,14},{7,15},{8,0},{9,1},... | collective-permute-start | bytes 110600 | tf_op jit(solution)/shard_map/ppermute | solution.py:370
  30.4 1.3 %collective-permute-start.9 = (f32[72,128]{1,0:T(8,128)S(1)}, f32[72,128]{1,0:T(8,128)S(1)}, u32[]{:S(2)}, u32[]{:S(2)}) collective-permute-start(f32[72,128]{1,0:T(8,128)S(1)} %add_add_fusion.refs_0_), channel_id=1, source_target_pairs={{0,1},{1,0},{2,3},{3,2},{4,5},{5,4},{6,7},{7,6},{8,9},{9,8},{10,11... | collective-permute-start | bytes 110600 | tf_op jit(solution)/shard_map/ppermute | solution.py:395

commit v6 on v5

--- a/solution.py
+++ b/solution.py
@@ -191,7 +191,7 @@
 
 
 def project(axis, s_ref, sym_ref, cl_ref, ct_ref, first_ref, pre_ref, pass_ref, even_ref, odd_ref, filt_ref, keep_ref, send_ref):
-    nblocks, block, _ = s_ref.shape
+    nblocks, block, unused = s_ref.shape
     last = nblocks - 1
     parity = lax.rem(lax.axis_index(axis), 2)
     rows = odd_ref.shape[0] - block
@@ -213,17 +213,21 @@
     beyond = other + scale * (dot(left3(unpack(right[2])), right3(onward)) / half_width + dot(ct_ref[last], tail_r))
     filtered.append(beyond)
     fr = [right3(x) for x in filtered]
-    both = []
+    images = []
     for b in range(nblocks):
         filt_ref[b] = filtered[b]
         image = dot(beside(sym_ref[b] * 0.5, cl_ref[b]), stack(fr[b], fr[b + 1])) + 0.5 * center * filtered[b]
-        both.append(jnp.concatenate([filtered[b], image], 1))
-    total = None
-    for b in range(nblocks):
-        term = dot(left6(filtered[b], 0), right6(both[b], 0), (0, 0))
+        images.append(image)
+    total, fine = None, None
+    for b in range(nblocks):
+        (high, mid, low), (ihigh, imid, unused) = three(filtered[b]), three(images[b])
+        upper = jnp.concatenate([jnp.concatenate([high, mid, high], 0), jnp.concatenate([ihigh, imid, ihigh], 0)], 1)
+        term = dot(jnp.concatenate([high, high, mid], 0), upper, (0, 0))
+        extra = dot(jnp.concatenate([high, low, mid], 0), jnp.concatenate([low, high, mid], 0), (0, 0))
         total = term if total is None else total + term
+        fine = extra if fine is None else fine + extra
     width = filtered[0].shape[1]
-    correlation, half = total[:, :width], total[:, width:]
+    correlation, half = total[:, :width] + fine, total[:, width:]
     mixed = half + half.T
     rows, cols = iotas((width, width))
     packed = jnp.where(rows >= cols, correlation, mixed)

time: 35.4 us -> 35.1 us (level)
  no operation moved by 1% of the time
where the time goes in v6:
time: 35.1 us; the launch traced here: 34.9 us
  starting transfers between devices  14.7 us (42%)
  waiting for transfers between devices  12 us (34%)
  Pallas kernels  7.52 us (21%)
  between operations  0.69 us (2%)
    ppermute x6, starting transfers between devices, add_up(): parts.append(lax.ppermute(values, axis, route(lambda k: k ^ flip)))  7.94 us
    ppermute x6, waiting for transfers between devices, add_up(): parts.append(lax.ppermute(values, axis, route(lambda k: k ^ flip)))  7.09 us
    ppermute x4, starting transfers between devices, swap(): return lax.ppermute(values, axis, route)  6.73 us
    ppermute x4, waiting for transfers between devices, swap(): return lax.ppermute(values, axis, route)  4.92 us
    pallas_call x1, Pallas kernels, body(): call(lambda *refs: finish(axis, nodes_dev * devices, *refs), [here] * 3,...  3.56 us
    pallas_call x1, Pallas kernels, body(): call(lambda *refs: edge(axis, *refs), [far] * 3, [(cross, here), (tall, h...  1.64 us
    pallas_call x1, Pallas kernels, body(): call(lambda *refs: inner(axis, *refs), [here] * 3, [(cross, here), (wide,...  1.25 us
    pallas_call x1, Pallas kernels, body(): call(lambda *refs: project(axis, *refs), [here] * 9, [(tall, here), (piec...  1.07 us
  transfers between devices with their start and end apart: 10, of which 8 were waited for; matrix products, arithmetic and copies ran while one was open for 0% of the time, Pallas kernels for 4%

profile of v6, /device:TPU:0, one launch (start us, length us, event | category | flops | bytes accessed | tf_op | source)
XLA Modules:
  0.0 34.9 jit_solution(12625704162065309176)
XLA Ops:
  0.6 1.6 %shard_map.50 = (f32[456,128]{1,0:T(8,128)S(1)}, f32[4,128,128]{2,1,0:T(8,128)S(1)}, f32[4,128,128]{2,1,0:T(8,128)S(1)}, f32[4,128,128]{2,1,0:T(8,128)S(1)}) custom-call(f32[4,128,128]{2,1,0:T(8,128)} %bitcast.2, f32[4,128,128]{2,1,0:T(8,128)} %refs_1_.1, f32[4,128,128]{2,1,0:T(8,128)} %refs_2_.1), custom_call_target="tpu_custom_call" | custom-call | tf_op jit(solution)/shard_map/pallas_call | solution.py:424
  2.3 6.5 %collective-permute-start.1 = (f32[456,128]{1,0:T(8,128)S(1)}, f32[456,128]{1,0:T(8,128)S(1)}, u32[]{:S(2)}, u32[]{:S(2)}) collective-permute-start(f32[456,128]{1,0:T(8,128)S(1)} %get-tuple-element.28), channel_id=1, source_target_pairs={{1,2},{2,1},{3,4},{4,3},{5,6},{6,5},{7,8},{8,7},{9,10},{10,9},{11,... | collective-permute-start | bytes 700424 | tf_op jit(solution)/shard_map/ppermute | solution.py:399
  8.8 1.2 %shard_map.51 = (f32[456,128]{1,0:T(8,128)S(1)}, bf16[4,128,384]{2,1,0:T(8,128)(2,1)S(1)}, bf16[4,128,384]{2,1,0:T(8,128)(2,1)S(1)}, bf16[4,128,384]{2,1,0:T(8,1...) custom-call(f32[4,128,128]{2,1,0:T(8,128)S(1)} %get-tuple-element.18.refs_0_, ...), custom_call_target="tpu_custom_call" | custom-call | tf_op jit(solution)/shard_map/pallas_call | solution.py:431
  10.0 0.1 collective-permute-start
  10.1 2.5 %collective-permute-done.1.refs_8_ = f32[456,128]{1,0:T(8,128)S(1)} collective-permute-done((f32[456,128]{1,0:T(8,128)S(1)}, f32[456,128]{1,0:T(8,128)S(1)}, u32[]{:S(2)}, u32[]{:S(2)}) %collective-permute-start.1) | collective-permute-done | bytes 233504 | tf_op jit(solution)/shard_map/ppermute | solution.py:399
  12.6 0.0 collective-permute-done.refs_7_
  12.6 1.1 %shard_map.52 = (f32[4,128,128]{2,1,0:T(8,128)S(1)}, f32[72,128]{1,0:T(8,128)S(1)}, f32[72,128]{1,0:T(8,128)S(1)}) custom-call(f32[4,128,128]{2,1,0:T(8,128)S(1)} %get-tuple-element.18.refs_0_, bf16[4,128,384]{2,1,0:T(8,128)(2,1)S(1)} %get-tuple-element.21.refs_1_, bf16[4,128,384]{2,1,0:T(8,128)(2,1)S(1)} %get-tuple-element.22.refs_2_, ...), custom_call_target="tpu_custom_call" | custom-call | tf_op jit(solution)/shard_map/pallas_call | solution.py:438
  13.7 0.1 collective-permute-start.2
  13.8 1.2 %collective-permute-done.2 = f32[72,128]{1,0:T(8,128)S(1)} collective-permute-done((f32[72,128]{1,0:T(8,128)S(1)}, f32[72,128]{1,0:T(8,128)S(1)}, u32[]{:S(2)}, u32[]{:S(2)}) %collective-permute-start.2) | collective-permute-done | bytes 36896 | tf_op jit(solution)/shard_map/ppermute | solution.py:399
  15.0 1.6 %collective-permute-start.5 = (f32[72,128]{1,0:T(8,128)S(1)}, f32[72,128]{1,0:T(8,128)S(1)}, u32[]{:S(2)}, u32[]{:S(2)}) collective-permute-start(f32[72,128]{1,0:T(8,128)S(1)} %add.21), channel_id=1, source_target_pairs={{0,6},{1,7},{2,4},{3,5},{4,2},{5,3},{6,0},{7,1},{8,14},{9,15},{10,... | collective-permute-start | bytes 110600 | tf_op jit(solution)/shard_map/ppermute | solution.py:374
  16.6 1.0 %collective-permute-start.4 = (f32[72,128]{1,0:T(8,128)S(1)}, f32[72,128]{1,0:T(8,128)S(1)}, u32[]{:S(2)}, u32[]{:S(2)}) collective-permute-start(f32[72,128]{1,0:T(8,128)S(1)} %add.21), channel_id=1, source_target_pairs={{0,4},{1,5},{2,6},{3,7},{4,0},{5,1},{6,2},{7,3},{8,12},{9,13},{10,... | collective-permute-start | bytes 110600 | tf_op jit(solution)/shard_map/ppermute | solution.py:374
  17.6 0.9 %collective-permute-start.3 = (f32[72,128]{1,0:T(8,128)S(1)}, f32[72,128]{1,0:T(8,128)S(1)}, u32[]{:S(2)}, u32[]{:S(2)}) collective-permute-start(f32[72,128]{1,0:T(8,128)S(1)} %add.21), channel_id=1, source_target_pairs={{0,2},{1,3},{2,0},{3,1},{4,6},{5,7},{6,4},{7,5},{8,10},{9,11},{10,... | collective-permute-start | bytes 110600 | tf_op jit(solution)/shard_map/ppermute | solution.py:374
  18.5 1.4 %collective-permute-done.5 = f32[72,128]{1,0:T(8,128)S(1)} collective-permute-done((f32[72,128]{1,0:T(8,128)S(1)}, f32[72,128]{1,0:T(8,128)S(1)}, u32[]{:S(2)}, u32[]{:S(2)}) %collective-permute-start.5) | collective-permute-done | bytes 36896 | tf_op jit(solution)/shard_map/ppermute | solution.py:374
  19.9 0.7 %collective-permute-done.4 = f32[72,128]{1,0:T(8,128)S(1)} collective-permute-done((f32[72,128]{1,0:T(8,128)S(1)}, f32[72,128]{1,0:T(8,128)S(1)}, u32[]{:S(2)}, u32[]{:S(2)}) %collective-permute-start.4) | collective-permute-done | bytes 36896 | tf_op jit(solution)/shard_map/ppermute | solution.py:374
  20.6 1.0 %collective-permute-done.3 = f32[72,128]{1,0:T(8,128)S(1)} collective-permute-done((f32[72,128]{1,0:T(8,128)S(1)}, f32[72,128]{1,0:T(8,128)S(1)}, u32[]{:S(2)}, u32[]{:S(2)}) %collective-permute-start.3) | collective-permute-done | bytes 36896 | tf_op jit(solution)/shard_map/ppermute | solution.py:374
  21.5 3.7 %collective-permute-start.8 = (f32[72,128]{1,0:T(8,128)S(1)}, f32[72,128]{1,0:T(8,128)S(1)}, u32[]{:S(2)}, u32[]{:S(2)}) collective-permute-start(f32[72,128]{1,0:T(8,128)S(1)} %add_add_fusion.1), channel_id=1, source_target_pairs={{0,24},{1,25},{2,26},{3,27},{4,28},{5,29},{6,30},{7,31},{8,16},{9,... | collective-permute-start | bytes 110600 | tf_op jit(solution)/shard_map/ppermute | solution.py:374
  25.2 0.0 collective-permute-start.7
  25.2 0.8 %collective-permute-start.6 = (f32[72,128]{1,0:T(8,128)S(1)}, f32[72,128]{1,0:T(8,128)S(1)}, u32[]{:S(2)}, u32[]{:S(2)}) collective-permute-start(f32[72,128]{1,0:T(8,128)S(1)} %add_add_fusion.1), channel_id=1, source_target_pairs={{0,8},{1,9},{2,10},{3,11},{4,12},{5,13},{6,14},{7,15},{8,0},{9,1},... | collective-permute-start | bytes 110600 | tf_op jit(solution)/shard_map/ppermute | solution.py:374
  26.0 1.4 %collective-permute-done.8 = f32[72,128]{1,0:T(8,128)S(1)} collective-permute-done((f32[72,128]{1,0:T(8,128)S(1)}, f32[72,128]{1,0:T(8,128)S(1)}, u32[]{:S(2)}, u32[]{:S(2)}) %collective-permute-start.8) | collective-permute-done | bytes 36896 | tf_op jit(solution)/shard_map/ppermute | solution.py:374
  27.4 2.7 %collective-permute-done.7 = f32[72,128]{1,0:T(8,128)S(1)} collective-permute-done((f32[72,128]{1,0:T(8,128)S(1)}, f32[72,128]{1,0:T(8,128)S(1)}, u32[]{:S(2)}, u32[]{:S(2)}) %collective-permute-start.7) | collective-permute-done | bytes 36896 | tf_op jit(solution)/shard_map/ppermute | solution.py:374
  30.1 0.0 collective-permute-done.6
  30.1 0.1 collective-permute-start.9
  30.1 1.2 %collective-permute-done.9.refs_1_ = f32[72,128]{1,0:T(8,128)S(1)} collective-permute-done((f32[72,128]{1,0:T(8,128)S(1)}, f32[72,128]{1,0:T(8,128)S(1)}, u32[]{:S(2)}, u32[]{:S(2)}) %collective-permute-start.9) | collective-permute-done | bytes 36896 | tf_op jit(solution)/shard_map/ppermute | solution.py:399
  31.4 3.6 %shard_map.53 = (f32[4,128,128]{2,1,0:T(8,128)}, f32[128,128]{1,0:T(8,128)}) custom-call(f32[72,128]{1,0:T(8,128)S(1)} %add_add_fusion.refs_0_, f32[72,128]{1,0:T(8,128)S(1)} %collective-permute-done.9.refs_1_, f32[4,128,128]{2,1,0:T(8,128)S(1)} %get-tuple-element.31.refs_2_), custom_call_target="tpu_custom_call" | custom-call | tf_op jit(solution)/shard_map/pallas_call | solution.py:443
  (3 shorter events, 0.0 us)
Async XLA Ops:
  2.3 10.4 %collective-permute-start.1 = (f32[456,128]{1,0:T(8,128)S(1)}, f32[456,128]{1,0:T(8,128)S(1)}, u32[]{:S(2)}, u32[]{:S(2)}) collective-permute-start(f32[456,128]{1,0:T(8,128)S(1)} %get-tuple-element.28), channel_id=1, source_target_pairs={{1,2},{2,1},{3,4},{4,3},{5,6},{6,5},{7,8},{8,7},{9,10},{10,9},{11,... | collective-permute-start | bytes 700424 | tf_op jit(solution)/shard_map/ppermute | solution.py:399
  10.0 2.6 %collective-permute-start = (f32[456,128]{1,0:T(8,128)S(1)}, f32[456,128]{1,0:T(8,128)S(1)}, u32[]{:S(2)}, u32[]{:S(2)}) collective-permute-start(f32[456,128]{1,0:T(8,128)S(1)} %get-tuple-element.27), channel_id=1, source_target_pairs={{0,1},{1,0},{2,3},{3,2},{4,5},{5,4},{6,7},{7,6},{8,9},{9,8},{10,11... | collective-permute-start | bytes 700424 | tf_op jit(solution)/shard_map/ppermute | solution.py:399
  13.7 1.3 %collective-permute-start.2 = (f32[72,128]{1,0:T(8,128)S(1)}, f32[72,128]{1,0:T(8,128)S(1)}, u32[]{:S(2)}, u32[]{:S(2)}) collective-permute-start(f32[72,128]{1,0:T(8,128)S(1)} %get-tuple-element.30), channel_id=1, source_target_pairs={{0,1},{1,0},{2,3},{3,2},{4,5},{5,4},{6,7},{7,6},{8,9},{9,8},{10,11... | collective-permute-start | bytes 110600 | tf_op jit(solution)/shard_map/ppermute | solution.py:399
  15.0 4.9 %collective-permute-start.5 = (f32[72,128]{1,0:T(8,128)S(1)}, f32[72,128]{1,0:T(8,128)S(1)}, u32[]{:S(2)}, u32[]{:S(2)}) collective-permute-start(f32[72,128]{1,0:T(8,128)S(1)} %add.21), channel_id=1, source_target_pairs={{0,6},{1,7},{2,4},{3,5},{4,2},{5,3},{6,0},{7,1},{8,14},{9,15},{10,... | collective-permute-start | bytes 110600 | tf_op jit(solution)/shard_map/ppermute | solution.py:374
  16.6 4.0 %collective-permute-start.4 = (f32[72,128]{1,0:T(8,128)S(1)}, f32[72,128]{1,0:T(8,128)S(1)}, u32[]{:S(2)}, u32[]{:S(2)}) collective-permute-start(f32[72,128]{1,0:T(8,128)S(1)} %add.21), channel_id=1, source_target_pairs={{0,4},{1,5},{2,6},{3,7},{4,0},{5,1},{6,2},{7,3},{8,12},{9,13},{10,... | collective-permute-start | bytes 110600 | tf_op jit(solution)/shard_map/ppermute | solution.py:374
  17.6 4.0 %collective-permute-start.3 = (f32[72,128]{1,0:T(8,128)S(1)}, f32[72,128]{1,0:T(8,128)S(1)}, u32[]{:S(2)}, u32[]{:S(2)}) collective-permute-start(f32[72,128]{1,0:T(8,128)S(1)} %add.21), channel_id=1, source_target_pairs={{0,2},{1,3},{2,0},{3,1},{4,6},{5,7},{6,4},{7,5},{8,10},{9,11},{10,... | collective-permute-start | bytes 110600 | tf_op jit(solution)/shard_map/ppermute | solution.py:374
  21.5 5.8 %collective-permute-start.8 = (f32[72,128]{1,0:T(8,128)S(1)}, f32[72,128]{1,0:T(8,128)S(1)}, u32[]{:S(2)}, u32[]{:S(2)}) collective-permute-start(f32[72,128]{1,0:T(8,128)S(1)} %add_add_fusion.1), channel_id=1, source_target_pairs={{0,24},{1,25},{2,26},{3,27},{4,28},{5,29},{6,30},{7,31},{8,16},{9,... | collective-permute-start | bytes 110600 | tf_op jit(solution)/shard_map/ppermute | solution.py:374
  25.2 4.9 %collective-permute-start.7 = (f32[72,128]{1,0:T(8,128)S(1)}, f32[72,128]{1,0:T(8,128)S(1)}, u32[]{:S(2)}, u32[]{:S(2)}) collective-permute-start(f32[72,128]{1,0:T(8,128)S(1)} %add_add_fusion.1), channel_id=1, source_target_pairs={{0,16},{1,17},{2,18},{3,19},{4,20},{5,21},{6,22},{7,23},{8,24},{9,... | collective-permute-start | bytes 110600 | tf_op jit(solution)/shard_map/ppermute | solution.py:374
  25.2 4.9 %collective-permute-start.6 = (f32[72,128]{1,0:T(8,128)S(1)}, f32[72,128]{1,0:T(8,128)S(1)}, u32[]{:S(2)}, u32[]{:S(2)}) collective-permute-start(f32[72,128]{1,0:T(8,128)S(1)} %add_add_fusion.1), channel_id=1, source_target_pairs={{0,8},{1,9},{2,10},{3,11},{4,12},{5,13},{6,14},{7,15},{8,0},{9,1},... | collective-permute-start | bytes 110600 | tf_op jit(solution)/shard_map/ppermute | solution.py:374
  30.1 1.3 %collective-permute-start.9 = (f32[72,128]{1,0:T(8,128)S(1)}, f32[72,128]{1,0:T(8,128)S(1)}, u32[]{:S(2)}, u32[]{:S(2)}) collective-permute-start(f32[72,128]{1,0:T(8,128)S(1)} %add_add_fusion.refs_0_), channel_id=1, source_target_pairs={{0,1},{1,0},{2,3},{3,2},{4,5},{5,4},{6,7},{7,6},{8,9},{9,8},{10,11... | collective-permute-start | bytes 110600 | tf_op jit(solution)/shard_map/ppermute | solution.py:399

commit v7 on v6

--- a/solution.py
+++ b/solution.py
@@ -115,40 +115,49 @@
     more_ref[...] = jnp.zeros_like(c_last)
 
 
-def edge(axis, s_hbm, d_hbm, c_hbm, odd_ref, s_ref, d_ref, c_ref, sems):
-    nblocks = d_hbm.shape[0]
-    last = nblocks - 1
-    parity = lax.rem(lax.axis_index(axis), 2)
-    block = s_hbm.shape[1]
-    swap_ref, more_ref = odd_ref.at[: odd_ref.shape[0] - block], odd_ref.at[odd_ref.shape[0] - block :]
-    is_last = lax.axis_index(axis) == lax.axis_size(axis) - 1
-    copies = []
-    for k, (source, target) in enumerate(((s_hbm, s_ref), (d_hbm, d_ref), (c_hbm, c_ref))):
-        copies.append(pltpu.make_async_copy(source, target, sems.at[k]))
+def load(pairs, sems):
+    copies = [pltpu.make_async_copy(source, target, sems.at[k]) for k, (source, target) in enumerate(pairs)]
     for copy in copies:
         copy.start()
     for copy in copies:
         copy.wait()
 
-    @pl.when(is_last)
+
+def cut(axis, c_ref, last):
+    @pl.when(lax.axis_index(axis) == lax.axis_size(axis) - 1)
     def _():
         c_ref[last] = jnp.zeros_like(c_ref[last])
 
+
+def edge(axis, s_hbm, d_hbm, c_hbm, odd_ref, s_ref, d_ref, c_ref, sems):
+    nblocks, block, _ = d_hbm.shape
+    last = nblocks - 1
+    parity = lax.rem(lax.axis_index(axis), 2)
+    swap_ref, more_ref = odd_ref.at[: odd_ref.shape[0] - block], odd_ref.at[odd_ref.shape[0] - block :]
+
+    def bring(s_range, d_range, c_range):
+        ranges = ((s_hbm, s_ref, s_range), (d_hbm, d_ref, d_range), (c_hbm, c_ref, c_range))
+        load([(x.at[a:b], y.at[a:b]) for x, y, (a, b) in ranges], sems)
+
     @pl.when(parity == 0)
     def _():
+        bring((0, 3), (0, 2), (0, 2))
         leftward(s_ref[0], s_ref[1], s_ref[2], symmetric(d_ref[0]), symmetric(d_ref[1]), c_ref[0], c_ref[1], swap_ref, more_ref)
 
     @pl.when(parity != 0)
     def _():
+        bring((last - 1, nblocks), (last, nblocks), (last - 1, nblocks))
+        cut(axis, c_ref, last)
         rightward(s_ref[last - 1], s_ref[last], symmetric(d_ref[last]), c_ref[last - 1], c_ref[last], swap_ref, more_ref)
 
 
-def inner(axis, s_ref, d_ref, c_ref, even_ref, sym_ref, cl_ref, ct_ref, first_ref, pre_ref, pass_ref):
-    nblocks = d_ref.shape[0]
+def inner(axis, s_hbm, d_hbm, c_hbm, s_ref, even_ref, sym_ref, cl_ref, ct_ref, first_ref, pre_ref, pass_ref, d_ref, c_ref, sems):
+    nblocks, block, _ = d_hbm.shape
     last = nblocks - 1
-    block = s_ref.shape[1]
     parity = lax.rem(lax.axis_index(axis), 2)
     swap_ref, more_ref = even_ref.at[: even_ref.shape[0] - block], even_ref.at[even_ref.shape[0] - block :]
+    load(((s_hbm, s_ref), (d_hbm, d_ref), (c_hbm, c_ref)), sems)
+    cut(axis, c_ref, last)
 
     @pl.when(parity != 0)
     def _():
@@ -371,7 +380,9 @@
         if radix in (2, 4):
             parts = [values]
             for flip in range(1, radix):
-                parts.append(lax.ppermute(values, axis, route(lambda k: k ^ flip)))
+                parts.append(lax.ppermute(values, axis, route((lambda k: (k - flip) % 4) if radix == 4 and stride > 2 else (lambda k: k ^ flip))))
+            if radix == 4:
+                parts = [parts[0], parts[2], parts[1], parts[3]]
             while len(parts) > 1:
                 parts = [a + b for a, b in zip(parts[::2], parts[1::2])]
             values = parts[0]
@@ -421,18 +432,18 @@
             compiler_params=params,
         )
 
-    odd, s, d, c = call(
-        lambda *refs: edge(axis, *refs),
+    inputs = tuple(pltpu.with_memory_space_constraint(x, pltpu.HBM) for x in (field, diag_blocks, couplings))
+    squares = [pltpu.VMEM(square.shape, jnp.float32)] * 2 + [pltpu.SemaphoreType.DMA((3,))]
+    (odd,) = call(
+        lambda *refs: edge(axis, *refs), [far] * 3, [(cross, here)], [pltpu.VMEM(tall.shape, jnp.float32)] + squares
+    )(*inputs)
+    odd = swap(odd, axis, 1)
+    s, even, sym, cl, ct, first, pre, onward = call(
+        lambda *refs: inner(axis, *refs),
         [far] * 3,
-        [(cross, here), (tall, here), (square, here), (square, here)],
-        [pltpu.SemaphoreType.DMA((3,))],
-    )(*(pltpu.with_memory_space_constraint(x, pltpu.HBM) for x in (field, diag_blocks, couplings)))
-    odd = swap(odd, axis, 1)
-    even, sym, cl, ct, first, pre, onward = call(
-        lambda *refs: inner(axis, *refs),
-        [here] * 3,
-        [(cross, here), (wide, here), (wide, here), (wide, here), (tall, here), (tall, here), (shape(block, width), here)],
-    )(s, d, c)
+        [(tall, here), (cross, here), (wide, here), (wide, here), (wide, here), (tall, here), (tall, here), (shape(block, width), here)],
+        squares,
+    )(*inputs)
     even = swap(even, axis, 0)
     piece = shape(width // 2 + 8, width)
     filtered, keep, send = call(

time: 35.1 us -> 34.9 us (level)
  waiting for transfers between devices: 12 us -> 10.4 us
  Pallas kernels: 7.52 us -> 8.65 us
    ppermute x4, waiting for transfers between devices: 4.92 us -> 3.77 us  [swap(): return lax.ppermute(values, axis, route)]
    pallas_call x2, Pallas kernels: 2.89 us -> 3.99 us  [the longest x1 2.39 us: body(): call(lambda *refs: inner(axis, *refs), [far] * 3, [(tall, here), (cross,...]
    ppermute x6, waiting for transfers between devices: 7.09 us -> 6.62 us  [add_up(): lax.ppermute(values, axis, route((lambda k: (k - flip) % 4) if radix == 4...]
  transfers between devices with their start and end apart: 10 -> 10, of which waited for: 8 -> 9; matrix products, arithmetic and copies ran while one was open for 0% -> 0% of each run, Pallas kernels for 4% -> 7%
where the time goes in v7:
time: 34.9 us; the launch traced here: 34.7 us
  starting transfers between devices  14.9 us (43%)
  waiting for transfers between devices  10.4 us (30%)
  Pallas kernels  8.65 us (25%)
  between operations  0.69 us (2%)
    ppermute x6, starting transfers between devices, add_up(): lax.ppermute(values, axis, route((lambda k: (k - flip) % 4) if radix == 4...  8.16 us
    ppermute x4, starting transfers between devices, swap(): return lax.ppermute(values, axis, route)  6.79 us
    ppermute x6, waiting for transfers between devices, add_up(): lax.ppermute(values, axis, route((lambda k: (k - flip) % 4) if radix == 4...  6.62 us
    ppermute x4, waiting for transfers between devices, swap(): return lax.ppermute(values, axis, route)  3.77 us
    pallas_call x1, Pallas kernels, body(): call(lambda *refs: finish(axis, nodes_dev * devices, *refs), [here] * 3,...  3.56 us
    pallas_call x1, Pallas kernels, body(): call(lambda *refs: inner(axis, *refs), [far] * 3, [(tall, here), (cross,...  2.39 us
    pallas_call x1, Pallas kernels, body(): call(lambda *refs: edge(axis, *refs), [far] * 3, [(cross, here)], [pltpu....  1.6 us
    pallas_call x1, Pallas kernels, body(): call(lambda *refs: project(axis, *refs), [here] * 9, [(tall, here), (piec...  1.09 us
  transfers between devices with their start and end apart: 10, of which 9 were waited for; matrix products, arithmetic and copies ran while one was open for 0% of the time, Pallas kernels for 7%

profile of v7, /device:TPU:0, one launch (start us, length us, event | category | flops | bytes accessed | tf_op | source)
XLA Modules:
  0.0 34.7 jit_solution(15541284414437019884)
XLA Ops:
  0.6 1.6 %shard_map.51 = f32[456,128]{1,0:T(8,128)S(1)} custom-call(f32[4,128,128]{2,1,0:T(8,128)} %bitcast.2, f32[4,128,128]{2,1,0:T(8,128)} %refs_1_.3, f32[4,128,128]{2,1,0:T(8,128)} %refs_2_.3), custom_call_target="tpu_custom_call" | custom-call | tf_op jit(solution)/shard_map/pallas_call | solution.py:437
  2.2 6.5 %collective-permute-start.1 = (f32[456,128]{1,0:T(8,128)S(1)}, f32[456,128]{1,0:T(8,128)S(1)}, u32[]{:S(2)}, u32[]{:S(2)}) collective-permute-start(f32[456,128]{1,0:T(8,128)S(1)} %shard_map.51), channel_id=1, source_target_pairs={{1,2},{2,1},{3,4},{4,3},{5,6},{6,5},{7,8},{8,7},{9,10},{10,9},{11,... | collective-permute-start | bytes 700424 | tf_op jit(solution)/shard_map/ppermute | solution.py:410
  8.7 2.4 %shard_map.50 = (f32[4,128,128]{2,1,0:T(8,128)S(1)}, f32[456,128]{1,0:T(8,128)S(1)}, bf16[4,128,384]{2,1,0:T(8,128)(2,1)S(1)}, bf16[4,128,384]{2,1,0:T(8,128)(2,...) custom-call(f32[4,128,128]{2,1,0:T(8,128)} %bitcast.3, ...), custom_call_target="tpu_custom_call" | custom-call | tf_op jit(solution)/shard_map/pallas_call | solution.py:441
  11.1 0.1 collective-permute-start
  11.2 1.4 %collective-permute-done.1.refs_8_ = f32[456,128]{1,0:T(8,128)S(1)} collective-permute-done((f32[456,128]{1,0:T(8,128)S(1)}, f32[456,128]{1,0:T(8,128)S(1)}, u32[]{:S(2)}, u32[]{:S(2)}) %collective-permute-start.1) | collective-permute-done | bytes 233504 | tf_op jit(solution)/shard_map/ppermute | solution.py:410
  12.6 0.1 collective-permute-done.refs_7_
  12.7 1.1 %shard_map.52 = (f32[4,128,128]{2,1,0:T(8,128)S(1)}, f32[72,128]{1,0:T(8,128)S(1)}, f32[72,128]{1,0:T(8,128)S(1)}) custom-call(f32[4,128,128]{2,1,0:T(8,128)S(1)} %get-tuple-element.15.refs_0_, bf16[4,128,384]{2,1,0:T(8,128)(2,1)S(1)} %get-tuple-element.16.refs_1_, bf16[4,128,384]{2,1,0:T(8,128)(2,1)S(1)} %get-tuple-element.17.refs_2_, ...), custom_call_target="tpu_custom_call" | custom-call | tf_op jit(solution)/shard_map/pallas_call | solution.py:449
  13.8 0.2 collective-permute-start.2
  14.0 1.1 %collective-permute-done.2 = f32[72,128]{1,0:T(8,128)S(1)} collective-permute-done((f32[72,128]{1,0:T(8,128)S(1)}, f32[72,128]{1,0:T(8,128)S(1)}, u32[]{:S(2)}, u32[]{:S(2)}) %collective-permute-start.2) | collective-permute-done | bytes 36896 | tf_op jit(solution)/shard_map/ppermute | solution.py:410
  15.0 1.5 %collective-permute-start.5 = (f32[72,128]{1,0:T(8,128)S(1)}, f32[72,128]{1,0:T(8,128)S(1)}, u32[]{:S(2)}, u32[]{:S(2)}) collective-permute-start(f32[72,128]{1,0:T(8,128)S(1)} %add.21), channel_id=1, source_target_pairs={{0,6},{1,7},{2,4},{3,5},{4,2},{5,3},{6,0},{7,1},{8,14},{9,15},{10,... | collective-permute-start | bytes 110600 | tf_op jit(solution)/shard_map/ppermute | solution.py:383
  16.5 0.6 %collective-permute-start.4 = (f32[72,128]{1,0:T(8,128)S(1)}, f32[72,128]{1,0:T(8,128)S(1)}, u32[]{:S(2)}, u32[]{:S(2)}) collective-permute-start(f32[72,128]{1,0:T(8,128)S(1)} %add.21), channel_id=1, source_target_pairs={{0,2},{1,3},{2,0},{3,1},{4,6},{5,7},{6,4},{7,5},{8,10},{9,11},{10,... | collective-permute-start | bytes 110600 | tf_op jit(solution)/shard_map/ppermute | solution.py:383
  17.1 1.4 %collective-permute-start.3 = (f32[72,128]{1,0:T(8,128)S(1)}, f32[72,128]{1,0:T(8,128)S(1)}, u32[]{:S(2)}, u32[]{:S(2)}) collective-permute-start(f32[72,128]{1,0:T(8,128)S(1)} %add.21), channel_id=1, source_target_pairs={{0,4},{1,5},{2,6},{3,7},{4,0},{5,1},{6,2},{7,3},{8,12},{9,13},{10,... | collective-permute-start | bytes 110600 | tf_op jit(solution)/shard_map/ppermute | solution.py:383
  18.5 1.7 %collective-permute-done.5 = f32[72,128]{1,0:T(8,128)S(1)} collective-permute-done((f32[72,128]{1,0:T(8,128)S(1)}, f32[72,128]{1,0:T(8,128)S(1)}, u32[]{:S(2)}, u32[]{:S(2)}) %collective-permute-start.5) | collective-permute-done | bytes 36896 | tf_op jit(solution)/shard_map/ppermute | solution.py:383
  20.3 0.2 collective-permute-done.4
  20.5 0.6 %collective-permute-done.3 = f32[72,128]{1,0:T(8,128)S(1)} collective-permute-done((f32[72,128]{1,0:T(8,128)S(1)}, f32[72,128]{1,0:T(8,128)S(1)}, u32[]{:S(2)}, u32[]{:S(2)}) %collective-permute-start.3) | collective-permute-done | bytes 36896 | tf_op jit(solution)/shard_map/ppermute | solution.py:383
  21.1 1.6 %collective-permute-start.8 = (f32[72,128]{1,0:T(8,128)S(1)}, f32[72,128]{1,0:T(8,128)S(1)}, u32[]{:S(2)}, u32[]{:S(2)}) collective-permute-start(f32[72,128]{1,0:T(8,128)S(1)} %add_add_fusion.1), channel_id=1, source_target_pairs={{0,8},{1,9},{2,10},{3,11},{4,12},{5,13},{6,14},{7,15},{8,16},{9,17... | collective-permute-start | bytes 110600 | tf_op jit(solution)/shard_map/ppermute | solution.py:383
  22.7 2.2 %collective-permute-start.7 = (f32[72,128]{1,0:T(8,128)S(1)}, f32[72,128]{1,0:T(8,128)S(1)}, u32[]{:S(2)}, u32[]{:S(2)}) collective-permute-start(f32[72,128]{1,0:T(8,128)S(1)} %add_add_fusion.1), channel_id=1, source_target_pairs={{0,24},{1,25},{2,26},{3,27},{4,28},{5,29},{6,30},{7,31},{8,0},{9,1... | collective-permute-start | bytes 110600 | tf_op jit(solution)/shard_map/ppermute | solution.py:383
  25.0 0.8 %collective-permute-start.6 = (f32[72,128]{1,0:T(8,128)S(1)}, f32[72,128]{1,0:T(8,128)S(1)}, u32[]{:S(2)}, u32[]{:S(2)}) collective-permute-start(f32[72,128]{1,0:T(8,128)S(1)} %add_add_fusion.1), channel_id=1, source_target_pairs={{0,16},{1,17},{2,18},{3,19},{4,20},{5,21},{6,22},{7,23},{8,24},{9,... | collective-permute-start | bytes 110600 | tf_op jit(solution)/shard_map/ppermute | solution.py:383
  25.8 1.5 %collective-permute-done.8 = f32[72,128]{1,0:T(8,128)S(1)} collective-permute-done((f32[72,128]{1,0:T(8,128)S(1)}, f32[72,128]{1,0:T(8,128)S(1)}, u32[]{:S(2)}, u32[]{:S(2)}) %collective-permute-start.8) | collective-permute-done | bytes 36896 | tf_op jit(solution)/shard_map/ppermute | solution.py:383
  27.2 0.0 collective-permute-done.7
  27.2 2.6 %collective-permute-done.6 = f32[72,128]{1,0:T(8,128)S(1)} collective-permute-done((f32[72,128]{1,0:T(8,128)S(1)}, f32[72,128]{1,0:T(8,128)S(1)}, u32[]{:S(2)}, u32[]{:S(2)}) %collective-permute-start.6) | collective-permute-done | bytes 36896 | tf_op jit(solution)/shard_map/ppermute | solution.py:383
  29.9 0.1 collective-permute-start.9
  29.9 1.2 %collective-permute-done.9.refs_1_ = f32[72,128]{1,0:T(8,128)S(1)} collective-permute-done((f32[72,128]{1,0:T(8,128)S(1)}, f32[72,128]{1,0:T(8,128)S(1)}, u32[]{:S(2)}, u32[]{:S(2)}) %collective-permute-start.9) | collective-permute-done | bytes 36896 | tf_op jit(solution)/shard_map/ppermute | solution.py:410
  31.1 3.6 %shard_map.53 = (f32[4,128,128]{2,1,0:T(8,128)}, f32[128,128]{1,0:T(8,128)}) custom-call(f32[72,128]{1,0:T(8,128)S(1)} %add_add_fusion.refs_0_, f32[72,128]{1,0:T(8,128)S(1)} %collective-permute-done.9.refs_1_, f32[4,128,128]{2,1,0:T(8,128)S(1)} %get-tuple-element.25.refs_2_), custom_call_target="tpu_custom_call" | custom-call | tf_op jit(solution)/shard_map/pallas_call | solution.py:454
  (3 shorter events, 0.0 us)
Async XLA Ops:
  2.2 10.3 %collective-permute-start.1 = (f32[456,128]{1,0:T(8,128)S(1)}, f32[456,128]{1,0:T(8,128)S(1)}, u32[]{:S(2)}, u32[]{:S(2)}) collective-permute-start(f32[456,128]{1,0:T(8,128)S(1)} %shard_map.51), channel_id=1, source_target_pairs={{1,2},{2,1},{3,4},{4,3},{5,6},{6,5},{7,8},{8,7},{9,10},{10,9},{11,... | collective-permute-start | bytes 700424 | tf_op jit(solution)/shard_map/ppermute | solution.py:410
  11.1 1.6 %collective-permute-start = (f32[456,128]{1,0:T(8,128)S(1)}, f32[456,128]{1,0:T(8,128)S(1)}, u32[]{:S(2)}, u32[]{:S(2)}) collective-permute-start(f32[456,128]{1,0:T(8,128)S(1)} %get-tuple-element.22), channel_id=1, source_target_pairs={{0,1},{1,0},{2,3},{3,2},{4,5},{5,4},{6,7},{7,6},{8,9},{9,8},{10,11... | collective-permute-start | bytes 700424 | tf_op jit(solution)/shard_map/ppermute | solution.py:410
  13.8 1.3 %collective-permute-start.2 = (f32[72,128]{1,0:T(8,128)S(1)}, f32[72,128]{1,0:T(8,128)S(1)}, u32[]{:S(2)}, u32[]{:S(2)}) collective-permute-start(f32[72,128]{1,0:T(8,128)S(1)} %get-tuple-element.24), channel_id=1, source_target_pairs={{0,1},{1,0},{2,3},{3,2},{4,5},{5,4},{6,7},{7,6},{8,9},{9,8},{10,11... | collective-permute-start | bytes 110600 | tf_op jit(solution)/shard_map/ppermute | solution.py:410
  15.0 5.2 %collective-permute-start.5 = (f32[72,128]{1,0:T(8,128)S(1)}, f32[72,128]{1,0:T(8,128)S(1)}, u32[]{:S(2)}, u32[]{:S(2)}) collective-permute-start(f32[72,128]{1,0:T(8,128)S(1)} %add.21), channel_id=1, source_target_pairs={{0,6},{1,7},{2,4},{3,5},{4,2},{5,3},{6,0},{7,1},{8,14},{9,15},{10,... | collective-permute-start | bytes 110600 | tf_op jit(solution)/shard_map/ppermute | solution.py:383
  16.5 4.0 %collective-permute-start.4 = (f32[72,128]{1,0:T(8,128)S(1)}, f32[72,128]{1,0:T(8,128)S(1)}, u32[]{:S(2)}, u32[]{:S(2)}) collective-permute-start(f32[72,128]{1,0:T(8,128)S(1)} %add.21), channel_id=1, source_target_pairs={{0,2},{1,3},{2,0},{3,1},{4,6},{5,7},{6,4},{7,5},{8,10},{9,11},{10,... | collective-permute-start | bytes 110600 | tf_op jit(solution)/shard_map/ppermute | solution.py:383
  17.1 4.0 %collective-permute-start.3 = (f32[72,128]{1,0:T(8,128)S(1)}, f32[72,128]{1,0:T(8,128)S(1)}, u32[]{:S(2)}, u32[]{:S(2)}) collective-permute-start(f32[72,128]{1,0:T(8,128)S(1)} %add.21), channel_id=1, source_target_pairs={{0,4},{1,5},{2,6},{3,7},{4,0},{5,1},{6,2},{7,3},{8,12},{9,13},{10,... | collective-permute-start | bytes 110600 | tf_op jit(solution)/shard_map/ppermute | solution.py:383
  21.1 6.1 %collective-permute-start.8 = (f32[72,128]{1,0:T(8,128)S(1)}, f32[72,128]{1,0:T(8,128)S(1)}, u32[]{:S(2)}, u32[]{:S(2)}) collective-permute-start(f32[72,128]{1,0:T(8,128)S(1)} %add_add_fusion.1), channel_id=1, source_target_pairs={{0,8},{1,9},{2,10},{3,11},{4,12},{5,13},{6,14},{7,15},{8,16},{9,17... | collective-permute-start | bytes 110600 | tf_op jit(solution)/shard_map/ppermute | solution.py:383
  22.7 4.5 %collective-permute-start.7 = (f32[72,128]{1,0:T(8,128)S(1)}, f32[72,128]{1,0:T(8,128)S(1)}, u32[]{:S(2)}, u32[]{:S(2)}) collective-permute-start(f32[72,128]{1,0:T(8,128)S(1)} %add_add_fusion.1), channel_id=1, source_target_pairs={{0,24},{1,25},{2,26},{3,27},{4,28},{5,29},{6,30},{7,31},{8,0},{9,1... | collective-permute-start | bytes 110600 | tf_op jit(solution)/shard_map/ppermute | solution.py:383
  25.0 4.9 %collective-permute-start.6 = (f32[72,128]{1,0:T(8,128)S(1)}, f32[72,128]{1,0:T(8,128)S(1)}, u32[]{:S(2)}, u32[]{:S(2)}) collective-permute-start(f32[72,128]{1,0:T(8,128)S(1)} %add_add_fusion.1), channel_id=1, source_target_pairs={{0,16},{1,17},{2,18},{3,19},{4,20},{5,21},{6,22},{7,23},{8,24},{9,... | collective-permute-start | bytes 110600 | tf_op jit(solution)/shard_map/ppermute | solution.py:383
  29.9 1.3 %collective-permute-start.9 = (f32[72,128]{1,0:T(8,128)S(1)}, f32[72,128]{1,0:T(8,128)S(1)}, u32[]{:S(2)}, u32[]{:S(2)}) collective-permute-start(f32[72,128]{1,0:T(8,128)S(1)} %add_add_fusion.refs_0_), channel_id=1, source_target_pairs={{0,1},{1,0},{2,3},{3,2},{4,5},{5,4},{6,7},{7,6},{8,9},{9,8},{10,11... | collective-permute-start | bytes 110600 | tf_op jit(solution)/shard_map/ppermute | solution.py:410

commit v8 on v7

--- a/solution.py
+++ b/solution.py
@@ -279,24 +279,28 @@
         inside = (lane >= at) & (lane < at + 8)
         if p == start:
             done = []
-            col = [along(work[p], at + j) + nought for j in range(8)]
+            col = [along(work[p], at + j) for j in range(8)]
+            col[0] = col[0] + nought
         raw = {(t, j): along(work[t], at + j) for j in range(8) for t in range(p + 1, end)}
         diagonal, recip, m = [], [], {}
         for j in range(8):
             diagonal.append(down(col[j], j))
             recip.append(1.0 / diagonal[j])
+            ratio = col[j] * recip[j]
             for k in range(j + 1, 8):
-                m[k, j] = down(col[j], k) * recip[j]
+                m[k, j] = down(ratio, k) if k > j + 2 else down(col[j], k) * recip[j]
                 col[k] = col[k] - col[j] * m[k, j]
         coming = []
         if p + 1 < end:
-            w = [raw[p + 1, j] + nought for j in range(8)]
-            coming = [along(work[p + 1], at + 8 + k) + nought for k in range(8)]
+            w = [raw[p + 1, j] for j in range(8)]
+            w[0] = w[0] + nought
+            coming = [along(work[p + 1], at + 8 + k) for k in range(8)]
             for j in range(8):
                 for k in range(j + 1, 8):
                     w[k] = w[k] - w[j] * m[k, j]
+                ratio = w[j] * recip[j]
                 for k in range(8):
-                    coming[k] = coming[k] - w[j] * (down(w[j], k) * recip[j])
+                    coming[k] = coming[k] - w[j] * down(ratio, k)
         cleared = jnp.where(inside, jnp.where(lane == sub + at, 1.0, 0.0), work[p])
         pivot = []
         for j in range(8):

time: 34.9 us -> 34.9 us (level)
  no operation moved by 1% of the time
where the time goes in v8:
time: 34.9 us; the launch traced here: 34.7 us
  starting transfers between devices  14.9 us (43%)
  waiting for transfers between devices  10.4 us (30%)
  Pallas kernels  8.64 us (25%)
  between operations  0.69 us (2%)
    ppermute x6, starting transfers between devices, add_up(): lax.ppermute(values, axis, route((lambda k: (k - flip) % 4) if radix == 4...  8.16 us
    ppermute x4, starting transfers between devices, swap(): return lax.ppermute(values, axis, route)  6.79 us
    ppermute x6, waiting for transfers between devices, add_up(): lax.ppermute(values, axis, route((lambda k: (k - flip) % 4) if radix == 4...  6.62 us
    ppermute x4, waiting for transfers between devices, swap(): return lax.ppermute(values, axis, route)  3.77 us
    pallas_call x1, Pallas kernels, body(): call(lambda *refs: finish(axis, nodes_dev * devices, *refs), [here] * 3,...  3.56 us
    pallas_call x1, Pallas kernels, body(): call(lambda *refs: inner(axis, *refs), [far] * 3, [(tall, here), (cross,...  2.39 us
    pallas_call x1, Pallas kernels, body(): call(lambda *refs: edge(axis, *refs), [far] * 3, [(cross, here)], [pltpu....  1.6 us
    pallas_call x1, Pallas kernels, body(): call(lambda *refs: project(axis, *refs), [here] * 9, [(tall, here), (piec...  1.09 us
  transfers between devices with their start and end apart: 10, of which 9 were waited for; matrix products, arithmetic and copies ran while one was open for 0% of the time, Pallas kernels for 7%

profile of v8, /device:TPU:0, one launch (start us, length us, event | category | flops | bytes accessed | tf_op | source)
XLA Modules:
  0.0 34.7 jit_solution(16113614117410590725)
XLA Ops:
  0.6 1.6 %shard_map.51 = f32[456,128]{1,0:T(8,128)S(1)} custom-call(f32[4,128,128]{2,1,0:T(8,128)} %bitcast.2, f32[4,128,128]{2,1,0:T(8,128)} %refs_1_.3, f32[4,128,128]{2,1,0:T(8,128)} %refs_2_.3), custom_call_target="tpu_custom_call" | custom-call | tf_op jit(solution)/shard_map/pallas_call | solution.py:441
  2.2 6.5 %collective-permute-start.1 = (f32[456,128]{1,0:T(8,128)S(1)}, f32[456,128]{1,0:T(8,128)S(1)}, u32[]{:S(2)}, u32[]{:S(2)}) collective-permute-start(f32[456,128]{1,0:T(8,128)S(1)} %shard_map.51), channel_id=1, source_target_pairs={{1,2},{2,1},{3,4},{4,3},{5,6},{6,5},{7,8},{8,7},{9,10},{10,9},{11,... | collective-permute-start | bytes 700424 | tf_op jit(solution)/shard_map/ppermute | solution.py:414
  8.7 2.4 %shard_map.50 = (f32[4,128,128]{2,1,0:T(8,128)S(1)}, f32[456,128]{1,0:T(8,128)S(1)}, bf16[4,128,384]{2,1,0:T(8,128)(2,1)S(1)}, bf16[4,128,384]{2,1,0:T(8,128)(2,...) custom-call(f32[4,128,128]{2,1,0:T(8,128)} %bitcast.3, ...), custom_call_target="tpu_custom_call" | custom-call | tf_op jit(solution)/shard_map/pallas_call | solution.py:445
  11.1 0.1 collective-permute-start
  11.2 1.4 %collective-permute-done.1.refs_8_ = f32[456,128]{1,0:T(8,128)S(1)} collective-permute-done((f32[456,128]{1,0:T(8,128)S(1)}, f32[456,128]{1,0:T(8,128)S(1)}, u32[]{:S(2)}, u32[]{:S(2)}) %collective-permute-start.1) | collective-permute-done | bytes 233504 | tf_op jit(solution)/shard_map/ppermute | solution.py:414
  12.6 0.1 collective-permute-done.refs_7_
  12.7 1.1 %shard_map.52 = (f32[4,128,128]{2,1,0:T(8,128)S(1)}, f32[72,128]{1,0:T(8,128)S(1)}, f32[72,128]{1,0:T(8,128)S(1)}) custom-call(f32[4,128,128]{2,1,0:T(8,128)S(1)} %get-tuple-element.15.refs_0_, bf16[4,128,384]{2,1,0:T(8,128)(2,1)S(1)} %get-tuple-element.16.refs_1_, bf16[4,128,384]{2,1,0:T(8,128)(2,1)S(1)} %get-tuple-element.17.refs_2_, ...), custom_call_target="tpu_custom_call" | custom-call | tf_op jit(solution)/shard_map/pallas_call | solution.py:453
  13.8 0.2 collective-permute-start.2
  14.0 1.1 %collective-permute-done.2 = f32[72,128]{1,0:T(8,128)S(1)} collective-permute-done((f32[72,128]{1,0:T(8,128)S(1)}, f32[72,128]{1,0:T(8,128)S(1)}, u32[]{:S(2)}, u32[]{:S(2)}) %collective-permute-start.2) | collective-permute-done | bytes 36896 | tf_op jit(solution)/shard_map/ppermute | solution.py:414
  15.0 1.5 %collective-permute-start.5 = (f32[72,128]{1,0:T(8,128)S(1)}, f32[72,128]{1,0:T(8,128)S(1)}, u32[]{:S(2)}, u32[]{:S(2)}) collective-permute-start(f32[72,128]{1,0:T(8,128)S(1)} %add.21), channel_id=1, source_target_pairs={{0,6},{1,7},{2,4},{3,5},{4,2},{5,3},{6,0},{7,1},{8,14},{9,15},{10,... | collective-permute-start | bytes 110600 | tf_op jit(solution)/shard_map/ppermute | solution.py:387
  16.5 0.6 %collective-permute-start.4 = (f32[72,128]{1,0:T(8,128)S(1)}, f32[72,128]{1,0:T(8,128)S(1)}, u32[]{:S(2)}, u32[]{:S(2)}) collective-permute-start(f32[72,128]{1,0:T(8,128)S(1)} %add.21), channel_id=1, source_target_pairs={{0,2},{1,3},{2,0},{3,1},{4,6},{5,7},{6,4},{7,5},{8,10},{9,11},{10,... | collective-permute-start | bytes 110600 | tf_op jit(solution)/shard_map/ppermute | solution.py:387
  17.1 1.4 %collective-permute-start.3 = (f32[72,128]{1,0:T(8,128)S(1)}, f32[72,128]{1,0:T(8,128)S(1)}, u32[]{:S(2)}, u32[]{:S(2)}) collective-permute-start(f32[72,128]{1,0:T(8,128)S(1)} %add.21), channel_id=1, source_target_pairs={{0,4},{1,5},{2,6},{3,7},{4,0},{5,1},{6,2},{7,3},{8,12},{9,13},{10,... | collective-permute-start | bytes 110600 | tf_op jit(solution)/shard_map/ppermute | solution.py:387
  18.5 1.7 %collective-permute-done.5 = f32[72,128]{1,0:T(8,128)S(1)} collective-permute-done((f32[72,128]{1,0:T(8,128)S(1)}, f32[72,128]{1,0:T(8,128)S(1)}, u32[]{:S(2)}, u32[]{:S(2)}) %collective-permute-start.5) | collective-permute-done | bytes 36896 | tf_op jit(solution)/shard_map/ppermute | solution.py:387
  20.3 0.2 collective-permute-done.4
  20.5 0.6 %collective-permute-done.3 = f32[72,128]{1,0:T(8,128)S(1)} collective-permute-done((f32[72,128]{1,0:T(8,128)S(1)}, f32[72,128]{1,0:T(8,128)S(1)}, u32[]{:S(2)}, u32[]{:S(2)}) %collective-permute-start.3) | collective-permute-done | bytes 36896 | tf_op jit(solution)/shard_map/ppermute | solution.py:387
  21.1 1.6 %collective-permute-start.8 = (f32[72,128]{1,0:T(8,128)S(1)}, f32[72,128]{1,0:T(8,128)S(1)}, u32[]{:S(2)}, u32[]{:S(2)}) collective-permute-start(f32[72,128]{1,0:T(8,128)S(1)} %add_add_fusion.1), channel_id=1, source_target_pairs={{0,8},{1,9},{2,10},{3,11},{4,12},{5,13},{6,14},{7,15},{8,16},{9,17... | collective-permute-start | bytes 110600 | tf_op jit(solution)/shard_map/ppermute | solution.py:387
  22.7 2.2 %collective-permute-start.7 = (f32[72,128]{1,0:T(8,128)S(1)}, f32[72,128]{1,0:T(8,128)S(1)}, u32[]{:S(2)}, u32[]{:S(2)}) collective-permute-start(f32[72,128]{1,0:T(8,128)S(1)} %add_add_fusion.1), channel_id=1, source_target_pairs={{0,24},{1,25},{2,26},{3,27},{4,28},{5,29},{6,30},{7,31},{8,0},{9,1... | collective-permute-start | bytes 110600 | tf_op jit(solution)/shard_map/ppermute | solution.py:387
  25.0 0.8 %collective-permute-start.6 = (f32[72,128]{1,0:T(8,128)S(1)}, f32[72,128]{1,0:T(8,128)S(1)}, u32[]{:S(2)}, u32[]{:S(2)}) collective-permute-start(f32[72,128]{1,0:T(8,128)S(1)} %add_add_fusion.1), channel_id=1, source_target_pairs={{0,16},{1,17},{2,18},{3,19},{4,20},{5,21},{6,22},{7,23},{8,24},{9,... | collective-permute-start | bytes 110600 | tf_op jit(solution)/shard_map/ppermute | solution.py:387
  25.8 1.5 %collective-permute-done.8 = f32[72,128]{1,0:T(8,128)S(1)} collective-permute-done((f32[72,128]{1,0:T(8,128)S(1)}, f32[72,128]{1,0:T(8,128)S(1)}, u32[]{:S(2)}, u32[]{:S(2)}) %collective-permute-start.8) | collective-permute-done | bytes 36896 | tf_op jit(solution)/shard_map/ppermute | solution.py:387
  27.2 0.0 collective-permute-done.7
  27.2 2.6 %collective-permute-done.6 = f32[72,128]{1,0:T(8,128)S(1)} collective-permute-done((f32[72,128]{1,0:T(8,128)S(1)}, f32[72,128]{1,0:T(8,128)S(1)}, u32[]{:S(2)}, u32[]{:S(2)}) %collective-permute-start.6) | collective-permute-done | bytes 36896 | tf_op jit(solution)/shard_map/ppermute | solution.py:387
  29.9 0.1 collective-permute-start.9
  29.9 1.2 %collective-permute-done.9.refs_1_ = f32[72,128]{1,0:T(8,128)S(1)} collective-permute-done((f32[72,128]{1,0:T(8,128)S(1)}, f32[72,128]{1,0:T(8,128)S(1)}, u32[]{:S(2)}, u32[]{:S(2)}) %collective-permute-start.9) | collective-permute-done | bytes 36896 | tf_op jit(solution)/shard_map/ppermute | solution.py:414
  31.1 3.6 %shard_map.53 = (f32[4,128,128]{2,1,0:T(8,128)}, f32[128,128]{1,0:T(8,128)}) custom-call(f32[72,128]{1,0:T(8,128)S(1)} %add_add_fusion.refs_0_, f32[72,128]{1,0:T(8,128)S(1)} %collective-permute-done.9.refs_1_, f32[4,128,128]{2,1,0:T(8,128)S(1)} %get-tuple-element.25.refs_2_), custom_call_target="tpu_custom_call" | custom-call | tf_op jit(solution)/shard_map/pallas_call | solution.py:458
  (3 shorter events, 0.0 us)
Async XLA Ops:
  2.2 10.3 %collective-permute-start.1 = (f32[456,128]{1,0:T(8,128)S(1)}, f32[456,128]{1,0:T(8,128)S(1)}, u32[]{:S(2)}, u32[]{:S(2)}) collective-permute-start(f32[456,128]{1,0:T(8,128)S(1)} %shard_map.51), channel_id=1, source_target_pairs={{1,2},{2,1},{3,4},{4,3},{5,6},{6,5},{7,8},{8,7},{9,10},{10,9},{11,... | collective-permute-start | bytes 700424 | tf_op jit(solution)/shard_map/ppermute | solution.py:414
  11.1 1.6 %collective-permute-start = (f32[456,128]{1,0:T(8,128)S(1)}, f32[456,128]{1,0:T(8,128)S(1)}, u32[]{:S(2)}, u32[]{:S(2)}) collective-permute-start(f32[456,128]{1,0:T(8,128)S(1)} %get-tuple-element.22), channel_id=1, source_target_pairs={{0,1},{1,0},{2,3},{3,2},{4,5},{5,4},{6,7},{7,6},{8,9},{9,8},{10,11... | collective-permute-start | bytes 700424 | tf_op jit(solution)/shard_map/ppermute | solution.py:414
  13.8 1.3 %collective-permute-start.2 = (f32[72,128]{1,0:T(8,128)S(1)}, f32[72,128]{1,0:T(8,128)S(1)}, u32[]{:S(2)}, u32[]{:S(2)}) collective-permute-start(f32[72,128]{1,0:T(8,128)S(1)} %get-tuple-element.24), channel_id=1, source_target_pairs={{0,1},{1,0},{2,3},{3,2},{4,5},{5,4},{6,7},{7,6},{8,9},{9,8},{10,11... | collective-permute-start | bytes 110600 | tf_op jit(solution)/shard_map/ppermute | solution.py:414
  15.0 5.2 %collective-permute-start.5 = (f32[72,128]{1,0:T(8,128)S(1)}, f32[72,128]{1,0:T(8,128)S(1)}, u32[]{:S(2)}, u32[]{:S(2)}) collective-permute-start(f32[72,128]{1,0:T(8,128)S(1)} %add.21), channel_id=1, source_target_pairs={{0,6},{1,7},{2,4},{3,5},{4,2},{5,3},{6,0},{7,1},{8,14},{9,15},{10,... | collective-permute-start | bytes 110600 | tf_op jit(solution)/shard_map/ppermute | solution.py:387
  16.5 4.0 %collective-permute-start.4 = (f32[72,128]{1,0:T(8,128)S(1)}, f32[72,128]{1,0:T(8,128)S(1)}, u32[]{:S(2)}, u32[]{:S(2)}) collective-permute-start(f32[72,128]{1,0:T(8,128)S(1)} %add.21), channel_id=1, source_target_pairs={{0,2},{1,3},{2,0},{3,1},{4,6},{5,7},{6,4},{7,5},{8,10},{9,11},{10,... | collective-permute-start | bytes 110600 | tf_op jit(solution)/shard_map/ppermute | solution.py:387
  17.1 4.0 %collective-permute-start.3 = (f32[72,128]{1,0:T(8,128)S(1)}, f32[72,128]{1,0:T(8,128)S(1)}, u32[]{:S(2)}, u32[]{:S(2)}) collective-permute-start(f32[72,128]{1,0:T(8,128)S(1)} %add.21), channel_id=1, source_target_pairs={{0,4},{1,5},{2,6},{3,7},{4,0},{5,1},{6,2},{7,3},{8,12},{9,13},{10,... | collective-permute-start | bytes 110600 | tf_op jit(solution)/shard_map/ppermute | solution.py:387
  21.1 6.1 %collective-permute-start.8 = (f32[72,128]{1,0:T(8,128)S(1)}, f32[72,128]{1,0:T(8,128)S(1)}, u32[]{:S(2)}, u32[]{:S(2)}) collective-permute-start(f32[72,128]{1,0:T(8,128)S(1)} %add_add_fusion.1), channel_id=1, source_target_pairs={{0,8},{1,9},{2,10},{3,11},{4,12},{5,13},{6,14},{7,15},{8,16},{9,17... | collective-permute-start | bytes 110600 | tf_op jit(solution)/shard_map/ppermute | solution.py:387
  22.7 4.5 %collective-permute-start.7 = (f32[72,128]{1,0:T(8,128)S(1)}, f32[72,128]{1,0:T(8,128)S(1)}, u32[]{:S(2)}, u32[]{:S(2)}) collective-permute-start(f32[72,128]{1,0:T(8,128)S(1)} %add_add_fusion.1), channel_id=1, source_target_pairs={{0,24},{1,25},{2,26},{3,27},{4,28},{5,29},{6,30},{7,31},{8,0},{9,1... | collective-permute-start | bytes 110600 | tf_op jit(solution)/shard_map/ppermute | solution.py:387
  25.0 4.9 %collective-permute-start.6 = (f32[72,128]{1,0:T(8,128)S(1)}, f32[72,128]{1,0:T(8,128)S(1)}, u32[]{:S(2)}, u32[]{:S(2)}) collective-permute-start(f32[72,128]{1,0:T(8,128)S(1)} %add_add_fusion.1), channel_id=1, source_target_pairs={{0,16},{1,17},{2,18},{3,19},{4,20},{5,21},{6,22},{7,23},{8,24},{9,... | collective-permute-start | bytes 110600 | tf_op jit(solution)/shard_map/ppermute | solution.py:387
  29.9 1.3 %collective-permute-start.9 = (f32[72,128]{1,0:T(8,128)S(1)}, f32[72,128]{1,0:T(8,128)S(1)}, u32[]{:S(2)}, u32[]{:S(2)}) collective-permute-start(f32[72,128]{1,0:T(8,128)S(1)} %add_add_fusion.refs_0_), channel_id=1, source_target_pairs={{0,1},{1,0},{2,3},{3,2},{4,5},{5,4},{6,7},{7,6},{8,9},{9,8},{10,11... | collective-permute-start | bytes 110600 | tf_op jit(solution)/shard_map/ppermute | solution.py:414
